TPU v7x, 32 devices: a whole 2x2x4 slice. The times are simulated.
32 devices in a mesh: ctx: 16 (over z, y, core), wsh: 2 (over x).
Axes of the slice: x: 2, y: 2, z: 4, core: 2. Of those that a mesh axis runs over, the one named last changes fastest.
Arguments:
- content: bfloat16 [2, 2048, 768], P('wsh', 'ctx')
- query_stream: bfloat16 [2, 2048, 768], P('wsh', 'ctx'), may hold values from -6 to 6
- block_rank: int32 [2, 16], P('wsh', 'ctx'), may hold values from 0 to 15, each once within a row
- segments: int32 [2, 2048], P('wsh', 'ctx'), may hold values from 0 to 3, never falling along the last dimension, each value on 1 to 1024 neighbouring positions
- positions: int32 [2, 2048], P('wsh', 'ctx'), may hold values from 0 to 2152, as said below
- query_weight: bfloat16 [768, 768], P('wsh'), may hold values from -0.21875 to 0.21875
- key_weight: bfloat16 [768, 768], P('wsh'), may hold values from -0.21875 to 0.21875
- value_weight: bfloat16 [768, 768], P('wsh'), may hold values from -0.21875 to 0.21875
- output_weight: bfloat16 [768, 768], P('wsh'), may hold values from -1.75 to 1.75
- content_bias: bfloat16 [768], P('wsh'), may hold values from -3 to 3
- segment_bias: bfloat16 [768], P('wsh'), may hold values from -3 to 3
- segment_embed: bfloat16 [2, 768], P(None, 'wsh'), may hold values from -4 to 4
- relative_table: bfloat16 [12, 33], P('wsh'), may hold values from -4 to 4
- attention_gain: bfloat16 [768], P('wsh'), may hold values from 0.5 to 1.5
- attention_shift: bfloat16 [768], P('wsh'), may hold values from -1 to 1
- inner_weight: bfloat16 [768, 3072], P('wsh'), may hold values from -0.21875 to 0.21875
- inner_bias: bfloat16 [3072], P('wsh'), may hold values from -1 to 1
- outer_weight: bfloat16 [3072, 768], P('wsh'), may hold values from -0.109375 to 0.109375
- outer_bias: bfloat16 [768], P('wsh'), may hold values from -1 to 1
- final_gain: bfloat16 [768], P('wsh'), may hold values from 0.5 to 1.5
- final_shift: bfloat16 [768], P('wsh'), may hold values from -1 to 1
- content_cotangent: bfloat16 [2, 2048, 768], P('wsh', 'ctx'), may hold values from -6 to 6
- query_cotangent: bfloat16 [2, 2048, 768], P('wsh', 'ctx'), may hold values from -6 to 6
Outputs:
- content_result: bfloat16 [2, 2048, 768], P('wsh', 'ctx')
- query_result: bfloat16 [2, 2048, 768], P('wsh', 'ctx')
- content_gradient: float32 [2, 2048, 768], P('wsh', 'ctx')
- query_gradient: float32 [2, 2048, 768], P('wsh', 'ctx')
- query_weight_gradient: float32 [768, 768], P('wsh')
- key_weight_gradient: float32 [768, 768], P('wsh')
- value_weight_gradient: float32 [768, 768], P('wsh')
- output_weight_gradient: float32 [768, 768], P('wsh')
- content_bias_gradient: float32 [768], P('wsh')
- segment_bias_gradient: float32 [768], P('wsh')
- segment_embed_gradient: float32 [2, 768], P(None, 'wsh')
- relative_table_gradient: float32 [12, 33], P('wsh')
- attention_gain_gradient: float32 [768], P('wsh')
- attention_shift_gradient: float32 [768], P('wsh')
- inner_weight_gradient: float32 [768, 3072], P('wsh')
- inner_bias_gradient: float32 [3072], P('wsh')
- outer_weight_gradient: float32 [3072, 768], P('wsh')
- outer_bias_gradient: float32 [768], P('wsh')
- final_gain_gradient: float32 [768], P('wsh')
- final_shift_gradient: float32 [768], P('wsh')
- root_mean_squares: float32 [3], replicated
Inputs may be any that keep to these rules, and one draw needn't show every extreme that they name: In each sequence positions rise by one inside each block of 128 tokens and never fall between blocks; the first token has position 0.
All inputs are finite; a program needn't handle non-finite values.
Results may differ from a plain program's by a relative error of at most 0.025.
Values may be sent and summed in bfloat16 or wider, within the bound.
No kernel may reach another device: no remote copies, remote signals or barrier semaphores. Data moves between devices by JAX's collectives and lax.ppermute only.
A program may use at most 448 MiB of HBM per device.

v0:
```python
import functools

import jax
import jax.numpy as jnp
from jax import lax
from jax.experimental import pallas as pl
from jax.experimental.pallas import tpu as pltpu
from jax.sharding import PartitionSpec as P

negative = -1e30
epsilon = 1e-05
bucket_steps = 16
key_tile = 256
lanes = 128
highest = lax.Precision.HIGHEST
f32 = jnp.float32
bf16 = jnp.bfloat16


free = pl.CostEstimate(flops=0, bytes_accessed=0, transcendentals=0)
in_vmem = pl.BlockSpec(memory_space=pltpu.VMEM)
in_smem = pl.BlockSpec(memory_space=pltpu.SMEM)


def takes(microseconds):
    return pl.CostEstimate(
        flops=microseconds * 1_000_000_000, bytes_accessed=0, transcendentals=0
    )


def normalized(values):
    centred = values - jnp.mean(values, axis=-1, keepdims=True)
    spread = jnp.mean(centred * centred, axis=-1, keepdims=True)
    scale = lax.rsqrt(spread + epsilon)
    return centred * scale, scale


def norm_back(cotangent, rows, scale):
    mean = jnp.mean(cotangent, axis=-1, keepdims=True)
    along = jnp.mean(cotangent * rows, axis=-1, keepdims=True)
    return scale * (cotangent - mean - rows * along)


def dot(left, right):
    return jnp.dot(left, right, preferred_element_type=f32)


def dot_nt(left, right):
    return lax.dot_general(left, right, (((1,), (1,)), ((), ())), preferred_element_type=f32)


def dot_tn(left, right):
    return lax.dot_general(left, right, (((0,), (0,)), ((), ())), preferred_element_type=f32)


def partner(value, bit):
    count = lax.axis_size("ctx")
    return lax.ppermute(value, "ctx", [(place, place ^ bit) for place in range(count)])


def across(value):
    return lax.ppermute(value, "wsh", [(0, 1), (1, 0)])


def bits_of(count):
    result = []
    bit = 1
    while bit < count:
        result.append(bit)
        bit *= 2
    return result


def block_order(count):
    order = [0]
    for bit in reversed(bits_of(count)):
        order = order + [place | bit for place in order]
    return order


def gather_blocks(own):
    count = lax.axis_size("ctx")
    bits = bits_of(count)
    if count != 16:
        held = own
        for bit in reversed(bits):
            held = jnp.concatenate([held, partner(held, bit)], axis=0)
        return [held]
    low = bits[1]
    near = partner(own, low)
    first = [own] + [partner(own, place) for place in (bits[3], bits[2], bits[2] | bits[3])]
    second = [near] + [partner(block, low) for block in first[1:]]
    first_core = partner(jnp.concatenate(first, axis=0), 1)
    second_core = partner(jnp.concatenate(second, axis=0), 1)
    return first + second + [first_core, second_core]


def move_kernel(plan, inputs, place_ref, *refs):
    sources, targets = refs[:inputs], refs[inputs:]
    for source, taken, target, put in plan:
        targets[target][put(place_ref)] = sources[source][taken(place_ref)]


def moved(plan, shapes, places, *sources):
    whole = pl.BlockSpec(memory_space=pltpu.VMEM)
    size = sum(shape.size for shape in shapes)
    return pl.pallas_call(
        functools.partial(move_kernel, plan, len(sources)),
        in_specs=[pl.BlockSpec(memory_space=pltpu.SMEM)] + [whole] * len(sources),
        out_specs=[whole] * len(shapes),
        out_shape=shapes,
        compiler_params=pltpu.CompilerParams(vmem_limit_bytes=48 << 20),
        cost_estimate=takes(3),
    )(places, *sources)


def window(start, rows, left=None, columns=None):
    def make(place_ref):
        first = start
        if isinstance(start, str):
            first = pl.multiple_of(place_ref[int(start)], 16)
        if left is None:
            return (pl.ds(first, rows), slice(None))
        return (pl.ds(first, rows), pl.ds(left, columns))

    return make


def half_rows(places, *shards):
    rows = shards[0].shape[0] // 2
    plan = []
    left = 0
    for at, shard in enumerate(shards):
        columns = shard.shape[1]
        plan.append((at, window("0", rows, 0, columns), 0, window(0, rows, left, columns)))
        left += columns
    return moved(tuple(plan), [jax.ShapeDtypeStruct((rows, left), bf16)], places, *shards)[0]


def whole_rows(places, runs, widths, got, rest, *shards):
    rows = shards[0].shape[0]
    half = rows // 2
    lefts = [0]
    for shard in shards:
        lefts.append(lefts[-1] + shard.shape[1])
    plan = []
    for shard, first, columns, target, column in runs:
        plan.append(
            (2 + shard, window(0, rows, first, columns), target, window("1", rows, column, columns))
        )
        for source, place in ((0, "2"), (1, "3")):
            plan.append(
                (
                    source,
                    window(0, half, lefts[shard] + first, columns),
                    target,
                    window(place, half, column, columns),
                )
            )
    shapes = [jax.ShapeDtypeStruct((2 * rows, width), bf16) for width in widths]
    return moved(tuple(plan), shapes, places, got, rest, *shards)


def shard_places(rows):
    core = lax.axis_index("ctx") % 2
    side = lax.axis_index("wsh")
    half = rows // 2
    base = (1 - side) * rows
    return jnp.stack(
        [core * half, side * rows, base + core * half, base + (1 - core) * half]
    ).astype(jnp.int32)


def split_bits(count):
    bits = bits_of(count)
    return bits[1:4], bits[4:]


def own_bit(bit):
    if bit == 0:
        return lax.axis_index("wsh")
    return (lax.axis_index("ctx") // bit) % 2


def pass_on(value, bit):
    return across(value) if bit == 0 else partner(value, bit)


class Sequence:
    def __init__(self, mark):
        self.mark = mark

    def wait(self, *values):
        *values, self.mark = lax.optimization_barrier(tuple(values) + (self.mark,))
        return values[0] if len(values) == 1 else tuple(values)

    ready = wait


def piece_places(order, cuts):
    total = len(order)
    place = jnp.arange(1 << total, dtype=jnp.int32)
    result = jnp.zeros_like(place)
    for at, bit in enumerate(order):
        value = ((place >> (total - 1 - at)) & 1) ^ own_bit(bit)
        weight = 1 << len(cuts) if bit == 0 else 1 << (len(cuts) - 1 - cuts.index(bit))
        result = result + value * weight
    return result


def fold_kernel(keep_ref, received_ref, *target_refs):
    first = 0
    for target_ref in target_refs:

        @pl.loop(0, target_ref.shape[0])
        def _(place, first=first, target_ref=target_ref):
            target_ref[place] = (
                keep_ref[first + place].astype(f32) + received_ref[first + place].astype(f32)
            ).astype(bf16)

        first += target_ref.shape[0]


def fold_parts(keep, received, parts):
    piece = jax.ShapeDtypeStruct((keep.shape[0] // parts,) + keep.shape[1:], bf16)
    return pl.pallas_call(
        fold_kernel,
        in_specs=[in_vmem] * 2,
        out_specs=[in_vmem] * parts,
        out_shape=[piece] * parts,
        compiler_params=pltpu.CompilerParams(vmem_limit_bytes=40 << 20),
        cost_estimate=free,
    )(keep, received)


def fold(keep, received):
    return fold_parts(keep, received, 2)


def fold_last(keep, received):
    return fold_parts(keep, received, 1)[0]


def pile_kernel(*refs):
    target_ref = refs[-1]
    first = 0
    for source_ref in refs[:-1]:

        @pl.loop(0, source_ref.shape[0])
        def _(place, first=first, source_ref=source_ref):
            target_ref[first + place] = source_ref[place]

        first += source_ref.shape[0]


def piled(*values):
    height = sum(value.shape[0] for value in values)
    return pl.pallas_call(
        pile_kernel,
        in_specs=[in_vmem] * len(values),
        out_specs=in_vmem,
        out_shape=jax.ShapeDtypeStruct((height,) + values[0].shape[1:], values[0].dtype),
        compiler_params=pltpu.CompilerParams(vmem_limit_bytes=40 << 20),
        cost_estimate=free,
    )(*values)


def share_kernel(back_ref, weight_ref, out_ref):
    out_ref[...] = dot_nt(back_ref[...], weight_ref[...]).astype(bf16).reshape(out_ref.shape)


def share_of_content(both_back, weight_both):
    count, columns = both_back.shape
    width = weight_both.shape[0]
    step = 2 * lanes
    return pl.pallas_call(
        share_kernel,
        grid=(count // step,),
        in_specs=[
            pl.BlockSpec((step, columns), lambda at: (at, 0)),
            pl.BlockSpec((width, columns), lambda at: (0, 0), pipeline_mode=pl.Buffered(1)),
        ],
        out_specs=pl.BlockSpec((2, lanes, width), lambda at: (at, 0, 0)),
        out_shape=jax.ShapeDtypeStruct((count // lanes, lanes, width), bf16),
        compiler_params=pltpu.CompilerParams(vmem_limit_bytes=40 << 20),
        cost_estimate=takes(7),
    )(both_back, weight_both)


def after(value, *others):
    return lax.optimization_barrier((value,) + others)[0]


def product_kernel(groups, place_ref, *refs):
    operands, (keep_ref, send_ref, total_ref) = refs[: 4 * groups], refs[4 * groups :]
    rows = keep_ref.shape[1]
    step = 256
    left = 0
    for group in range(groups):
        left_own, left_other, right_own, right_other = operands[4 * group : 4 * group + 4]
        columns = right_own.shape[1]
        for start in range(0, left_own.shape[1], step):
            total_ref[start : start + step, left : left + columns] = dot_tn(
                left_own[:, start : start + step], right_own[...]
            ) + dot_tn(left_other[:, start : start + step], right_other[...])
        left += columns
    for at, ref in enumerate((keep_ref, send_ref)):

        @pl.loop(0, ref.shape[0])
        def _(place, at=at, ref=ref):
            block = place_ref[at * ref.shape[0] + place]
            start = pl.multiple_of(block * rows, 8)
            ref[place] = total_ref[pl.ds(start, rows), :].astype(bf16)


def product_pieces(places, *operands):
    groups = len(operands) // 4
    half = places.shape[0] // 2
    height = operands[0].shape[1]
    columns = sum(operands[4 * group + 2].shape[1] for group in range(groups))
    piece = jax.ShapeDtypeStruct((half, height // (2 * half), columns), bf16)
    whole = pl.BlockSpec(memory_space=pltpu.VMEM)
    return pl.pallas_call(
        functools.partial(product_kernel, groups),
        in_specs=[pl.BlockSpec(memory_space=pltpu.SMEM)] + [whole] * len(operands),
        out_specs=[whole, whole],
        out_shape=[piece, piece],
        scratch_shapes=[pltpu.VMEM((height, columns), f32)],
        compiler_params=pltpu.CompilerParams(vmem_limit_bytes=40 << 20),
        cost_estimate=takes(4),
    )(places, *operands)


def cut_kernel(place_ref, vector_ref, small_ref, *refs):
    parts, (keep_ref, send_ref, turned_ref) = refs[:-3], refs[-3:]
    rows = keep_ref.shape[1]
    height = vector_ref.shape[1]
    filled = jnp.concatenate(
        [
            small_ref[...] + vector_ref[0:8, :],
            vector_ref[8:, :],
            jnp.zeros((lanes - vector_ref.shape[0], height), f32),
        ],
        axis=0,
    )
    for start in range(0, height, lanes):
        turned_ref[start : start + lanes, :] = filled[:, start : start + lanes].T
    parts = parts + (turned_ref,)
    for at, ref in enumerate((keep_ref, send_ref)):

        @pl.loop(0, ref.shape[0])
        def _(place, at=at, ref=ref):
            block = place_ref[at * ref.shape[0] + place]
            start = pl.multiple_of(block * rows, 8)
            left = 0
            for part in parts:
                columns = part.shape[1]
                ref[place, :, left : left + columns] = part[pl.ds(start, rows), :].astype(bf16)
                left += columns


def cut_gradient(places, vectors, small, *parts):
    half = places.shape[0] // 2
    height = parts[0].shape[0]
    columns = sum(part.shape[1] for part in parts) + lanes
    piece = jax.ShapeDtypeStruct((half, height // (2 * half), columns), bf16)
    whole = pl.BlockSpec(memory_space=pltpu.VMEM)
    return pl.pallas_call(
        cut_kernel,
        in_specs=[pl.BlockSpec(memory_space=pltpu.SMEM)] + [whole] * (len(parts) + 2),
        out_specs=[whole, whole],
        out_shape=[piece, piece],
        scratch_shapes=[pltpu.VMEM((height, lanes), f32)],
        compiler_params=pltpu.CompilerParams(vmem_limit_bytes=40 << 20),
        cost_estimate=takes(3),
    )(places, vectors, small, *parts)


def lay_out_kernel(plan, place_ref, *refs):
    outputs = len(plan)
    sources, targets = refs[:-outputs], refs[-outputs:]
    halves = 2 if place_ref.shape[0] > sources[0].shape[0] + 1 else 1
    for half in range(halves):
      for runs, target in zip(plan, targets, strict=True):
        for source, first, columns, column in runs:
            piece_ref = sources[source + half]
            count, rows = piece_ref.shape[:2]

            @pl.loop(0, count)
            def _(place, piece_ref=piece_ref, rows=rows, target=target, first=first, columns=columns, column=column, half=half):
                start = pl.multiple_of(place_ref[half * count + place] * rows, 8)
                value = piece_ref[place, :, first : first + columns].astype(f32)
                if column >= 0:
                    target[pl.ds(start, rows), column : column + columns] = value
                else:
                    core = place_ref[count]
                    which = core if column == -1 else 1 - core
                    left = pl.multiple_of(which * columns, lanes)
                    target[pl.ds(start, rows), pl.ds(left, columns)] = value


def lay_out(places, plan, *pieces):
    whole = pl.BlockSpec(memory_space=pltpu.VMEM)
    shapes = []
    halves = 2 if places.shape[0] > pieces[0].shape[0] + 1 else 1
    for runs in plan:
        count, rows = pieces[runs[0][0]].shape[:2]
        shapes.append(jax.ShapeDtypeStruct((halves * count * rows, sum(run[2] for run in runs)), f32))
    return pl.pallas_call(
        functools.partial(lay_out_kernel, plan),
        in_specs=[pl.BlockSpec(memory_space=pltpu.SMEM)] + [whole] * len(pieces),
        out_specs=[whole] * len(plan),
        out_shape=shapes,
        compiler_params=pltpu.CompilerParams(vmem_limit_bytes=48 << 20),
        cost_estimate=takes(3),
    )(places, *pieces)


def stream_bias(table_ref, head, block):
    spread = jnp.broadcast_to(table_ref[head, pl.ds(block, 1), :], (lanes, 2 * lanes))
    return pltpu.roll(spread, 0, 1, stride=1, stride_axis=0)[:, :lanes]


def tile_bias(table_ref, block):
    parts = []
    for piece in range(key_tile // lanes):
        first = stream_bias(table_ref, 0, block + piece)
        second = stream_bias(table_ref, 1, block + piece)
        parts.append(jnp.concatenate([first, first, second, second], axis=1))
    return jnp.concatenate(parts, axis=0)


def own_mask():
    row = lax.broadcasted_iota(jnp.int32, (key_tile, 4 * lanes), 0)
    column = lax.broadcasted_iota(jnp.int32, (key_tile, 4 * lanes), 1)
    stream = (column // lanes) % 2
    return jnp.where((stream == 1) & (row == column % lanes), negative, 0.0)


def forward_kernel(
    query_ref,
    content_bias_ref,
    segment_bias_ref,
    embed_ref,
    row_code_ref,
    key_code_ref,
    both_ref,
    table_ref,
    out_ref,
    log_ref,
    stack_ref,
    score_ref,
):
    rows = query_ref.shape[0]
    tiles = both_ref.shape[0] // key_tile
    lane = lax.broadcasted_iota(jnp.int32, (rows, lanes), 1)
    first = lane < lanes // 2
    query = query_ref[...]
    low = (query + content_bias_ref[...]).astype(bf16).astype(f32) * 0.125
    shifted = query + segment_bias_ref[...]
    zero_term = shifted * embed_ref[0:1, :]
    one_term = shifted * embed_ref[1:2, :]
    code = row_code_ref[...]
    for head in range(2):
        own = first if head == 0 else jnp.logical_not(first)
        zero_sum = jnp.sum(jnp.where(own, zero_term, 0.0), axis=1, keepdims=True) * 0.125
        one_sum = jnp.sum(jnp.where(own, one_term, 0.0), axis=1, keepdims=True) * 0.125
        step = zero_sum - one_sum
        step_high = step.astype(bf16).astype(f32)
        step_low = step - step_high
        one_high = one_sum.astype(bf16).astype(f32)
        one_low = one_sum - one_high
        extra = jnp.where(
            lane < 4,
            step_high,
            jnp.where(lane < 8, step_low, jnp.where(lane == 8, one_high, one_low)),
        )
        stack_ref[0, pl.ds(head * rows, rows), 0:lanes] = jnp.where(own, low, 0.0).astype(bf16)
        stack_ref[0, pl.ds(head * rows, rows), lanes : 2 * lanes] = (extra * code).astype(bf16)
    stack = stack_ref[0]

    def scores(tile, top):
        start = pl.multiple_of(tile * key_tile, key_tile)
        keys = jnp.concatenate(
            [both_ref[pl.ds(start, key_tile), :lanes], key_code_ref[pl.ds(start, key_tile), :]], axis=1
        )
        score = dot_nt(keys, stack) + tile_bias(table_ref, tile * (key_tile // lanes))
        if isinstance(tile, int) and tile == 0:
            score = score + own_mask()
        score_ref[pl.ds(start, key_tile), :] = score
        return jnp.maximum(top, jnp.max(score.reshape(key_tile // 8, 8, 4 * lanes), axis=0))

    top = jnp.full((8, 4 * lanes), negative, f32)
    top = scores(0, top)
    top = lax.fori_loop(1, tiles, scores, top, unroll=min(7, tiles - 1))
    peak = jnp.max(top, axis=0, keepdims=True)

    def gathered(tile, running):
        total, mixed = running
        start = pl.multiple_of(tile * key_tile, key_tile)
        weight = jnp.exp(score_ref[pl.ds(start, key_tile), :] - peak)
        total = total + jnp.sum(weight.reshape(key_tile // 8, 8, 4 * lanes), axis=0)
        mixed = mixed + dot_tn(both_ref[pl.ds(start, key_tile), lanes:], weight.astype(bf16))
        return total, mixed

    total, mixed = lax.fori_loop(
        0,
        tiles,
        gathered,
        (jnp.zeros((8, 4 * lanes), f32), jnp.zeros((lanes, 4 * lanes), f32)),
        unroll=min(8, tiles),
    )
    total = jnp.sum(total, axis=0, keepdims=True)
    mixed = mixed / total
    half = lanes // 2
    joined = jnp.concatenate([mixed[:half, :rows], mixed[half:, rows:]], axis=0)
    out_ref[...] = joined.T
    log_ref[0] = peak + jnp.log(total)


def diagonal_sums(square):
    lane = lax.broadcasted_iota(jnp.int32, (8, lanes), 1)
    near = square[0:8]
    far = jnp.zeros((8, lanes), f32)
    for group in range(1, lanes // 8):
        turned = pltpu.roll(square[8 * group : 8 * group + 8], lanes - 8 * group, 1)
        inside = lane < lanes - 8 * group
        near = near + jnp.where(inside, turned, 0.0)
        far = far + jnp.where(inside, 0.0, turned)
    both = jnp.concatenate([near, far], axis=1)
    row = lax.broadcasted_iota(jnp.int32, (8, 2 * lanes), 0)
    for bit in (1, 2, 4):
        both = jnp.where((row // bit) % 2 == 1, pltpu.roll(both, 2 * lanes - bit, 1), both)
    return jnp.sum(both, axis=0, keepdims=True)


def backward_kernel(
    stack_ref,
    query_ref,
    segment_bias_ref,
    embed_ref,
    row_code_ref,
    key_code_ref,
    both_ref,
    table_ref,
    number_ref,
    out_back_ref,
    attended_ref,
    log_ref,
    query_back_ref,
    both_back_ref,
    small_ref,
    diagonal_ref,
):
    rows = query_ref.shape[0]
    tiles = both_ref.shape[0] // key_tile
    half = lanes // 2
    lane = lax.broadcasted_iota(jnp.int32, (rows, lanes), 1)
    first = lane < half
    out_back = out_back_ref[...]
    product = (out_back.astype(f32) * attended_ref[...]).T
    delta = jnp.concatenate(
        [
            jnp.sum(product[:half], axis=0, keepdims=True),
            jnp.sum(product[half:], axis=0, keepdims=True),
        ],
        axis=1,
    )
    zeros = jnp.zeros_like(out_back)
    back_stack = jnp.concatenate(
        [jnp.where(first, out_back, zeros), jnp.where(first, zeros, out_back)], axis=0
    )
    stack = stack_ref[0]
    query_stack = stack[:, :lanes]
    log_row = log_ref[0]

    def step(tile, running):
        start = pl.multiple_of(tile * key_tile, key_tile)
        block = tile * (key_tile // lanes)
        keys = jnp.concatenate(
            [both_ref[pl.ds(start, key_tile), :lanes], key_code_ref[pl.ds(start, key_tile), :]], axis=1
        )
        score = dot_nt(keys, stack) + tile_bias(table_ref, block)
        if isinstance(tile, int) and tile == 0:
            score = score + own_mask()
        weight = jnp.exp(score - log_row)
        weight_back = dot_nt(both_ref[pl.ds(start, key_tile), lanes:], back_stack)
        score_back = weight * (weight_back - delta)
        score_low = score_back.astype(bf16)
        both_back_ref[pl.ds(start, key_tile), lanes:] = dot(
            weight.astype(bf16), back_stack
        ).astype(bf16)
        both_back_ref[pl.ds(start, key_tile), :lanes] = dot(score_low, query_stack).astype(bf16)
        for head in range(2):
            for piece in range(key_tile // lanes):
                part = score_back[
                    piece * lanes : (piece + 1) * lanes, head * rows : (head + 1) * rows
                ]
                square = part[:, :lanes] + part[:, lanes:]
                diagonal_ref[head, block + piece] = diagonal_sums(square)[0]
        return running + dot_tn(keys, score_low)

    diagonal_ref[2:] = jnp.zeros(diagonal_ref[2:].shape, f32)
    running = step(0, jnp.zeros((2 * lanes, 2 * rows), f32))
    running = lax.fori_loop(1, tiles, step, running, unroll=min(7, tiles - 1))
    joined = jnp.concatenate([running[:half, :rows], running[half:lanes, rows:]], axis=0).T * 0.125
    shifted = query_ref[...] + segment_bias_ref[...]
    code = row_code_ref[...]
    zero_columns = []
    one_columns = []
    for head in range(2):
        part = running[lanes:, head * rows : (head + 1) * rows].T * 0.125
        same = jnp.sum(jnp.where(lane < 4, part * code, 0.0), axis=1, keepdims=True)
        total = jnp.sum(jnp.where(lane == 8, part, 0.0), axis=1, keepdims=True)
        zero_columns.append(same)
        one_columns.append(total - same)
    zero_back = jnp.where(first, zero_columns[0], zero_columns[1])
    one_back = jnp.where(first, one_columns[0], one_columns[1])
    shift_back = zero_back * embed_ref[0:1, :] + one_back * embed_ref[1:2, :]
    query_back_ref[...] = (joined + shift_back).astype(bf16)
    small_ref[0:1, :] = jnp.sum(joined, axis=0, keepdims=True)
    small_ref[1:2, :] = jnp.sum(shift_back, axis=0, keepdims=True)
    small_ref[2:3, :] = jnp.sum(zero_back * shifted, axis=0, keepdims=True)
    small_ref[3:4, :] = jnp.sum(one_back * shifted, axis=0, keepdims=True)
    blocks = number_ref.shape[0]
    bucket = lax.broadcasted_iota(jnp.int32, (lanes, 2 * lanes), 0)
    table_back = jnp.zeros((8, lanes), f32)
    for block in range(blocks):
        chosen = jnp.where(bucket == number_ref[block : block + 1, :], 1.0, 0.0).astype(bf16)
        sums = diagonal_ref[:, block, :]
        for _ in range(3):
            part = sums.astype(bf16)
            table_back = table_back + dot_nt(part, chosen)
            sums = sums - part.astype(f32)
    small_ref[4:8, :] = table_back[:4]


def attention_specs(rows, keys, blocks, first_pair=0):
    column = lambda pair: (0, pair + first_pair)
    fixed = lambda pair: (0, 0)
    front = lambda pair: (pair + first_pair, 0, 0)
    return {
        "rows": pl.BlockSpec((rows, lanes), column),
        "row": pl.BlockSpec((1, lanes), column),
        "embed": pl.BlockSpec((2, lanes), column),
        "small": pl.BlockSpec((8, lanes), column),
        "row_code": pl.BlockSpec((rows, lanes), fixed),
        "key_code": pl.BlockSpec((keys, lanes), fixed, pipeline_mode=pl.Buffered(1)),
        "both": pl.BlockSpec((keys, 2 * lanes), column),
        "table": pl.BlockSpec((2, blocks, 2 * lanes), front),
        "log": pl.BlockSpec((1, 1, 2 * rows), front),
        "stack": pl.BlockSpec((1, 2 * rows, 2 * lanes), front),
    }


def attention_forward(query_full, bias_content, bias_segment, embed, row_code, key_code, both, table):
    rows, width = query_full.shape
    count = both.shape[0]
    pairs = width // lanes
    spec = attention_specs(rows, count, count // lanes)
    return pl.pallas_call(
        forward_kernel,
        grid=(pairs,),
        in_specs=[
            spec["rows"],
            spec["row"],
            spec["row"],
            spec["embed"],
            spec["row_code"],
            spec["key_code"],
            spec["both"],
            spec["table"],
        ],
        out_specs=[spec["rows"], spec["log"], spec["stack"]],
        out_shape=[
            jax.ShapeDtypeStruct((rows, width), f32),
            jax.ShapeDtypeStruct((pairs, 1, 2 * rows), f32),
            jax.ShapeDtypeStruct((pairs, 2 * rows, 2 * lanes), bf16),
        ],
        scratch_shapes=[pltpu.VMEM((count, 2 * rows), f32)],
        compiler_params=pltpu.CompilerParams(
            dimension_semantics=("arbitrary",), vmem_limit_bytes=60 << 20
        ),
        cost_estimate=takes(18),
    )(query_full, bias_content, bias_segment, embed, row_code, key_code, both, table)


def attention_backward(stack, query_full, bias_segment, embed, row_code, key_code, both, table, number, out_back, attended, log_row):
    rows, width = query_full.shape
    count = both.shape[0]
    pairs = width // lanes
    blocks = count // lanes
    spec = attention_specs(rows, count, blocks)
    return pl.pallas_call(
        backward_kernel,
        grid=(pairs,),
        in_specs=[
            spec["stack"],
            spec["rows"],
            spec["row"],
            spec["embed"],
            spec["row_code"],
            spec["key_code"],
            spec["both"],
            spec["table"],
            pl.BlockSpec((blocks, 2 * lanes), lambda pair: (0, 0)),
            spec["rows"],
            spec["rows"],
            spec["log"],
        ],
        out_specs=[spec["rows"], spec["both"], spec["small"]],
        out_shape=[
            jax.ShapeDtypeStruct((rows, width), bf16),
            jax.ShapeDtypeStruct((count, 2 * width), bf16),
            jax.ShapeDtypeStruct((8, width), f32),
        ],
        scratch_shapes=[pltpu.VMEM((8, blocks, 2 * lanes), f32)],
        compiler_params=pltpu.CompilerParams(
            dimension_semantics=("arbitrary",), vmem_limit_bytes=60 << 20
        ),
        cost_estimate=takes(34),
    )(stack, query_full, bias_segment, embed, row_code, key_code, both, table, number, out_back, attended, log_row)


def marks_kernel(bound_list, meta_ref, table_ref, key_code_ref, bias_ref, number_ref, row_code_ref):
    blocks = meta_ref.shape[0]
    info = meta_ref[:, 0, :].astype(f32)
    segment = info[:, :lanes]
    rank = info[:, lanes : lanes + 1]
    first = info[:, lanes + 1 : lanes + 2] * lanes + info[:, lanes + 2 : lanes + 3]
    turn = lax.broadcasted_iota(jnp.int32, (blocks, 2 * lanes), 1)
    turn = jnp.where(turn < lanes, turn, turn - 2 * lanes)
    distance = (first[0:1, :] - first).astype(jnp.int32) + turn
    number = jnp.full(distance.shape, bucket_steps, jnp.int32)
    for bound in bound_list:
        number = number + (distance >= bound).astype(jnp.int32) - (distance <= -bound).astype(jnp.int32)
    number_ref[...] = number
    hidden = rank > rank[0:1, :]
    for head in range(bias_ref.shape[0]):
        value = jnp.zeros((blocks, 2 * lanes), f32)
        for bucket in range(2 * bucket_steps + 1):
            value = jnp.where(number == bucket, table_ref[head, bucket], value)
        bias_ref[head] = jnp.where(hidden, negative, value)
    lane = lax.broadcasted_iota(jnp.int32, (lanes, lanes), 1)
    code = (lane % 4).astype(f32)
    for block in range(blocks):
        column = jnp.broadcast_to(segment[block : block + 1, :], (lanes, lanes)).T
        marked = jnp.where(
            lane < 8, jnp.where(column == code, 1.0, 0.0), jnp.where(lane < 10, 1.0, 0.0)
        )
        key_code_ref[block * lanes : (block + 1) * lanes, :] = marked.astype(bf16)
        if block == 0:
            row_code_ref[:lanes, :] = marked
            row_code_ref[lanes:, :] = marked


def key_marks(meta_all, table_full, length):
    blocks = meta_all.shape[0]
    heads = table_full.shape[0]
    bounds = tuple(
        1 + level * level * length // (bucket_steps * bucket_steps) for level in range(bucket_steps)
    )
    whole = pl.BlockSpec(memory_space=pltpu.VMEM)
    scalars = pl.BlockSpec(memory_space=pltpu.SMEM)
    return pl.pallas_call(
        functools.partial(marks_kernel, bounds),
        in_specs=[whole, scalars],
        out_specs=[whole] * 4,
        out_shape=[
            jax.ShapeDtypeStruct((blocks * lanes, lanes), bf16),
            jax.ShapeDtypeStruct((heads, blocks, 2 * lanes), f32),
            jax.ShapeDtypeStruct((blocks, 2 * lanes), jnp.int32),
            jax.ShapeDtypeStruct((2 * lanes, lanes), f32),
        ],
        compiler_params=pltpu.CompilerParams(vmem_limit_bytes=40 << 20),
        cost_estimate=takes(2),
    )(meta_all, table_full)


def assemble(target_ref, own_ref, got_ref, rest_ref, columns, places):
    rows = own_ref.shape[0]
    half = rows // 2
    own, got, rest = [pl.multiple_of(place, 16) for place in places]
    target_ref[pl.ds(own, rows), :] = own_ref[...]
    target_ref[pl.ds(got, half), :] = got_ref[:, columns]
    target_ref[pl.ds(rest, half), :] = rest_ref[:, columns]


def forward_half_kernel(
    place_ref,
    attended_ref,
    content_ref,
    stream_ref,
    output_own_ref,
    inner_own_ref,
    got_ref,
    rest_ref,
    vector_ref,
    bias_ref,
    out_low_ref,
    normed_ref,
    rows_ref,
    scale_ref,
    normed_low_ref,
    active_ref,
    slope_ref,
    square_ref,
    weight_output_ref,
    weight_inner_ref,
):
    width = attended_ref.shape[1]
    hidden = inner_own_ref.shape[1]
    half = content_ref.shape[0]
    places = (place_ref[1], place_ref[2], place_ref[3])
    assemble(weight_output_ref, output_own_ref, got_ref, rest_ref, slice(0, width), places)
    assemble(weight_inner_ref, inner_own_ref, got_ref, rest_ref, slice(width, width + hidden), places)
    out_low = attended_ref[...].astype(bf16)
    out_low_ref[...] = out_low
    attention_out = dot(out_low, weight_output_ref[...])
    streams = jnp.concatenate([content_ref[...], stream_ref[...]], axis=0).astype(f32)
    residual = streams + attention_out
    rows, scale = normalized(residual)
    normed = rows * vector_ref[2:3, :] + vector_ref[3:4, :]
    normed_low = normed.astype(bf16)
    rows_ref[...] = rows
    scale_ref[...] = jnp.broadcast_to(scale, scale_ref.shape)
    normed_ref[...] = normed
    normed_low_ref[...] = normed_low
    lane = lax.broadcasted_iota(jnp.int32, (1, width), 1)
    total = jnp.zeros((1, width), f32)
    for at, value in enumerate((streams, attention_out, residual)):
        part = value[:half]
        summed = jnp.sum(jnp.sum(part * part, axis=0, keepdims=True), axis=1, keepdims=True)
        total = total + jnp.where((lane == at) | (lane == at + width // 2), summed, 0.0)
    square_ref[...] = jnp.broadcast_to(total, square_ref.shape)
    step = 512

    @pl.loop(0, hidden // step)
    def _(at):
        span = pl.ds(pl.multiple_of(at * step, step), step)
        inner = dot(normed_low, weight_inner_ref[:, span]) + bias_ref[0:1, span]
        below = 0.5 + 0.5 * lax.erf(inner * 0.7071067811865476)
        density = 0.3989422804014327 * jnp.exp(-0.5 * inner * inner)
        active_ref[:, span] = (inner * below).astype(bf16)
        slope_ref[:, span] = below + inner * density


def backward_half_kernel(
    place_ref,
    active_ref,
    slope_ref,
    normed_ref,
    rows_ref,
    scale_ref,
    weight_output_ref,
    weight_inner_ref,
    outer_own_ref,
    got_ref,
    rest_ref,
    vector_ref,
    square_ref,
    content_cotangent_ref,
    query_cotangent_ref,
    content_result_ref,
    query_result_ref,
    residual_back_ref,
    out_back_ref,
    outer_kept_ref,
    outer_sent_ref,
    inner_kept_ref,
    inner_sent_ref,
    attention_kept_ref,
    attention_sent_ref,
    sums_ref,
    weight_outer_ref,
    inner_back_ref,
    held_ref,
    bias_back_ref,
):
    width = normed_ref.shape[1]
    hidden = active_ref.shape[1]
    count = content_cotangent_ref.shape[0]
    core = place_ref[4]
    assemble(
        weight_outer_ref,
        outer_own_ref,
        got_ref,
        rest_ref,
        slice(0, width),
        (place_ref[5], place_ref[6], place_ref[7]),
    )

    def give(value_ref, kept_ref, sent_ref):
        columns = kept_ref.shape[1]
        kept_ref[...] = value_ref[:, pl.ds(pl.multiple_of(core * columns, lanes), columns)]
        sent_ref[...] = value_ref[:, pl.ds(pl.multiple_of((1 - core) * columns, lanes), columns)]

    outer = dot(active_ref[...], weight_outer_ref[...]) + vector_ref[4:5, :]
    final_rows, final_scale = normalized(normed_ref[...] + outer)
    result = (final_rows * vector_ref[5:6, :] + vector_ref[6:7, :]).astype(bf16)
    content_result_ref[...] = result[:count]
    query_result_ref[...] = result[count:]
    cotangent = jnp.concatenate(
        [content_cotangent_ref[...], query_cotangent_ref[...]], axis=0
    ).astype(f32)
    sums_ref[9:10, :] = jnp.sum(cotangent * final_rows, axis=0, keepdims=True)
    sums_ref[10:11, :] = jnp.sum(cotangent, axis=0, keepdims=True)
    back_second = norm_back(cotangent * vector_ref[5:6, :], final_rows, final_scale)
    outer_back = back_second.astype(bf16)
    sums_ref[8:9, :] = jnp.sum(outer_back.astype(f32), axis=0, keepdims=True)
    held_ref[...] = outer_back
    give(held_ref, outer_kept_ref, outer_sent_ref)
    residual_back_ref[...] = back_second
    step = 512

    @pl.loop(0, hidden // step)
    def _(at):
        span = pl.ds(pl.multiple_of(at * step, step), step)
        back = dot_nt(outer_back, weight_outer_ref[span, :]) * slope_ref[:, span]
        low = back.astype(bf16)
        inner_back_ref[:, span] = low
        bias_back_ref[0:1, span] = jnp.sum(low.astype(f32), axis=0, keepdims=True)
        residual_back_ref[...] += dot_nt(low, weight_inner_ref[:, span])

    give(inner_back_ref, inner_kept_ref, inner_sent_ref)
    normed_back = residual_back_ref[...]
    rows = rows_ref[...]
    sums_ref[6:7, :] = jnp.sum(normed_back * rows, axis=0, keepdims=True)
    sums_ref[7:8, :] = jnp.sum(normed_back, axis=0, keepdims=True)
    residual_back = norm_back(normed_back * vector_ref[2:3, :], rows, scale_ref[:, 0:1])
    residual_back_ref[...] = residual_back
    attention_back = residual_back.astype(bf16)
    held_ref[...] = attention_back
    give(held_ref, attention_kept_ref, attention_sent_ref)
    out_back_ref[...] = dot_nt(attention_back, weight_output_ref[...]).astype(bf16)
    part = width // 2
    for at in range(hidden // width):
        sums_ref[11 + at : 12 + at, :part] = bias_back_ref[0:1, at * part : (at + 1) * part]
        sums_ref[11 + at : 12 + at, part:] = bias_back_ref[
            0:1, hidden // 2 + at * part : hidden // 2 + (at + 1) * part
        ]
    last = 11 + hidden // width
    sums_ref[last : last + 1, :] = square_ref[0:1, :]
    sums_ref[0:6, :] = jnp.zeros((6, width), f32)


def forward_half(places, attended, content, stream, output_own, inner_own, got, rest, vectors, bias):
    rows, width = attended.shape
    hidden = inner_own.shape[1]
    shapes = [
        jax.ShapeDtypeStruct((rows, width), bf16),
        jax.ShapeDtypeStruct((rows, width), f32),
        jax.ShapeDtypeStruct((rows, width), f32),
        jax.ShapeDtypeStruct((rows, lanes), f32),
        jax.ShapeDtypeStruct((rows, width), bf16),
        jax.ShapeDtypeStruct((rows, hidden), bf16),
        jax.ShapeDtypeStruct((rows, hidden), f32),
        jax.ShapeDtypeStruct((8, width), f32),
        jax.ShapeDtypeStruct((width, width), bf16),
        jax.ShapeDtypeStruct((width, hidden), bf16),
    ]
    return pl.pallas_call(
        forward_half_kernel,
        in_specs=[in_smem] + [in_vmem] * 9,
        out_specs=[in_vmem] * len(shapes),
        out_shape=shapes,
        compiler_params=pltpu.CompilerParams(vmem_limit_bytes=48 << 20),
        cost_estimate=takes(8),
    )(places, attended, content, stream, output_own, inner_own, got, rest, vectors, bias)


def backward_half(places, *operands):
    active, normed = operands[0], operands[2]
    rows, width = normed.shape
    hidden = active.shape[1]
    count = rows // 2
    shapes = (
        [jax.ShapeDtypeStruct((count, width), bf16)] * 2
        + [jax.ShapeDtypeStruct((rows, width), f32), jax.ShapeDtypeStruct((rows, width), bf16)]
        + [jax.ShapeDtypeStruct((rows, width // 2), bf16)] * 2
        + [jax.ShapeDtypeStruct((rows, hidden // 2), bf16)] * 2
        + [jax.ShapeDtypeStruct((rows, width // 2), bf16)] * 2
        + [jax.ShapeDtypeStruct((16, width), f32)]
    )
    return pl.pallas_call(
        backward_half_kernel,
        in_specs=[in_smem] + [in_vmem] * len(operands),
        out_specs=[in_vmem] * len(shapes),
        out_shape=shapes,
        scratch_shapes=[
            pltpu.VMEM((hidden, width), bf16),
            pltpu.VMEM((rows, hidden), bf16),
            pltpu.VMEM((rows, width), bf16),
            pltpu.VMEM((8, hidden), f32),
        ],
        compiler_params=pltpu.CompilerParams(vmem_limit_bytes=56 << 20),
        cost_estimate=takes(12),
    )(places, *operands)


def body(
    content,
    query_stream,
    block_rank,
    segments,
    positions,
    query_weight,
    key_weight,
    value_weight,
    output_weight,
    content_bias,
    segment_bias,
    segment_embed,
    relative_table,
    attention_gain,
    attention_shift,
    inner_weight,
    inner_bias,
    outer_weight,
    outer_bias,
    final_gain,
    final_shift,
    content_cotangent,
    query_cotangent,
):
    block_rows = content.shape[1]
    width = content.shape[2]
    rows = 2 * block_rows
    count = lax.axis_size("ctx")
    sides = lax.axis_size("wsh")
    side = lax.axis_index("wsh")
    core = lax.axis_index("ctx") % 2
    length = block_rows * count
    own_content = content[0]
    own_query = query_stream[0]
    part = width // sides
    table_heads, bucket_count = relative_table.shape
    head_count = table_heads * sides
    inner_rows = inner_bias.shape[0] // part
    low = 2

    first_places = shard_places(query_weight.shape[0])
    first_sent = half_rows(first_places, query_weight, key_weight, value_weight)
    first_got = across(first_sent)
    mark_rows = 16
    marks = jnp.concatenate(
        [
            segments[0].astype(bf16),
            block_rank[0].astype(bf16),
            (positions[0, :1] // lanes).astype(bf16),
            (positions[0, :1] % lanes).astype(bf16),
        ]
    )
    marks = jnp.pad(marks[None], ((0, mark_rows - 1), (0, width - marks.shape[0])))
    block = jnp.concatenate([own_content, marks], axis=0)
    gathered = gather_blocks(block)
    small = jnp.concatenate(
        [
            content_bias,
            segment_bias,
            attention_gain,
            attention_shift,
            outer_bias,
            final_gain,
            final_shift,
            segment_embed.reshape(-1),
            inner_bias,
            relative_table.reshape(-1),
        ]
    )
    small_height = 16
    small = jnp.pad(small, (0, small_height * part - small.shape[0])).reshape(small_height, part)
    small_other = across(small)
    first_rest = partner(first_got, 1)
    second_sent = half_rows(first_places, output_weight, inner_weight)
    second_got = across(second_sent)
    third_places = shard_places(outer_weight.shape[0])
    third_sent = half_rows(third_places, outer_weight)
    third_got = across(third_sent)

    small_pair = jnp.where(
        side == 0,
        jnp.concatenate([small, small_other], axis=1),
        jnp.concatenate([small_other, small], axis=1),
    ).astype(f32)
    bias_content = small_pair[0:1]
    bias_segment = small_pair[1:2]
    embed = small_pair[7:9]
    bias_inner = jnp.concatenate(
        [
            small_pair[9 : 9 + inner_rows, :part].reshape(-1),
            small_pair[9 : 9 + inner_rows, part:].reshape(-1),
        ]
    )
    table_row = small_pair[9 + inner_rows]
    table_full = jnp.concatenate(
        [
            table_row[: table_heads * bucket_count],
            table_row[part : part + table_heads * bucket_count],
        ]
    ).reshape(head_count, bucket_count)

    held = block_rows + mark_rows
    if len(gathered) == 1:
        stacked = gathered[0].reshape(count, held, width)
        content_all = stacked[:, :block_rows].reshape(length, width)
        meta_all = stacked[:, block_rows:]
    else:
        plan = []
        place = 0
        for at, piece in enumerate(gathered):
            for row in range(0, piece.shape[0], held):
                plan.append(
                    (at, window(row, block_rows), 0, window(place * block_rows, block_rows))
                )
                plan.append(
                    (at, window(row + block_rows, mark_rows), 1, window(place * mark_rows, mark_rows))
                )
                place += 1
        content_all, meta_all = moved(
            tuple(plan),
            [
                jax.ShapeDtypeStruct((length, width), bf16),
                jax.ShapeDtypeStruct((count * mark_rows, width), bf16),
            ],
            first_places,
            *gathered,
        )
        meta_all = meta_all.reshape(count, mark_rows, width)
    pairs = width // lanes
    runs = [(0, 0, width, 0, 0)]
    for pair in range(pairs):
        runs.append((1, pair * lanes, lanes, 1, 2 * pair * lanes))
        runs.append((2, pair * lanes, lanes, 1, (2 * pair + 1) * lanes))
    weight_query, weight_both = whole_rows(
        first_places, runs, (width, 2 * width), first_got, first_rest, query_weight, key_weight, value_weight
    )
    key_code, table, number, row_code = key_marks(meta_all, table_full, length)

    streams = jnp.concatenate([own_content, own_query], axis=0)
    query_full = dot(streams, weight_query)
    both = dot(content_all, weight_both).astype(bf16)
    attended, log_row, stack = attention_forward(
        query_full, bias_content, bias_segment, embed, row_code, key_code, both, table
    )

    hidden = inner_weight.shape[1]
    second_got, third_got, attended = lax.optimization_barrier((second_got, third_got, attended))
    second_rest = partner(second_got, 1)
    third_rest = partner(third_got, 1)
    half_places = jnp.concatenate(
        [first_places, core[None].astype(jnp.int32), third_places[1:]]
    )
    (
        out_low,
        normed,
        norm_rows,
        norm_scale,
        normed_low,
        active_low,
        slope,
        squares,
        weight_output,
        weight_inner,
    ) = forward_half(
        half_places,
        attended,
        own_content,
        own_query,
        output_weight,
        inner_weight,
        second_got,
        second_rest,
        small_pair,
        bias_inner[None],
    )
    out_low_other = partner(out_low, 1)
    normed_other = partner(normed_low, 1)
    active_other = partner(active_low, 1)
    (
        content_result,
        query_result,
        residual_back,
        out_back,
        outer_kept,
        outer_sent,
        inner_kept,
        inner_sent,
        attention_kept,
        attention_sent,
        vectors,
    ) = backward_half(
        half_places,
        active_low,
        slope,
        normed,
        norm_rows,
        norm_scale,
        weight_output,
        weight_inner,
        outer_weight,
        third_got,
        third_rest,
        small_pair,
        squares,
        content_cotangent[0],
        query_cotangent[0],
    )

    cuts, extra = split_bits(count)
    wide_cuts = [1] + cuts
    order_one = [0] + cuts
    order_two = cuts[:1] + [0] + cuts[1:]
    places_one = piece_places(order_one, cuts)
    places_two = piece_places(order_two, cuts)
    wide_places = piece_places([1, 0] + cuts, wide_cuts)
    places_out = jnp.concatenate([piece_places(cuts, cuts), core[None].astype(jnp.int32)])
    wide_places_out = piece_places(wide_cuts, wide_cuts)

    outer_keep, outer_send = product_pieces(
        places_one, active_low, active_other, outer_kept, partner(outer_sent, 1)
    )
    outer_got = pass_on(outer_send, order_one[0])
    inner_keep, inner_send = product_pieces(
        places_two,
        normed_low,
        normed_other,
        inner_kept,
        partner(inner_sent, 1),
        out_low,
        out_low_other,
        attention_kept,
        partner(attention_sent, 1),
    )
    inner_got = pass_on(inner_send, order_two[0])

    line = cuts[1:]
    last = cuts[2]

    def add_extra(value):
        for bit in extra:
            value = fold_last(value, partner(value, bit))
        return value

    query_back, both_back, small_back = attention_backward(
        stack,
        query_full,
        bias_segment,
        embed,
        row_code,
        key_code,
        both,
        table,
        number,
        after(out_back, outer_send, inner_send),
        attended,
        log_row,
    )
    order = Sequence(small_back)
    outer_got, inner_got = order.wait(outer_got, inner_got)
    outer_keep, outer_send = fold(outer_keep, outer_got)
    outer_send = order.ready(outer_send)
    outer_got = partner(outer_send, cuts[0])
    inner_keep, inner_send = fold(inner_keep, inner_got)
    inner_send = order.ready(inner_send)
    inner_got = across(inner_send)

    hidden_rows = hidden // part // sides
    tail_keep, tail_send = cut_gradient(
        wide_places,
        vectors,
        small_back,
        dot_tn(streams, query_back),
        dot_tn(content_all, order.ready(both_back)),
    )
    tail_send = order.ready(tail_send)
    tail_got = partner(tail_send, 1)
    outer_got = order.wait(outer_got)
    outer_keep, outer_send = fold(outer_keep, outer_got)
    outer_send = order.ready(outer_send)
    outer_got = partner(outer_send, line[0])
    content_share = share_of_content(order.ready(both_back), weight_both)
    share_keep, share_send = content_share[: count // 2], order.ready(content_share[count // 2 :])
    share_got = partner(share_send, 1)
    tail_got = order.wait(tail_got)
    tail_keep, tail_send = fold(tail_keep, tail_got)
    tail_send = order.ready(tail_send)
    tail_got = across(tail_send)
    inner_got = order.wait(inner_got)
    inner_keep, inner_send = fold(inner_keep, inner_got)
    inner_send = order.ready(inner_send)
    inner_got = partner(inner_send, line[0])
    share_got = order.wait(share_got)
    share_keep, share_send = fold(share_keep, share_got)
    share_send = order.ready(share_send)
    share_got = partner(share_send, cuts[0])
    outer_got = order.wait(outer_got)
    outer_keep, outer_send = fold(outer_keep, outer_got)
    outer_send = order.ready(outer_send)
    outer_got = partner(outer_send, last)
    inner_got = order.wait(inner_got)
    inner_keep, inner_send = fold(inner_keep, inner_got)
    inner_send = order.ready(inner_send)
    inner_got = partner(inner_send, last)
    outer_got = order.wait(outer_got)
    outer_value = order.ready(add_extra(fold_last(outer_keep, outer_got)))
    outer_got = partner(outer_value, last)
    tail_got = order.wait(tail_got)
    tail_keep, tail_send = fold(tail_keep, tail_got)
    tail_send = order.ready(tail_send)
    tail_got = partner(tail_send, cuts[0])
    inner_got = order.wait(inner_got)
    inner_value = order.ready(add_extra(fold_last(inner_keep, inner_got)))
    inner_got = partner(inner_value, last)
    outer_got = order.wait(outer_got)
    outer_value = order.ready(piled(outer_value, outer_got))
    outer_got = partner(outer_value, line[0])
    share_got = order.wait(share_got)
    share_keep, share_send = fold(share_keep, share_got)
    share_send = order.ready(share_send)
    share_got = partner(share_send, line[0])
    inner_got = order.wait(inner_got)
    inner_value = order.ready(piled(inner_value, inner_got))
    inner_got = partner(inner_value, line[0])
    tail_got = order.wait(tail_got)
    tail_keep, tail_send = fold(tail_keep, tail_got)
    tail_send = order.ready(tail_send)
    tail_got = partner(tail_send, line[0])
    outer_got = order.wait(outer_got)
    outer_value = order.ready(piled(outer_value, outer_got))
    outer_got = partner(outer_value, cuts[0])
    share_got = order.wait(share_got)
    share_keep, share_send = fold(share_keep, share_got)
    share_send = order.ready(share_send)
    share_got = partner(share_send, last)
    streams_back = residual_back + dot_nt(order.ready(query_back), weight_query)
    tail_got = order.wait(tail_got)
    tail_keep, tail_send = fold(tail_keep, tail_got)
    tail_send = order.ready(tail_send)
    tail_got = partner(tail_send, last)
    inner_got = order.wait(inner_got)
    inner_value = order.ready(piled(inner_value, inner_got))
    inner_got = partner(inner_value, cuts[0])
    tail_got = order.wait(tail_got)
    tail_value = order.ready(add_extra(fold_last(tail_keep, tail_got)))
    tail_got = partner(tail_value, last)
    outer_got = order.wait(outer_got)
    outer_value = order.ready(piled(outer_value, outer_got))
    outer_got = partner(outer_value, 1)
    share_got = order.wait(share_got)
    for bit in extra:
        share_keep, share_send = fold(share_keep, share_got)
        share_got = partner(share_send, bit)
    content_back = streams_back[:block_rows] + share_keep[0].astype(f32) + share_got[0].astype(f32)
    content_back, outer_got = order.wait(content_back, outer_got)
    (outer_weight_sum,) = lay_out(
        places_out,
        (((0, 0, width // 2, -1), (1, 0, width // 2, -2)),),
        outer_value,
        outer_got,
    )
    outer_weight_sum = order.ready(outer_weight_sum)
    tail_got = order.wait(tail_got)
    tail_value = order.ready(piled(tail_value, tail_got))
    tail_got = partner(tail_value, line[0])
    inner_got = order.wait(inner_got)
    inner_value = order.ready(piled(inner_value, inner_got))
    inner_got = partner(inner_value, 1)
    tail_got = order.wait(tail_got)
    tail_value = order.ready(piled(tail_value, tail_got))
    tail_got = partner(tail_value, cuts[0])
    inner_got = order.wait(inner_got)
    inner_weight_sum, output_weight_sum = lay_out(
        places_out,
        (
            ((0, 0, hidden // 2, -1), (1, 0, hidden // 2, -2)),
            ((0, hidden // 2, width // 2, -1), (1, hidden // 2, width // 2, -2)),
        ),
        inner_value,
        inner_got,
    )
    inner_weight_sum, output_weight_sum = order.ready(inner_weight_sum, output_weight_sum)
    tail_got = order.wait(tail_got)
    tail_value = order.ready(piled(tail_value, tail_got))
    tail_got = partner(tail_value, 1)
    plan = []
    for kind in range(3):
        row = []
        for pair in range(pairs):
            taken = pair * lanes if kind == 0 else width + (2 * pair + kind - 1) * lanes
            row.append((0, taken, lanes, pair * lanes))
        plan.append(tuple(row))
    plan.append(((0, 3 * width, lanes, 0),))
    query_weight_sum, key_weight_sum, value_weight_sum, vector_sums = lay_out(
        wide_places_out, tuple(plan), tail_value, tail_got
    )
    sums = vector_sums[:, :16].T
    table_sum = jnp.swapaxes(sums[4:6].reshape(2, -1, lanes)[:, :, :bucket_count], 0, 1).reshape(
        table_heads, bucket_count
    )
    inner_bias_sum = sums[11 : 11 + hidden_rows].reshape(-1)
    token_total = length * sides * width
    root_mean = jnp.sqrt(sums[11 + hidden_rows, :3] / token_total)
    return (
        content_result[None],
        query_result[None],
        content_back[None],
        streams_back[block_rows:][None],
        query_weight_sum,
        key_weight_sum,
        value_weight_sum,
        output_weight_sum,
        sums[0],
        sums[1],
        sums[2:4],
        table_sum,
        sums[6],
        sums[7],
        inner_weight_sum,
        inner_bias_sum,
        outer_weight_sum,
        sums[8],
        sums[9],
        sums[10],
        root_mean,
    )


def solution(mesh):
    tokens = P("wsh", "ctx", None)
    marks = P("wsh", "ctx")
    matrix = P("wsh", None)
    vector = P("wsh")
    placed = (
        (tokens, tokens, marks, marks, marks)
        + (matrix,) * 4
        + (vector, vector, P(None, "wsh"), matrix, vector, vector, matrix, vector, matrix)
        + (vector,) * 3
        + (tokens, tokens)
    )
    given = (
        (tokens,) * 4
        + (matrix,) * 4
        + (vector, vector, P(None, "wsh"), matrix, vector, vector, matrix, vector, matrix)
        + (vector,) * 3
        + (P(),)
    )
    return jax.shard_map(body, mesh=mesh, in_specs=placed, out_specs=given, check_vma=False)
```

profile of v0, /device:TPU:1, one launch (start us, length us, event | category | flops | bytes accessed | tf_op | source)
XLA Modules:
  0.0 366.8 jit_solution(7287600297415845877)
XLA Ops:
  25.0 6.5 %collective-permute-done.5.refs_1_ = bf16[144,768]{1,0:T(8,128)(2,1)S(1)} collective-permute-done((bf16[144,768]{1,0:T(8,128)(2,1)S(1)}, bf16[144,768]{1,0:T(8,128)(2,1)S(1)}, u32[]{:S(2)}, u32[]{:S(2)}) %collective-permute-start.5) | collective-permute-done | bytes 221216 | tf_op jit(solution)/shard_map/ppermute | solution.py:58
  60.7 6.8 %convolution_convert_fusion.both_ref = bf16[2048,1536]{1,0:T(8,128)(2,1)} fusion(bf16[2048,768]{1,0:T(8,128)(2,1)S(1)} %copy-done.53, bf16[768,1536]{1,0:T(8,128)(2,1)S(1)} %copy-done.24), kind=kOutput, calls=%fused_computation | convolution fusion | flops 4834983936 | bytes 11796480 | tf_op jit(solution)/shard_map/dot_general | solution.py:45
  67.5 17.8 %shard_map.388 = (f32[256,768]{1,0:T(8,128)}, f32[6,1,512]{2,1,0:T(1,128)}, bf16[6,512,256]{2,1,0:T(8,128)(2,1)}) custom-call(f32[256,768]{1,0:T(8,128)} %fusion.2.query_ref, f32[1,768]{1,0:T(1,128)} %get-tuple-element.419.content_bias_ref, f32[1,768]{1,0:T(1,128)} %get-tuple-element.418.segment_bias_ref, f32[2,768]{1,0:T(2,128)} %slice.110.embed_ref, ...), custom_call_target="tpu_custom_call" | custom-call | flops 17999998976 | tf_op jit(solution)/shard_map/pallas_call | solution.py:661
  85.3 17.7 %collective-permute-done.got_ref = bf16[192,3840]{1,0:T(8,128)(2,1)} collective-permute-done((bf16[192,3840]{1,0:T(8,128)(2,1)}, bf16[192,3840]{1,0:T(8,128)(2,1)}, u32[]{:S(2)}, u32[]{:S(2)}) %collective-permute-start) | collective-permute-done | bytes 1474592 | tf_op jit(solution)/shard_map/ppermute | solution.py:62
  108.4 10.8 %shard_map.389 = (bf16[256,768]{1,0:T(8,128)(2,1)S(1)}, f32[256,768]{1,0:T(8,128)S(1)}, f32[256,768]{1,0:T(8,128)S(1)}, f32[256,128]{1,0:T(8,128)S(1)}, bf16[256...) custom-call(s32[8]{0:T(128)S(1)} %concatenate.45.place_ref, ...), custom_call_target="tpu_custom_call" | custom-call | flops 8000000000 | tf_op jit(solution)/shard_map/pallas_call | solution.py:962
  123.6 15.1 %shard_map.390 = (bf16[128,768]{1,0:T(8,128)(2,1)}, bf16[128,768]{1,0:T(8,128)(2,1)}, f32[256,768]{1,0:T(8,128)}, bf16[256,768]{1,0:T(8,128)(2,1)}, bf16[256,384...) custom-call(s32[8]{0:T(128)} %copy-done.5, ...), custom_call_target="tpu_custom_call" | custom-call | flops 12000000000 | tf_op jit(solution)/shard_map/pallas_call | solution.py:985
  147.6 4.6 %shard_map.392 = (bf16[8,48,1920]{2,1,0:T(8,128)(2,1)S(1)}, bf16[8,48,1920]{2,1,0:T(8,128)(2,1)}) custom-call(s32[16]{0:T(128)S(1)} %add_add_fusion.1.place_ref, bf16[256,768]{1,0:T(8,128)(2,1)S(1)} %copy-done.22, bf16[256,768]{1,0:T(8,128)(2,1)} %collective-permute-done.18.refs_1_, bf16[256,1536]{1,0:T(8,128)(2,1)S(1)} %copy-done.27, ...), custom_call_target="tpu_custom_call" | custom-call | flops 4000000000 | tf_op jit(solution)/shard_map/pallas_call | solution.py:323
  152.5 4.7 %shard_map.391 = (bf16[8,192,384]{2,1,0:T(8,128)(2,1)S(1)}, bf16[8,192,384]{2,1,0:T(8,128)(2,1)}) custom-call(s32[16]{0:T(128)S(1)} %add_add_fusion.2.place_ref, bf16[256,3072]{1,0:T(8,128)(2,1)S(1)} %copy-done.8, bf16[256,3072]{1,0:T(8,128)(2,1)} %collective-permute-done.16.refs_1_, bf16[256,384]{1,0:T(8,128)(2,1)S(1)} %copy-done.36, ...), custom_call_target="tpu_custom_call" | custom-call | flops 4000000000 | tf_op jit(solution)/shard_map/pallas_call | solution.py:323
  159.3 34.5 %shard_map.393 = (bf16[256,768]{1,0:T(8,128)(2,1)}, bf16[2048,1536]{1,0:T(8,128)(2,1)}, f32[8,768]{1,0:T(8,128)}) custom-call(bf16[6,512,256]{2,1,0:T(8,128)(2,1)} %get-tuple-element.212.stack_ref, f32[256,768]{1,0:T(8,128)} %fusion.2.query_ref, f32[1,768]{1,0:T(1,128)} %get-tuple-element.418.segment_bias_ref, f32[2,768]{1,0:T(2,128)} %slice.110.embed_ref, ...), custom_call_target="tpu_custom_call" | custom-call | flops 33999998976 | tf_op jit(solution)/shard_map/pallas_call | solution.py:694
  200.3 7.4 %fusion.19.refs_1_ = f32[768,1536]{1,0:T(8,128)S(1)} fusion(bf16[2048,768]{1,0:T(8,128)(2,1)S(1)} %copy-done.54, bf16[2048,1536]{1,0:T(8,128)(2,1)} %get-tuple-element.250.back_ref), kind=kOutput, calls=%fused_computation.67 | convolution fusion | flops 4831838208 | bytes 14155776 | tf_op jit(solution)/shard_map/dot_general | solution.py:53
  217.8 6.5 %shard_map.398 = bf16[16,128,768]{2,1,0:T(8,128)(2,1)S(1)} custom-call(bf16[2048,1536]{1,0:T(8,128)(2,1)S(1)} %copy-done.23, bf16[768,1536]{1,0:T(8,128)(2,1)S(1)} %copy-done.25), custom_call_target="tpu_custom_call" | custom-call | flops 7000000000 | tf_op jit(solution)/shard_map/pallas_call | solution.py:276
  231.5 12.1 %collective-permute-done.26.received_ref = bf16[4,48,1920]{2,1,0:T(8,128)(2,1)S(1)} collective-permute-done((bf16[4,48,1920]{2,1,0:T(8,128)(2,1)S(1)}, bf16[4,48,1920]{2,1,0:T(8,128)(2,1)S(1)}, u32[]{:S(2)}, u32[]{:S(2)}) %collective-permute-start.26) | collective-permute-done | bytes 737312 | tf_op jit(solution)/shard_map/ppermute | solution.py:62
  247.6 7.1 %collective-permute-done.31.received_ref = bf16[2,48,1920]{2,1,0:T(8,128)(2,1)S(1)} collective-permute-done((bf16[2,48,1920]{2,1,0:T(8,128)(2,1)S(1)}, bf16[2,48,1920]{2,1,0:T(8,128)(2,1)S(1)}, u32[]{:S(2)}, u32[]{:S(2)}) %collective-permute-start.31) | collective-permute-done | bytes 368672 | tf_op jit(solution)/shard_map/ppermute | solution.py:58
  255.2 8.4 %collective-permute-done.34.received_ref = bf16[8,24,2432]{2,1,0:T(8,128)(2,1)S(1)} collective-permute-done((bf16[8,24,2432]{2,1,0:T(8,128)(2,1)S(1)}, bf16[8,24,2432]{2,1,0:T(8,128)(2,1)S(1)}, u32[]{:S(2)}, u32[]{:S(2)}) %collective-permute-start.34) | collective-permute-done | bytes 933920 | tf_op jit(solution)/shard_map/ppermute | solution.py:62
  270.5 10.1 %collective-permute-done.32.refs_1_ = bf16[1,192,384]{2,1,0:T(8,128)(2,1)S(1)} collective-permute-done((bf16[1,192,384]{2,1,0:T(8,128)(2,1)S(1)}, bf16[1,192,384]{2,1,0:T(8,128)(2,1)S(1)}, u32[]{:S(2)}, u32[]{:S(2)}) %collective-permute-start.32) | collective-permute-done | bytes 147488 | tf_op jit(solution)/shard_map/ppermute | solution.py:58
  282.4 5.0 %collective-permute-done.36.refs_1_ = bf16[2,192,384]{2,1,0:T(8,128)(2,1)S(1)} collective-permute-done((bf16[2,192,384]{2,1,0:T(8,128)(2,1)S(1)}, bf16[2,192,384]{2,1,0:T(8,128)(2,1)S(1)}, u32[]{:S(2)}, u32[]{:S(2)}) %collective-permute-start.36) | collective-permute-done | bytes 294944 | tf_op jit(solution)/shard_map/ppermute | solution.py:58
  292.5 4.8 %collective-permute-start.42 = (bf16[1,24,2432]{2,1,0:T(8,128)(2,1)S(1)}, bf16[1,24,2432]{2,1,0:T(8,128)(2,1)S(1)}, u32[]{:S(2)}, u32[]{:S(2)}) collective-permute-start(bf16[1,24,2432]{2,1,0:T(8,128)(2,1)S(1)} %get-tuple-element.339), channel_id=1, source_target_pairs={{0,16},{2,18},{4,20},{6,22},{8,24},{10,26},{12,28},{14,30},{16,0},... | collective-permute-start | bytes 350216 | tf_op jit(solution)/shard_map/ppermute | solution.py:58
  297.3 5.3 %collective-permute-done.42.received_ref = bf16[1,24,2432]{2,1,0:T(8,128)(2,1)S(1)} collective-permute-done((bf16[1,24,2432]{2,1,0:T(8,128)(2,1)S(1)}, bf16[1,24,2432]{2,1,0:T(8,128)(2,1)S(1)}, u32[]{:S(2)}, u32[]{:S(2)}) %collective-permute-start.42) | collective-permute-done | bytes 116768 | tf_op jit(solution)/shard_map/ppermute | solution.py:58
  302.7 4.5 %collective-permute-done.45.refs_1_ = bf16[1,24,2432]{2,1,0:T(8,128)(2,1)S(1)} collective-permute-done((bf16[1,24,2432]{2,1,0:T(8,128)(2,1)S(1)}, bf16[1,24,2432]{2,1,0:T(8,128)(2,1)S(1)}, u32[]{:S(2)}, u32[]{:S(2)}) %collective-permute-start.45) | collective-permute-done | bytes 116768 | tf_op jit(solution)/shard_map/ppermute | solution.py:58
  316.9 4.0 %collective-permute-start.43 = (bf16[2,48,1920]{2,1,0:T(8,128)(2,1)S(1)}, bf16[2,48,1920]{2,1,0:T(8,128)(2,1)S(1)}, u32[]{:S(2)}, u32[]{:S(2)}) collective-permute-start(bf16[2,48,1920]{2,1,0:T(8,128)(2,1)S(1)} %shard_map.409.refs_0_), channel_id=1, source_target_pairs={{0,8},{2,10},{4,12},{6,14},{8,0},{10,2},{12,4},{14,6},{16,24},{18,... | collective-permute-start | bytes 1105928 | tf_op jit(solution)/shard_map/ppermute | solution.py:58
  321.6 6.1 %collective-permute-done.43.refs_1_ = bf16[2,48,1920]{2,1,0:T(8,128)(2,1)S(1)} collective-permute-done((bf16[2,48,1920]{2,1,0:T(8,128)(2,1)S(1)}, bf16[2,48,1920]{2,1,0:T(8,128)(2,1)S(1)}, u32[]{:S(2)}, u32[]{:S(2)}) %collective-permute-start.43) | collective-permute-done | bytes 368672 | tf_op jit(solution)/shard_map/ppermute | solution.py:58
  330.9 6.2 %collective-permute-start.48 = (bf16[8,24,2432]{2,1,0:T(8,128)(2,1)S(1)}, bf16[8,24,2432]{2,1,0:T(8,128)(2,1)S(1)}, u32[]{:S(2)}, u32[]{:S(2)}) collective-permute-start(bf16[8,24,2432]{2,1,0:T(8,128)(2,1)S(1)} %shard_map.419.refs_0_), channel_id=1, source_target_pairs={{0,2},{2,0},{4,6},{6,4},{8,10},{10,8},{12,14},{14,12},{16,18},{18,... | collective-permute-start | bytes 2801672 | tf_op jit(solution)/shard_map/ppermute | solution.py:58
  339.4 9.6 %collective-permute-done.39 = bf16[1,128,768]{2,1,0:T(8,128)(2,1)S(1)} collective-permute-done((bf16[1,128,768]{2,1,0:T(8,128)(2,1)S(1)}, bf16[1,128,768]{2,1,0:T(8,128)(2,1)S(1)}, u32[]{:S(2)}, u32[]{:S(2)}) %collective-permute-start.39) | collective-permute-done | bytes 196640 | tf_op jit(solution)/shard_map/ppermute | solution.py:58
  353.9 4.6 %shard_map.420 = (f32[384,768]{1,0:T(8,128)}, f32[384,768]{1,0:T(8,128)}, f32[384,768]{1,0:T(8,128)}, f32[384,128]{1,0:T(8,128)S(1)}) custom-call(s32[16]{0:T(128)S(1)} %add_add_fusion.place_ref, bf16[8,24,2432]{2,1,0:T(8,128)(2,1)S(1)} %shard_map.419.refs_0_, bf16[8,24,2432]{2,1,0:T(8,128)(2,1)S(1)} %collective-permute-done.48.refs_1_), custom_call_target="tpu_custom_call" | custom-call | flops 3000000000 | tf_op jit(solution)/shard_map/pallas_call | solution.py:409
  (294 shorter events, 144.6 us)
Async XLA Ops:
  7.7 26.1 %collective-permute-start.8 = (bf16[144,768]{1,0:T(8,128)(2,1)S(1)}, bf16[144,768]{1,0:T(8,128)(2,1)S(1)}, u32[]{:S(2)}, u32[]{:S(2)}) collective-permute-start(bf16[144,768]{1,0:T(8,128)(2,1)S(1)} %pad_maximum_fusion.4.refs_0_), channel_id=1, source_target_pairs={{0,4},{2,6},{4,0},{6,2},{8,12},{10,14},{12,8},{14,10},{16,20},{18,... | collective-permute-start | bytes 663560 | tf_op jit(solution)/shard_map/ppermute | solution.py:58
  13.1 18.4 %collective-permute-start.5 = (bf16[144,768]{1,0:T(8,128)(2,1)S(1)}, bf16[144,768]{1,0:T(8,128)(2,1)S(1)}, u32[]{:S(2)}, u32[]{:S(2)}) collective-permute-start(bf16[144,768]{1,0:T(8,128)(2,1)S(1)} %pad_maximum_fusion.4.refs_0_), channel_id=1, source_target_pairs={{0,16},{2,18},{4,20},{6,22},{8,24},{10,26},{12,28},{14,30},{16,0},... | collective-permute-start | bytes 663560 | tf_op jit(solution)/shard_map/ppermute | solution.py:58
  18.3 29.2 %collective-permute-start.2 = (bf16[192,2304]{1,0:T(8,128)(2,1)}, bf16[192,2304]{1,0:T(8,128)(2,1)S(1)}, u32[]{:S(2)}, u32[]{:S(2)}) collective-permute-start(bf16[192,2304]{1,0:T(8,128)(2,1)} %shard_map.384), channel_id=1, source_target_pairs={{0,1},{1,0},{2,3},{3,2},{4,5},{5,4},{6,7},{7,6},{8,9},{9,8},{10,11... | collective-permute-start | bytes 2654216 | tf_op jit(solution)/shard_map/ppermute | solution.py:62
  35.0 14.0 %collective-permute-start.12 = (bf16[576,768]{1,0:T(8,128)(2,1)}, bf16[576,768]{1,0:T(8,128)(2,1)}, u32[]{:S(2)}, u32[]{:S(2)}) collective-permute-start(bf16[576,768]{1,0:T(8,128)(2,1)} %constant_dynamic-update-slice_fusion), channel_id=1, source_target_pairs={{0,2},{2,0},{4,6},{6,4},{8,10},{10,8},{12,14},{14,12},{16,18},{18,... | collective-permute-start | bytes 2654216 | tf_op jit(solution)/shard_map/ppermute | solution.py:58
  43.7 41.6 %collective-permute-start.1 = (bf16[768,768]{1,0:T(8,128)(2,1)}, bf16[768,768]{1,0:T(8,128)(2,1)}, u32[]{:S(2)}, u32[]{:S(2)}) collective-permute-start(bf16[768,768]{1,0:T(8,128)(2,1)} %shard_map.383), channel_id=1, source_target_pairs={{0,1},{1,0},{2,3},{3,2},{4,5},{5,4},{6,7},{7,6},{8,9},{9,8},{10,11... | collective-permute-start | bytes 3538952 | tf_op jit(solution)/shard_map/ppermute | solution.py:62
  46.6 56.4 %collective-permute-start = (bf16[192,3840]{1,0:T(8,128)(2,1)}, bf16[192,3840]{1,0:T(8,128)(2,1)}, u32[]{:S(2)}, u32[]{:S(2)}) collective-permute-start(bf16[192,3840]{1,0:T(8,128)(2,1)} %shard_map.382), channel_id=1, source_target_pairs={{0,1},{1,0},{2,3},{3,2},{4,5},{5,4},{6,7},{7,6},{8,9},{9,8},{10,11... | collective-permute-start | bytes 4423688 | tf_op jit(solution)/shard_map/ppermute | solution.py:62
  104.0 19.6 %collective-permute-start.15 = (bf16[768,768]{1,0:T(8,128)(2,1)}, bf16[768,768]{1,0:T(8,128)(2,1)}, u32[]{:S(2)}, u32[]{:S(2)}) collective-permute-start(bf16[768,768]{1,0:T(8,128)(2,1)} %collective-permute-done.1.got_ref), channel_id=1, source_target_pairs={{0,2},{2,0},{4,6},{6,4},{8,10},{10,8},{12,14},{14,12},{16,18},{18,... | collective-permute-start | bytes 3538952 | tf_op jit(solution)/shard_map/ppermute | solution.py:58
  123.2 29.3 %collective-permute-start.16 = (bf16[256,3072]{1,0:T(8,128)(2,1)}, bf16[256,3072]{1,0:T(8,128)(2,1)}, u32[]{:S(2)}, u32[]{:S(2)}) collective-permute-start(bf16[256,3072]{1,0:T(8,128)(2,1)} %get-tuple-element.200.active_ref.refs_0_), channel_id=1, source_target_pairs={{0,2},{2,0},{4,6},{6,4},{8,10},{10,8},{12,14},{14,12},{16,18},{18,... | collective-permute-start | bytes 4718600 | tf_op jit(solution)/shard_map/ppermute | solution.py:58
  152.2 43.2 %collective-permute-start.23 = (bf16[8,48,1920]{2,1,0:T(8,128)(2,1)}, bf16[8,48,1920]{2,1,0:T(8,128)(2,1)}, u32[]{:S(2)}, u32[]{:S(2)}) collective-permute-start(bf16[8,48,1920]{2,1,0:T(8,128)(2,1)} %get-tuple-element.224), channel_id=1, source_target_pairs={{0,4},{2,6},{4,0},{6,2},{8,12},{10,14},{12,8},{14,10},{16,20},{18,... | collective-permute-start | bytes 4423688 | tf_op jit(solution)/shard_map/ppermute | solution.py:58
  158.2 37.3 %collective-permute-start.22 = (bf16[8,192,384]{2,1,0:T(8,128)(2,1)}, bf16[8,192,384]{2,1,0:T(8,128)(2,1)}, u32[]{:S(2)}, u32[]{:S(2)}) collective-permute-start(bf16[8,192,384]{2,1,0:T(8,128)(2,1)} %get-tuple-element.217), channel_id=1, source_target_pairs={{0,1},{1,0},{2,3},{3,2},{4,5},{5,4},{6,7},{7,6},{8,9},{9,8},{10,11... | collective-permute-start | bytes 3538952 | tf_op jit(solution)/shard_map/ppermute | solution.py:62
  199.0 14.2 %collective-permute-start.24 = (bf16[4,192,384]{2,1,0:T(8,128)(2,1)S(1)}, bf16[4,192,384]{2,1,0:T(8,128)(2,1)S(1)}, u32[]{:S(2)}, u32[]{:S(2)}) collective-permute-start(bf16[4,192,384]{2,1,0:T(8,128)(2,1)S(1)} %get-tuple-element.235), channel_id=1, source_target_pairs={{0,4},{2,6},{4,0},{6,2},{8,12},{10,14},{12,8},{14,10},{16,20},{18,... | collective-permute-start | bytes 1769480 | tf_op jit(solution)/shard_map/ppermute | solution.py:58
  209.0 17.6 %collective-permute-start.27 = (bf16[16,24,2432]{2,1,0:T(8,128)(2,1)S(1)}, bf16[16,24,2432]{2,1,0:T(8,128)(2,1)S(1)}, u32[]{:S(2)}, u32[]{:S(2)}) collective-permute-start(bf16[16,24,2432]{2,1,0:T(8,128)(2,1)S(1)} %get-tuple-element.256), channel_id=1, source_target_pairs={{0,2},{2,0},{4,6},{6,4},{8,10},{10,8},{12,14},{14,12},{16,18},{18,... | collective-permute-start | bytes 5603336 | tf_op jit(solution)/shard_map/ppermute | solution.py:58
  224.6 22.4 %collective-permute-start.25 = (bf16[8,128,768]{2,1,0:T(8,128)(2,1)S(1)}, bf16[8,128,768]{2,1,0:T(8,128)(2,1)S(1)}, u32[]{:S(2)}, u32[]{:S(2)}) collective-permute-start(bf16[8,128,768]{2,1,0:T(8,128)(2,1)S(1)} %get-tuple-element.252), channel_id=1, source_target_pairs={{0,2},{2,0},{4,6},{6,4},{8,10},{10,8},{12,14},{14,12},{16,18},{18,... | collective-permute-start | bytes 4718600 | tf_op jit(solution)/shard_map/ppermute | solution.py:58
  226.3 17.3 %collective-permute-start.26 = (bf16[4,48,1920]{2,1,0:T(8,128)(2,1)S(1)}, bf16[4,48,1920]{2,1,0:T(8,128)(2,1)S(1)}, u32[]{:S(2)}, u32[]{:S(2)}) collective-permute-start(bf16[4,48,1920]{2,1,0:T(8,128)(2,1)S(1)} %copy-done.12), channel_id=1, source_target_pairs={{0,1},{1,0},{2,3},{3,2},{4,5},{5,4},{6,7},{7,6},{8,9},{9,8},{10,11... | collective-permute-start | bytes 2211848 | tf_op jit(solution)/shard_map/ppermute | solution.py:62
  227.1 36.5 %collective-permute-start.34 = (bf16[8,24,2432]{2,1,0:T(8,128)(2,1)S(1)}, bf16[8,24,2432]{2,1,0:T(8,128)(2,1)S(1)}, u32[]{:S(2)}, u32[]{:S(2)}) collective-permute-start(bf16[8,24,2432]{2,1,0:T(8,128)(2,1)S(1)} %get-tuple-element.292), channel_id=1, source_target_pairs={{0,1},{1,0},{2,3},{3,2},{4,5},{5,4},{6,7},{7,6},{8,9},{9,8},{10,11... | collective-permute-start | bytes 2801672 | tf_op jit(solution)/shard_map/ppermute | solution.py:62
  228.3 19.0 %collective-permute-start.29 = (bf16[2,192,384]{2,1,0:T(8,128)(2,1)S(1)}, bf16[2,192,384]{2,1,0:T(8,128)(2,1)S(1)}, u32[]{:S(2)}, u32[]{:S(2)}) collective-permute-start(bf16[2,192,384]{2,1,0:T(8,128)(2,1)S(1)} %get-tuple-element.272), channel_id=1, source_target_pairs={{0,8},{2,10},{4,12},{6,14},{8,0},{10,2},{12,4},{14,6},{16,24},{18,... | collective-permute-start | bytes 884744 | tf_op jit(solution)/shard_map/ppermute | solution.py:58
  263.8 18.3 %collective-permute-start.37 = (bf16[4,24,2432]{2,1,0:T(8,128)(2,1)S(1)}, bf16[4,24,2432]{2,1,0:T(8,128)(2,1)S(1)}, u32[]{:S(2)}, u32[]{:S(2)}) collective-permute-start(bf16[4,24,2432]{2,1,0:T(8,128)(2,1)S(1)} %get-tuple-element.311), channel_id=1, source_target_pairs={{0,4},{2,6},{4,0},{6,2},{8,12},{10,14},{12,8},{14,10},{16,20},{18,... | collective-permute-start | bytes 1400840 | tf_op jit(solution)/shard_map/ppermute | solution.py:58
  266.2 14.3 %collective-permute-start.32 = (bf16[1,192,384]{2,1,0:T(8,128)(2,1)S(1)}, bf16[1,192,384]{2,1,0:T(8,128)(2,1)S(1)}, u32[]{:S(2)}, u32[]{:S(2)}) collective-permute-start(bf16[1,192,384]{2,1,0:T(8,128)(2,1)S(1)} %shard_map.404.refs_0_), channel_id=1, source_target_pairs={{0,16},{2,18},{4,20},{6,22},{8,24},{10,26},{12,28},{14,30},{16,0},... | collective-permute-start | bytes 442376 | tf_op jit(solution)/shard_map/ppermute | solution.py:58
  287.5 24.8 %collective-permute-start.40 = (bf16[4,192,384]{2,1,0:T(8,128)(2,1)S(1)}, bf16[4,192,384]{2,1,0:T(8,128)(2,1)S(1)}, u32[]{:S(2)}, u32[]{:S(2)}) collective-permute-start(bf16[4,192,384]{2,1,0:T(8,128)(2,1)S(1)} %shard_map.411.refs_0_), channel_id=1, source_target_pairs={{0,4},{2,6},{4,0},{6,2},{8,12},{10,14},{12,8},{14,10},{16,20},{18,... | collective-permute-start | bytes 1769480 | tf_op jit(solution)/shard_map/ppermute | solution.py:58
  287.8 33.5 %collective-permute-start.28 = (bf16[4,128,768]{2,1,0:T(8,128)(2,1)S(1)}, bf16[4,128,768]{2,1,0:T(8,128)(2,1)S(1)}, u32[]{:S(2)}, u32[]{:S(2)}) collective-permute-start(bf16[4,128,768]{2,1,0:T(8,128)(2,1)S(1)} %get-tuple-element.270), channel_id=1, source_target_pairs={{0,4},{2,6},{4,0},{6,2},{8,12},{10,14},{12,8},{14,10},{16,20},{18,... | collective-permute-start | bytes 2359304 | tf_op jit(solution)/shard_map/ppermute | solution.py:58
  312.4 38.4 %collective-permute-start.44 = (bf16[8,192,384]{2,1,0:T(8,128)(2,1)S(1)}, bf16[8,192,384]{2,1,0:T(8,128)(2,1)S(1)}, u32[]{:S(2)}, u32[]{:S(2)}) collective-permute-start(bf16[8,192,384]{2,1,0:T(8,128)(2,1)S(1)} %shard_map.416.refs_0_), channel_id=1, source_target_pairs={{0,2},{2,0},{4,6},{6,4},{8,10},{10,8},{12,14},{14,12},{16,18},{18,... | collective-permute-start | bytes 3538952 | tf_op jit(solution)/shard_map/ppermute | solution.py:58
  321.5 15.7 %collective-permute-start.35 = (bf16[2,128,768]{2,1,0:T(8,128)(2,1)S(1)}, bf16[2,128,768]{2,1,0:T(8,128)(2,1)S(1)}, u32[]{:S(2)}, u32[]{:S(2)}) collective-permute-start(bf16[2,128,768]{2,1,0:T(8,128)(2,1)S(1)} %get-tuple-element.308), channel_id=1, source_target_pairs={{0,8},{2,10},{4,12},{6,14},{8,0},{10,2},{12,4},{14,6},{16,24},{18,... | collective-permute-start | bytes 1179656 | tf_op jit(solution)/shard_map/ppermute | solution.py:58
  327.8 22.2 %collective-permute-start.49 = (bf16[4,48,1920]{2,1,0:T(8,128)(2,1)S(1)}, bf16[4,48,1920]{2,1,0:T(8,128)(2,1)S(1)}, u32[]{:S(2)}, u32[]{:S(2)}) collective-permute-start(bf16[4,48,1920]{2,1,0:T(8,128)(2,1)S(1)} %shard_map.414.refs_0_), channel_id=1, source_target_pairs={{0,4},{2,6},{4,0},{6,2},{8,12},{10,14},{12,8},{14,10},{16,20},{18,... | collective-permute-start | bytes 2211848 | tf_op jit(solution)/shard_map/ppermute | solution.py:58
  330.9 23.0 %collective-permute-start.48 = (bf16[8,24,2432]{2,1,0:T(8,128)(2,1)S(1)}, bf16[8,24,2432]{2,1,0:T(8,128)(2,1)S(1)}, u32[]{:S(2)}, u32[]{:S(2)}) collective-permute-start(bf16[8,24,2432]{2,1,0:T(8,128)(2,1)S(1)} %shard_map.419.refs_0_), channel_id=1, source_target_pairs={{0,2},{2,0},{4,6},{6,4},{8,10},{10,8},{12,14},{14,12},{16,18},{18,... | collective-permute-start | bytes 2801672 | tf_op jit(solution)/shard_map/ppermute | solution.py:58
  (82 other events, 541.0 us)
where the time goes:
time: 368 us; the launch traced here: 367 us
  Pallas kernels  126 us (34%)
  waiting for transfers between devices  116 us (32%)
  starting transfers between devices  63.3 us (17%)
  local copies, waits for them, and re-layouts  35 us (10%)
  matrix products  17.7 us (5%)
  other arithmetic  7.05 us (2%)
    ppermute x44, waiting for transfers between devices, partner(): lax.ppermute(value, 'ctx', [(place, place ^ bit) for place in range(count)])  77.7 us
    ppermute x44, starting transfers between devices, partner(): lax.ppermute(value, 'ctx', [(place, place ^ bit) for place in range(count)])  56.7 us
    ppermute x7, waiting for transfers between devices, across(): return lax.ppermute(value, 'wsh', [(0, 1), (1, 0)])  38.2 us
    pallas_call x1, Pallas kernels, attention_backward(): pl.pallas_call(backward_kernel, grid=(pairs,), in_specs=[spec['stack'], s...  34.5 us
    unnamed x124, local copies, waits for them, and re-layouts  29.1 us
    pallas_call x1, Pallas kernels, attention_forward(): pl.pallas_call(forward_kernel, grid=(pairs,), in_specs=[spec['rows'], spe...  17.8 us
    pallas_call x1, Pallas kernels, backward_half(): pl.pallas_call(backward_half_kernel, in_specs=[in_smem] + [in_vmem] * len...  15.1 us
    pallas_call x3, Pallas kernels, lay_out(): pl.pallas_call(functools.partial(lay_out_kernel, plan), in_specs=[pl.Bloc...  11.6 us
  transfers between devices with their start and end apart: 51, of which 23 were waited for; matrix products, arithmetic and copies ran while one was open for 8% of the time, Pallas kernels for 32%

commit v1 on v0

--- a/solution.py
+++ b/solution.py
@@ -20,6 +20,11 @@
 free = pl.CostEstimate(flops=0, bytes_accessed=0, transcendentals=0)
 in_vmem = pl.BlockSpec(memory_space=pltpu.VMEM)
 in_smem = pl.BlockSpec(memory_space=pltpu.SMEM)
+
+
+def resident(value):
+    rank = len(value.shape)
+    return pl.BlockSpec(value.shape, lambda at: (0,) * rank, pipeline_mode=pl.Buffered(1))
 
 
 def takes(microseconds):
@@ -90,9 +95,8 @@
     near = partner(own, low)
     first = [own] + [partner(own, place) for place in (bits[3], bits[2], bits[2] | bits[3])]
     second = [near] + [partner(block, low) for block in first[1:]]
-    first_core = partner(jnp.concatenate(first, axis=0), 1)
-    second_core = partner(jnp.concatenate(second, axis=0), 1)
-    return first + second + [first_core, second_core]
+    others = partner(jnp.concatenate(first + second, axis=0), 1)
+    return first + second + [others]
 
 
 def move_kernel(plan, inputs, place_ref, *refs):
@@ -102,15 +106,14 @@
 
 
 def moved(plan, shapes, places, *sources):
-    whole = pl.BlockSpec(memory_space=pltpu.VMEM)
-    size = sum(shape.size for shape in shapes)
     return pl.pallas_call(
         functools.partial(move_kernel, plan, len(sources)),
-        in_specs=[pl.BlockSpec(memory_space=pltpu.SMEM)] + [whole] * len(sources),
-        out_specs=[whole] * len(shapes),
+        grid=(1,),
+        in_specs=[in_smem] + [resident(value) for value in sources],
+        out_specs=[resident(shape) for shape in shapes],
         out_shape=shapes,
-        compiler_params=pltpu.CompilerParams(vmem_limit_bytes=48 << 20),
-        cost_estimate=takes(3),
+        compiler_params=pltpu.CompilerParams(vmem_limit_bytes=40 << 20),
+        cost_estimate=free,
     )(places, *sources)
 
 
@@ -126,8 +129,8 @@
     return make
 
 
-def half_rows(places, *shards):
-    rows = shards[0].shape[0] // 2
+def half_rows(places, cut, *shards):
+    rows = shards[0].shape[0] // 2 // cut
     plan = []
     left = 0
     for at, shard in enumerate(shards):
@@ -161,6 +164,19 @@
     return moved(tuple(plan), shapes, places, got, rest, *shards)
 
 
+def quarter_places(rows):
+    core = lax.axis_index("ctx") % 2
+    near = (lax.axis_index("ctx") // 2) % 2
+    side = lax.axis_index("wsh")
+    quarter = rows // 4
+    base = (1 - side) * rows
+    spots = [(core, near), (core, 1 - near), (1 - core, near), (1 - core, 1 - near)]
+    return jnp.stack(
+        [(2 * core + near) * quarter, side * rows]
+        + [base + (2 * first + second) * quarter for first, second in spots]
+    ).astype(jnp.int32)
+
+
 def shard_places(rows):
     core = lax.axis_index("ctx") % 2
     side = lax.axis_index("wsh")
@@ -184,6 +200,26 @@
 
 def pass_on(value, bit):
     return across(value) if bit == 0 else partner(value, bit)
+
+
+def pass_mixed(value, even_bit, odd_bit):
+    count = lax.axis_size("ctx")
+    pairs = []
+    for place in range(count):
+        bit = odd_bit if place % 2 else even_bit
+        for side in range(2):
+            other = (place, 1 - side) if bit == 0 else (place ^ bit, side)
+            pairs.append((2 * place + side, 2 * other[0] + other[1]))
+    return lax.ppermute(value, ("ctx", "wsh"), pairs)
+
+
+def by_core(even, odd, half):
+    core = lax.axis_index("ctx") % 2
+    return jnp.where(
+        core == 0,
+        jnp.concatenate([even[:half], odd[half:]]),
+        jnp.concatenate([odd[:half], even[half:]]),
+    )
 
 
 class Sequence:
@@ -225,8 +261,9 @@
     piece = jax.ShapeDtypeStruct((keep.shape[0] // parts,) + keep.shape[1:], bf16)
     return pl.pallas_call(
         fold_kernel,
-        in_specs=[in_vmem] * 2,
-        out_specs=[in_vmem] * parts,
+        grid=(1,),
+        in_specs=[resident(keep)] * 2,
+        out_specs=[resident(piece)] * parts,
         out_shape=[piece] * parts,
         compiler_params=pltpu.CompilerParams(vmem_limit_bytes=40 << 20),
         cost_estimate=free,
@@ -283,7 +320,7 @@
         out_specs=pl.BlockSpec((2, lanes, width), lambda at: (at, 0, 0)),
         out_shape=jax.ShapeDtypeStruct((count // lanes, lanes, width), bf16),
         compiler_params=pltpu.CompilerParams(vmem_limit_bytes=40 << 20),
-        cost_estimate=takes(7),
+        cost_estimate=free,
     )(both_back, weight_both)
 
 
@@ -319,14 +356,14 @@
     height = operands[0].shape[1]
     columns = sum(operands[4 * group + 2].shape[1] for group in range(groups))
     piece = jax.ShapeDtypeStruct((half, height // (2 * half), columns), bf16)
-    whole = pl.BlockSpec(memory_space=pltpu.VMEM)
     return pl.pallas_call(
         functools.partial(product_kernel, groups),
-        in_specs=[pl.BlockSpec(memory_space=pltpu.SMEM)] + [whole] * len(operands),
-        out_specs=[whole, whole],
+        grid=(1,),
+        in_specs=[in_smem] + [resident(value) for value in operands],
+        out_specs=[resident(piece)] * 2,
         out_shape=[piece, piece],
         scratch_shapes=[pltpu.VMEM((height, columns), f32)],
-        compiler_params=pltpu.CompilerParams(vmem_limit_bytes=40 << 20),
+        compiler_params=pltpu.CompilerParams(vmem_limit_bytes=60 << 20),
         cost_estimate=takes(4),
     )(places, *operands)
 
@@ -364,15 +401,15 @@
     height = parts[0].shape[0]
     columns = sum(part.shape[1] for part in parts) + lanes
     piece = jax.ShapeDtypeStruct((half, height // (2 * half), columns), bf16)
-    whole = pl.BlockSpec(memory_space=pltpu.VMEM)
     return pl.pallas_call(
         cut_kernel,
-        in_specs=[pl.BlockSpec(memory_space=pltpu.SMEM)] + [whole] * (len(parts) + 2),
-        out_specs=[whole, whole],
+        grid=(1,),
+        in_specs=[in_smem] + [resident(value) for value in (vectors, small) + parts],
+        out_specs=[resident(piece)] * 2,
         out_shape=[piece, piece],
         scratch_shapes=[pltpu.VMEM((height, lanes), f32)],
         compiler_params=pltpu.CompilerParams(vmem_limit_bytes=40 << 20),
-        cost_estimate=takes(3),
+        cost_estimate=free,
     )(places, vectors, small, *parts)
 
 
@@ -400,7 +437,6 @@
 
 
 def lay_out(places, plan, *pieces):
-    whole = pl.BlockSpec(memory_space=pltpu.VMEM)
     shapes = []
     halves = 2 if places.shape[0] > pieces[0].shape[0] + 1 else 1
     for runs in plan:
@@ -408,10 +444,11 @@
         shapes.append(jax.ShapeDtypeStruct((halves * count * rows, sum(run[2] for run in runs)), f32))
     return pl.pallas_call(
         functools.partial(lay_out_kernel, plan),
-        in_specs=[pl.BlockSpec(memory_space=pltpu.SMEM)] + [whole] * len(pieces),
-        out_specs=[whole] * len(plan),
+        grid=(1,),
+        in_specs=[in_smem] + [resident(value) for value in pieces],
+        out_specs=[resident(shape) for shape in shapes],
         out_shape=shapes,
-        compiler_params=pltpu.CompilerParams(vmem_limit_bytes=48 << 20),
+        compiler_params=pltpu.CompilerParams(vmem_limit_bytes=40 << 20),
         cost_estimate=takes(3),
     )(places, *pieces)
 
@@ -681,7 +718,7 @@
         compiler_params=pltpu.CompilerParams(
             dimension_semantics=("arbitrary",), vmem_limit_bytes=60 << 20
         ),
-        cost_estimate=takes(18),
+        cost_estimate=free,
     )(query_full, bias_content, bias_segment, embed, row_code, key_code, both, table)
 
 
@@ -760,12 +797,10 @@
     bounds = tuple(
         1 + level * level * length // (bucket_steps * bucket_steps) for level in range(bucket_steps)
     )
-    whole = pl.BlockSpec(memory_space=pltpu.VMEM)
-    scalars = pl.BlockSpec(memory_space=pltpu.SMEM)
     return pl.pallas_call(
         functools.partial(marks_kernel, bounds),
-        in_specs=[whole, scalars],
-        out_specs=[whole] * 4,
+        in_specs=[in_vmem, in_smem],
+        out_specs=[in_vmem] * 4,
         out_shape=[
             jax.ShapeDtypeStruct((blocks * lanes, lanes), bf16),
             jax.ShapeDtypeStruct((heads, blocks, 2 * lanes), f32),
@@ -773,17 +808,29 @@
             jax.ShapeDtypeStruct((2 * lanes, lanes), f32),
         ],
         compiler_params=pltpu.CompilerParams(vmem_limit_bytes=40 << 20),
-        cost_estimate=takes(2),
+        cost_estimate=free,
     )(meta_all, table_full)
 
 
-def assemble(target_ref, own_ref, got_ref, rest_ref, columns, places):
-    rows = own_ref.shape[0]
-    half = rows // 2
-    own, got, rest = [pl.multiple_of(place, 16) for place in places]
-    target_ref[pl.ds(own, rows), :] = own_ref[...]
-    target_ref[pl.ds(got, half), :] = got_ref[:, columns]
-    target_ref[pl.ds(rest, half), :] = rest_ref[:, columns]
+def assemble_pair(first_ref, second_ref, first_own_ref, second_own_ref, parts, places):
+    own, *others = [pl.multiple_of(place, 16) for place in places]
+    first_ref[pl.ds(own, first_own_ref.shape[0]), :] = first_own_ref[...]
+    second_ref[pl.ds(own, second_own_ref.shape[0]), :] = second_own_ref[...]
+    width, hidden = first_ref.shape[1], second_ref.shape[1]
+    span = (width + hidden) // 2
+    for (part_ref, base), other in zip(parts, others, strict=True):
+        quarter = part_ref.shape[0] // 2
+        rows = pl.ds(other, quarter)
+        first_ref[rows, :] = part_ref[:quarter, base : base + width]
+        second_ref[rows, : span - width] = part_ref[:quarter, base + width : base + span]
+        second_ref[rows, span - width :] = part_ref[quarter:, base : base + span]
+
+
+def assemble(target_ref, own_ref, parts, columns, places):
+    own, *others = [pl.multiple_of(place, 16) for place in places]
+    target_ref[pl.ds(own, own_ref.shape[0]), :] = own_ref[...]
+    for part_ref, other in zip(parts, others, strict=True):
+        target_ref[pl.ds(other, part_ref.shape[0]), :] = part_ref[:, columns]
 
 
 def forward_half_kernel(
@@ -794,7 +841,9 @@
     output_own_ref,
     inner_own_ref,
     got_ref,
+    near_ref,
     rest_ref,
+    far_ref,
     vector_ref,
     bias_ref,
     out_low_ref,
@@ -811,9 +860,16 @@
     width = attended_ref.shape[1]
     hidden = inner_own_ref.shape[1]
     half = content_ref.shape[0]
-    places = (place_ref[1], place_ref[2], place_ref[3])
-    assemble(weight_output_ref, output_own_ref, got_ref, rest_ref, slice(0, width), places)
-    assemble(weight_inner_ref, inner_own_ref, got_ref, rest_ref, slice(width, width + hidden), places)
+    places = [place_ref[at] for at in range(1, 6)]
+    base = 3 * width
+    assemble_pair(
+        weight_output_ref,
+        weight_inner_ref,
+        output_own_ref,
+        inner_own_ref,
+        ((got_ref, base), (near_ref, 0), (rest_ref, base), (far_ref, 0)),
+        places,
+    )
     out_low = attended_ref[...].astype(bf16)
     out_low_ref[...] = out_low
     attention_out = dot(out_low, weight_output_ref[...])
@@ -880,14 +936,13 @@
     width = normed_ref.shape[1]
     hidden = active_ref.shape[1]
     count = content_cotangent_ref.shape[0]
-    core = place_ref[4]
+    core = place_ref[6]
     assemble(
         weight_outer_ref,
         outer_own_ref,
-        got_ref,
-        rest_ref,
+        (got_ref, rest_ref),
         slice(0, width),
-        (place_ref[5], place_ref[6], place_ref[7]),
+        [place_ref[at] for at in range(7, 10)],
     )
 
     def give(value_ref, kept_ref, sent_ref):
@@ -944,9 +999,9 @@
     sums_ref[0:6, :] = jnp.zeros((6, width), f32)
 
 
-def forward_half(places, attended, content, stream, output_own, inner_own, got, rest, vectors, bias):
-    rows, width = attended.shape
-    hidden = inner_own.shape[1]
+def forward_half(places, *operands):
+    rows, width = operands[0].shape
+    hidden = operands[4].shape[1]
     shapes = [
         jax.ShapeDtypeStruct((rows, width), bf16),
         jax.ShapeDtypeStruct((rows, width), f32),
@@ -961,12 +1016,13 @@
     ]
     return pl.pallas_call(
         forward_half_kernel,
-        in_specs=[in_smem] + [in_vmem] * 9,
-        out_specs=[in_vmem] * len(shapes),
+        grid=(1,),
+        in_specs=[in_smem] + [resident(value) for value in operands],
+        out_specs=[resident(shape) for shape in shapes],
         out_shape=shapes,
-        compiler_params=pltpu.CompilerParams(vmem_limit_bytes=48 << 20),
+        compiler_params=pltpu.CompilerParams(vmem_limit_bytes=60 << 20),
         cost_estimate=takes(8),
-    )(places, attended, content, stream, output_own, inner_own, got, rest, vectors, bias)
+    )(places, *operands)
 
 
 def backward_half(places, *operands):
@@ -984,8 +1040,9 @@
     )
     return pl.pallas_call(
         backward_half_kernel,
-        in_specs=[in_smem] + [in_vmem] * len(operands),
-        out_specs=[in_vmem] * len(shapes),
+        grid=(1,),
+        in_specs=[in_smem] + [resident(value) for value in operands],
+        out_specs=[resident(shape) for shape in shapes],
         out_shape=shapes,
         scratch_shapes=[
             pltpu.VMEM((hidden, width), bf16),
@@ -993,7 +1050,7 @@
             pltpu.VMEM((rows, width), bf16),
             pltpu.VMEM((8, hidden), f32),
         ],
-        compiler_params=pltpu.CompilerParams(vmem_limit_bytes=56 << 20),
+        compiler_params=pltpu.CompilerParams(vmem_limit_bytes=60 << 20),
         cost_estimate=takes(12),
     )(places, *operands)
 
@@ -1040,7 +1097,34 @@
     low = 2
 
     first_places = shard_places(query_weight.shape[0])
-    first_sent = half_rows(first_places, query_weight, key_weight, value_weight)
+    hidden = inner_weight.shape[1]
+    near = (lax.axis_index("ctx") // low) % 2
+    shard_rows = query_weight.shape[0]
+    half, quarter = shard_rows // 2, shard_rows // 4
+    base, span = 3 * width, (width + hidden) // 2
+    (first_sent,) = moved(
+        tuple(
+            (at, window("0", half, 0, width), 0, window(0, half, at * width, width))
+            for at in range(3)
+        )
+        + (
+            (3, window("1", quarter, 0, width), 0, window(0, quarter, base, width)),
+            (
+                4,
+                window("1", quarter, 0, span - width),
+                0,
+                window(0, quarter, base + width, span - width),
+            ),
+            (4, window("1", quarter, span - width, span), 0, window(quarter, quarter, base, span)),
+        ),
+        [jax.ShapeDtypeStruct((half, base + span), bf16)],
+        jnp.stack([core * half, (2 * core + near) * quarter]).astype(jnp.int32),
+        query_weight,
+        key_weight,
+        value_weight,
+        output_weight,
+        inner_weight,
+    )
     first_got = across(first_sent)
     mark_rows = 16
     marks = jnp.concatenate(
@@ -1054,28 +1138,29 @@
     marks = jnp.pad(marks[None], ((0, mark_rows - 1), (0, width - marks.shape[0])))
     block = jnp.concatenate([own_content, marks], axis=0)
     gathered = gather_blocks(block)
-    small = jnp.concatenate(
-        [
-            content_bias,
-            segment_bias,
-            attention_gain,
-            attention_shift,
-            outer_bias,
-            final_gain,
-            final_shift,
-            segment_embed.reshape(-1),
-            inner_bias,
-            relative_table.reshape(-1),
-        ]
-    )
     small_height = 16
-    small = jnp.pad(small, (0, small_height * part - small.shape[0])).reshape(small_height, part)
+    small = jnp.zeros((small_height * part,), bf16)
+    filled = 0
+    for vector in (
+        content_bias,
+        segment_bias,
+        attention_gain,
+        attention_shift,
+        outer_bias,
+        final_gain,
+        final_shift,
+        segment_embed.reshape(-1),
+        inner_bias,
+        relative_table.reshape(-1),
+    ):
+        small = small + jnp.pad(vector, (filled, small.shape[0] - filled - vector.shape[0]))
+        filled += vector.shape[0]
+    small = small.reshape(small_height, part)
     small_other = across(small)
     first_rest = partner(first_got, 1)
-    second_sent = half_rows(first_places, output_weight, inner_weight)
-    second_got = across(second_sent)
+    second_near = partner(first_got[:, base:], low)
     third_places = shard_places(outer_weight.shape[0])
-    third_sent = half_rows(third_places, outer_weight)
+    third_sent = half_rows(third_places, 1, outer_weight)
     third_got = across(third_sent)
 
     small_pair = jnp.where(
@@ -1145,11 +1230,17 @@
     )
 
     hidden = inner_weight.shape[1]
-    second_got, third_got, attended = lax.optimization_barrier((second_got, third_got, attended))
-    second_rest = partner(second_got, 1)
+    second_near, third_got, attended = lax.optimization_barrier(
+        (second_near, third_got, attended)
+    )
+    second_far = partner(second_near, 1)
     third_rest = partner(third_got, 1)
     half_places = jnp.concatenate(
-        [first_places, core[None].astype(jnp.int32), third_places[1:]]
+        [
+            quarter_places(query_weight.shape[0]),
+            core[None].astype(jnp.int32),
+            third_places[1:],
+        ]
     )
     (
         out_low,
@@ -1169,8 +1260,10 @@
         own_query,
         output_weight,
         inner_weight,
-        second_got,
-        second_rest,
+        first_got,
+        second_near,
+        first_rest,
+        second_far,
         small_pair,
         bias_inner[None],
     )
@@ -1213,9 +1306,17 @@
     order_two = cuts[:1] + [0] + cuts[1:]
     places_one = piece_places(order_one, cuts)
     places_two = piece_places(order_two, cuts)
-    wide_places = piece_places([1, 0] + cuts, wide_cuts)
+    wide_places = by_core(
+        piece_places([1, 0] + cuts, wide_cuts),
+        piece_places([1, cuts[0], 0] + cuts[1:], wide_cuts),
+        2 << len(cuts),
+    )
     places_out = jnp.concatenate([piece_places(cuts, cuts), core[None].astype(jnp.int32)])
-    wide_places_out = piece_places(wide_cuts, wide_cuts)
+    wide_places_out = by_core(
+        piece_places(wide_cuts, wide_cuts),
+        piece_places([1] + cuts[1:] + cuts[:1], wide_cuts),
+        1 << len(cuts),
+    )
 
     outer_keep, outer_send = product_pieces(
         places_one, active_low, active_other, outer_kept, partner(outer_sent, 1)
@@ -1256,7 +1357,8 @@
         attended,
         log_row,
     )
-    order = Sequence(small_back)
+    hidden_rows = hidden // part // sides
+    order = Sequence(after(wide_places_out, small_back))
     outer_got, inner_got = order.wait(outer_got, inner_got)
     outer_keep, outer_send = fold(outer_keep, outer_got)
     outer_send = order.ready(outer_send)
@@ -1264,8 +1366,7 @@
     inner_keep, inner_send = fold(inner_keep, inner_got)
     inner_send = order.ready(inner_send)
     inner_got = across(inner_send)
-
-    hidden_rows = hidden // part // sides
+    content_share = order.ready(share_of_content(order.ready(both_back), weight_both))
     tail_keep, tail_send = cut_gradient(
         wide_places,
         vectors,
@@ -1273,23 +1374,23 @@
         dot_tn(streams, query_back),
         dot_tn(content_all, order.ready(both_back)),
     )
+    tail_keep = order.ready(tail_keep)
+    outer_got = order.wait(outer_got)
+    inner_got = order.wait(inner_got)
     tail_send = order.ready(tail_send)
     tail_got = partner(tail_send, 1)
-    outer_got = order.wait(outer_got)
     outer_keep, outer_send = fold(outer_keep, outer_got)
     outer_send = order.ready(outer_send)
     outer_got = partner(outer_send, line[0])
-    content_share = share_of_content(order.ready(both_back), weight_both)
+    inner_keep, inner_send = fold(inner_keep, inner_got)
+    inner_send = order.ready(inner_send)
+    inner_got = partner(inner_send, line[0])
     share_keep, share_send = content_share[: count // 2], order.ready(content_share[count // 2 :])
     share_got = partner(share_send, 1)
     tail_got = order.wait(tail_got)
     tail_keep, tail_send = fold(tail_keep, tail_got)
     tail_send = order.ready(tail_send)
-    tail_got = across(tail_send)
-    inner_got = order.wait(inner_got)
-    inner_keep, inner_send = fold(inner_keep, inner_got)
-    inner_send = order.ready(inner_send)
-    inner_got = partner(inner_send, line[0])
+    tail_got = pass_mixed(tail_send, 0, cuts[0])
     share_got = order.wait(share_got)
     share_keep, share_send = fold(share_keep, share_got)
     share_send = order.ready(share_send)
@@ -1302,30 +1403,34 @@
     inner_keep, inner_send = fold(inner_keep, inner_got)
     inner_send = order.ready(inner_send)
     inner_got = partner(inner_send, last)
+    tail_got = order.wait(tail_got)
+    tail_keep, tail_send = fold(tail_keep, tail_got)
+    tail_send = order.ready(tail_send)
+    tail_got = pass_mixed(tail_send, cuts[0], 0)
     outer_got = order.wait(outer_got)
     outer_value = order.ready(add_extra(fold_last(outer_keep, outer_got)))
     outer_got = partner(outer_value, last)
+    inner_got = order.wait(inner_got)
+    inner_value = order.ready(add_extra(fold_last(inner_keep, inner_got)))
+    inner_got = partner(inner_value, last)
     tail_got = order.wait(tail_got)
     tail_keep, tail_send = fold(tail_keep, tail_got)
     tail_send = order.ready(tail_send)
-    tail_got = partner(tail_send, cuts[0])
-    inner_got = order.wait(inner_got)
-    inner_value = order.ready(add_extra(fold_last(inner_keep, inner_got)))
-    inner_got = partner(inner_value, last)
-    outer_got = order.wait(outer_got)
-    outer_value = order.ready(piled(outer_value, outer_got))
-    outer_got = partner(outer_value, line[0])
+    tail_got = partner(tail_send, line[0])
     share_got = order.wait(share_got)
     share_keep, share_send = fold(share_keep, share_got)
     share_send = order.ready(share_send)
     share_got = partner(share_send, line[0])
+    outer_got = order.wait(outer_got)
+    outer_value = order.ready(piled(outer_value, outer_got))
+    outer_got = partner(outer_value, line[0])
     inner_got = order.wait(inner_got)
     inner_value = order.ready(piled(inner_value, inner_got))
     inner_got = partner(inner_value, line[0])
     tail_got = order.wait(tail_got)
     tail_keep, tail_send = fold(tail_keep, tail_got)
     tail_send = order.ready(tail_send)
-    tail_got = partner(tail_send, line[0])
+    tail_got = partner(tail_send, last)
     outer_got = order.wait(outer_got)
     outer_value = order.ready(piled(outer_value, outer_got))
     outer_got = partner(outer_value, cuts[0])
@@ -1335,15 +1440,14 @@
     share_got = partner(share_send, last)
     streams_back = residual_back + dot_nt(order.ready(query_back), weight_query)
     tail_got = order.wait(tail_got)
-    tail_keep, tail_send = fold(tail_keep, tail_got)
-    tail_send = order.ready(tail_send)
-    tail_got = partner(tail_send, last)
+    tail_value = order.ready(add_extra(fold_last(tail_keep, tail_got)))
+    tail_got = pass_mixed(tail_value, last, cuts[0])
     inner_got = order.wait(inner_got)
     inner_value = order.ready(piled(inner_value, inner_got))
     inner_got = partner(inner_value, cuts[0])
     tail_got = order.wait(tail_got)
-    tail_value = order.ready(add_extra(fold_last(tail_keep, tail_got)))
-    tail_got = partner(tail_value, last)
+    tail_value = order.ready(piled(tail_value, tail_got))
+    tail_got = pass_mixed(tail_value, line[0], last)
     outer_got = order.wait(outer_got)
     outer_value = order.ready(piled(outer_value, outer_got))
     outer_got = partner(outer_value, 1)
@@ -1352,7 +1456,14 @@
         share_keep, share_send = fold(share_keep, share_got)
         share_got = partner(share_send, bit)
     content_back = streams_back[:block_rows] + share_keep[0].astype(f32) + share_got[0].astype(f32)
-    content_back, outer_got = order.wait(content_back, outer_got)
+    content_back = order.ready(content_back)
+    tail_got = order.wait(tail_got)
+    tail_value = order.ready(piled(tail_value, tail_got))
+    tail_got = pass_mixed(tail_value, cuts[0], line[0])
+    inner_got = order.wait(inner_got)
+    inner_value = order.ready(piled(inner_value, inner_got))
+    inner_got = partner(inner_value, 1)
+    outer_got = order.wait(outer_got)
     (outer_weight_sum,) = lay_out(
         places_out,
         (((0, 0, width // 2, -1), (1, 0, width // 2, -2)),),
@@ -1362,13 +1473,7 @@
     outer_weight_sum = order.ready(outer_weight_sum)
     tail_got = order.wait(tail_got)
     tail_value = order.ready(piled(tail_value, tail_got))
-    tail_got = partner(tail_value, line[0])
-    inner_got = order.wait(inner_got)
-    inner_value = order.ready(piled(inner_value, inner_got))
-    inner_got = partner(inner_value, 1)
-    tail_got = order.wait(tail_got)
-    tail_value = order.ready(piled(tail_value, tail_got))
-    tail_got = partner(tail_value, cuts[0])
+    tail_got = partner(tail_value, 1)
     inner_got = order.wait(inner_got)
     inner_weight_sum, output_weight_sum = lay_out(
         places_out,
@@ -1381,8 +1486,6 @@
     )
     inner_weight_sum, output_weight_sum = order.ready(inner_weight_sum, output_weight_sum)
     tail_got = order.wait(tail_got)
-    tail_value = order.ready(piled(tail_value, tail_got))
-    tail_got = partner(tail_value, 1)
     plan = []
     for kind in range(3):
         row = []
@@ -1392,7 +1495,7 @@
         plan.append(tuple(row))
     plan.append(((0, 3 * width, lanes, 0),))
     query_weight_sum, key_weight_sum, value_weight_sum, vector_sums = lay_out(
-        wide_places_out, tuple(plan), tail_value, tail_got
+        order.mark, tuple(plan), tail_value, tail_got
     )
     sums = vector_sums[:, :16].T
     table_sum = jnp.swapaxes(sums[4:6].reshape(2, -1, lanes)[:, :, :bucket_count], 0, 1).reshape(

time: 368 us -> 343 us (0.932)
  waiting for transfers between devices: 116 us -> 106 us
  local copies, waits for them, and re-layouts: 35 us -> 27.2 us
  starting transfers between devices: 63.3 us -> 56.5 us
    ppermute x7 -> x5, waiting for transfers between devices: 38.2 us -> 4.12 us  [across(): return lax.ppermute(value, 'wsh', [(0, 1), (1, 0)])]
    ppermute x44 -> x40, waiting for transfers between devices: 77.7 us -> 92.1 us  [partner(): lax.ppermute(value, 'ctx', [(place, place ^ bit) for place in range(count)])]
    ppermute x0 -> x5, waiting for transfers between devices: none -> 10.1 us  [pass_mixed(): return lax.ppermute(value, ('ctx', 'wsh'), pairs)]
    unnamed x124 -> x109, local copies, waits for them, and re-layouts: 29.1 us -> 19.9 us
    ppermute x44 -> x40, starting transfers between devices: 56.7 us -> 48.4 us  [partner(): lax.ppermute(value, 'ctx', [(place, place ^ bit) for place in range(count)])]
    pallas_call x30 -> x29, Pallas kernels: 66.7 us -> 67.2 us  [the longest x1 15.2 us: backward_half(): pl.pallas_call(backward_half_kernel, grid=(1,), in_specs=[in_smem] + [res...]
  transfers between devices with their start and end apart: 51 -> 50, of which waited for: 23 -> 23; matrix products, arithmetic and copies ran while one was open for 8% -> 9% of each run, Pallas kernels for 32% -> 32%
where the time goes in v1:
time: 343 us
  Pallas kernels  127 us (37%)
  waiting for transfers between devices  106 us (31%)
  starting transfers between devices  56.5 us (16%)
  local copies, waits for them, and re-layouts  27.2 us (8%)
  matrix products  17.7 us (5%)
  other arithmetic  5.78 us (2%)
    ppermute x40, waiting for transfers between devices, partner(): lax.ppermute(value, 'ctx', [(place, place ^ bit) for place in range(count)])  92.1 us
    ppermute x40, starting transfers between devices, partner(): lax.ppermute(value, 'ctx', [(place, place ^ bit) for place in range(count)])  48.4 us
    pallas_call x1, Pallas kernels, attention_backward(): pl.pallas_call(backward_kernel, grid=(pairs,), in_specs=[spec['stack'], s...  34.4 us
    unnamed x109, local copies, waits for them, and re-layouts  19.9 us
    pallas_call x1, Pallas kernels, attention_forward(): pl.pallas_call(forward_kernel, grid=(pairs,), in_specs=[spec['rows'], spe...  17.8 us
    pallas_call x1, Pallas kernels, backward_half(): pl.pallas_call(backward_half_kernel, grid=(1,), in_specs=[in_smem] + [res...  15.2 us
    pallas_call x1, Pallas kernels, forward_half(): pl.pallas_call(forward_half_kernel, grid=(1,), in_specs=[in_smem] + [resi...  12.4 us
    pallas_call x3, Pallas kernels, lay_out(): pl.pallas_call(functools.partial(lay_out_kernel, plan), grid=(1,), in_spe...  11.6 us
  transfers between devices with their start and end apart: 50, of which 23 were waited for; matrix products, arithmetic and copies ran while one was open for 9% of the time, Pallas kernels for 32%

profile of v1, /device:TPU:1, one launch (start us, length us, event | category | flops | bytes accessed | tf_op | source)
XLA Modules:
  0.0 342.5 jit_solution(11059673621209462111)
XLA Ops:
  18.4 7.1 %collective-permute-done.5.refs_1_ = bf16[144,768]{1,0:T(8,128)(2,1)S(1)} collective-permute-done((bf16[144,768]{1,0:T(8,128)(2,1)S(1)}, bf16[144,768]{1,0:T(8,128)(2,1)S(1)}, u32[]{:S(2)}, u32[]{:S(2)}) %collective-permute-start.5) | collective-permute-done | bytes 221216 | tf_op jit(solution)/shard_map/ppermute | solution.py:63
  27.0 4.1 %collective-permute-done.7.refs_3_ = bf16[144,768]{1,0:T(8,128)(2,1)S(1)} collective-permute-done((bf16[144,768]{1,0:T(8,128)(2,1)S(1)}, bf16[144,768]{1,0:T(8,128)(2,1)S(1)}, u32[]{:S(2)}, u32[]{:S(2)}) %collective-permute-start.7) | collective-permute-done | bytes 221216 | tf_op jit(solution)/shard_map/ppermute | solution.py:63
  37.2 7.1 %collective-permute-start.12 = (bf16[1152,768]{1,0:T(8,128)(2,1)}, bf16[1152,768]{1,0:T(8,128)(2,1)}, u32[]{:S(2)}, u32[]{:S(2)}) collective-permute-start(bf16[1152,768]{1,0:T(8,128)(2,1)} %constant_dynamic-update-slice_fusion), channel_id=1, source_target_pairs={{0,2},{2,0},{4,6},{6,4},{8,10},{10,8},{12,14},{14,12},{16,18},{18,... | collective-permute-start | bytes 5308424 | tf_op jit(solution)/shard_map/ppermute | solution.py:63
  62.3 6.8 %convolution_convert_fusion.both_ref = bf16[2048,1536]{1,0:T(8,128)(2,1)} fusion(bf16[2048,768]{1,0:T(8,128)(2,1)S(1)} %get-tuple-element.231, bf16[768,1536]{1,0:T(8,128)(2,1)S(1)} %get-tuple-element.232.weight_ref), kind=kOutput, calls=%fused_computation | convolution fusion | flops 4834983936 | bytes 11796480 | tf_op jit(solution)/shard_map/dot_general | solution.py:50
  69.2 17.8 %shard_map.387 = (f32[256,768]{1,0:T(8,128)}, f32[6,1,512]{2,1,0:T(1,128)}, bf16[6,512,256]{2,1,0:T(8,128)(2,1)}) custom-call(f32[256,768]{1,0:T(8,128)} %fusion.2.query_ref, f32[1,768]{1,0:T(1,128)} %get-tuple-element.493.content_bias_ref, f32[1,768]{1,0:T(1,128)} %get-tuple-element.492.segment_bias_ref, f32[2,768]{1,0:T(2,128)} %slice.147.embed_ref, ...), custom_call_target="tpu_custom_call" | custom-call | tf_op jit(solution)/shard_map/pallas_call | solution.py:698
  90.8 12.4 %shard_map.388 = (bf16[256,768]{1,0:T(8,128)(2,1)}, f32[256,768]{1,0:T(8,128)}, f32[256,768]{1,0:T(8,128)}, f32[256,128]{1,0:T(8,128)}, bf16[256,768]{1,0:T(8,12...) custom-call(s32[10]{0:T(128)} %concatenate.50.place_ref, ...), custom_call_target="tpu_custom_call" | custom-call | flops 8000000000 | tf_op jit(solution)/shard_map/pallas_call | solution.py:1017
  103.6 15.2 %shard_map.389 = (bf16[128,768]{1,0:T(8,128)(2,1)}, bf16[128,768]{1,0:T(8,128)(2,1)}, f32[256,768]{1,0:T(8,128)}, bf16[256,768]{1,0:T(8,128)(2,1)}, bf16[256,384...) custom-call(s32[10]{0:T(128)} %concatenate.50.place_ref, ...), custom_call_target="tpu_custom_call" | custom-call | flops 12000000000 | tf_op jit(solution)/shard_map/pallas_call | solution.py:1041
  124.1 5.8 %shard_map.391 = (bf16[8,48,1920]{2,1,0:T(8,128)(2,1)}, bf16[8,48,1920]{2,1,0:T(8,128)(2,1)}) custom-call(s32[16]{0:T(128)} %add_add_fusion.3.place_ref, bf16[256,768]{1,0:T(8,128)(2,1)} %get-tuple-element.255.refs_0_, bf16[256,768]{1,0:T(8,128)(2,1)} %copy-done.45, bf16[256,1536]{1,0:T(8,128)(2,1)} %get-tuple-element.256.refs_2_, ...), custom_call_target="tpu_custom_call" | custom-call | flops 4000000000 | tf_op jit(solution)/shard_map/pallas_call | solution.py:359
  131.1 5.5 %shard_map.390 = (bf16[8,192,384]{2,1,0:T(8,128)(2,1)}, bf16[8,192,384]{2,1,0:T(8,128)(2,1)}) custom-call(s32[16]{0:T(128)} %add_add_fusion.4.place_ref, bf16[256,3072]{1,0:T(8,128)(2,1)} %get-tuple-element.237.active_ref.refs_0_, bf16[256,3072]{1,0:T(8,128)(2,1)} %copy-done.42, bf16[256,384]{1,0:T(8,128)(2,1)} %get-tuple-element.252.refs_2_, ...), custom_call_target="tpu_custom_call" | custom-call | flops 4000000000 | tf_op jit(solution)/shard_map/pallas_call | solution.py:359
  138.0 34.4 %shard_map.392 = (bf16[256,768]{1,0:T(8,128)(2,1)}, bf16[2048,1536]{1,0:T(8,128)(2,1)}, f32[8,768]{1,0:T(8,128)}) custom-call(bf16[6,512,256]{2,1,0:T(8,128)(2,1)} %get-tuple-element.249.stack_ref, f32[256,768]{1,0:T(8,128)} %fusion.2.query_ref, f32[1,768]{1,0:T(1,128)} %get-tuple-element.492.segment_bias_ref, f32[2,768]{1,0:T(2,128)} %slice.147.embed_ref, ...), custom_call_target="tpu_custom_call" | custom-call | flops 33999998976 | tf_op jit(solution)/shard_map/pallas_call | solution.py:731
  180.9 6.9 %shard_map.395 = bf16[16,128,768]{2,1,0:T(8,128)(2,1)S(1)} custom-call(bf16[2048,1536]{1,0:T(8,128)(2,1)S(1)} %copy-done, bf16[768,1536]{1,0:T(8,128)(2,1)S(1)} %copy-done.11), custom_call_target="tpu_custom_call" | custom-call | tf_op jit(solution)/shard_map/pallas_call | solution.py:313
  189.4 7.1 %fusion.24.refs_1_ = f32[768,1536]{1,0:T(8,128)S(1)} fusion(bf16[2048,768]{1,0:T(8,128)(2,1)} %copy-done.22, bf16[2048,1536]{1,0:T(8,128)(2,1)S(1)} %copy-done), kind=kOutput, calls=%fused_computation.88 | convolution fusion | flops 4831838208 | bytes 14155776 | tf_op jit(solution)/shard_map/dot_general | solution.py:58
  202.3 3.8 %collective-permute-done.23.received_ref = bf16[4,48,1920]{2,1,0:T(8,128)(2,1)S(1)} collective-permute-done((bf16[4,48,1920]{2,1,0:T(8,128)(2,1)S(1)}, bf16[4,48,1920]{2,1,0:T(8,128)(2,1)S(1)}, u32[]{:S(2)}, u32[]{:S(2)}) %collective-permute-start.23) | collective-permute-done | bytes 737312 | tf_op jit(solution)/shard_map/ppermute | solution.py:67
  215.8 12.6 %collective-permute-done.30.received_ref = bf16[2,192,384]{2,1,0:T(8,128)(2,1)S(1)} collective-permute-done((bf16[2,192,384]{2,1,0:T(8,128)(2,1)S(1)}, bf16[2,192,384]{2,1,0:T(8,128)(2,1)S(1)}, u32[]{:S(2)}, u32[]{:S(2)}) %collective-permute-start.30) | collective-permute-done | bytes 294944 | tf_op jit(solution)/shard_map/ppermute | solution.py:63
  234.3 11.2 %collective-permute-done.33.received_ref = bf16[1,192,384]{2,1,0:T(8,128)(2,1)S(1)} collective-permute-done((bf16[1,192,384]{2,1,0:T(8,128)(2,1)S(1)}, bf16[1,192,384]{2,1,0:T(8,128)(2,1)S(1)}, u32[]{:S(2)}, u32[]{:S(2)}) %collective-permute-start.33) | collective-permute-done | bytes 147488 | tf_op jit(solution)/shard_map/ppermute | solution.py:63
  245.6 3.8 %collective-permute-done.32.received_ref = bf16[1,48,1920]{2,1,0:T(8,128)(2,1)S(1)} collective-permute-done((bf16[1,48,1920]{2,1,0:T(8,128)(2,1)S(1)}, bf16[1,48,1920]{2,1,0:T(8,128)(2,1)S(1)}, u32[]{:S(2)}, u32[]{:S(2)}) %collective-permute-start.32) | collective-permute-done | bytes 184352 | tf_op jit(solution)/shard_map/ppermute | solution.py:63
  249.8 5.6 %collective-permute-done.35.refs_1_ = bf16[1,192,384]{2,1,0:T(8,128)(2,1)S(1)} collective-permute-done((bf16[1,192,384]{2,1,0:T(8,128)(2,1)S(1)}, bf16[1,192,384]{2,1,0:T(8,128)(2,1)S(1)}, u32[]{:S(2)}, u32[]{:S(2)}) %collective-permute-start.35) | collective-permute-done | bytes 147488 | tf_op jit(solution)/shard_map/ppermute | solution.py:63
  259.5 11.9 %collective-permute-done.38.refs_1_ = bf16[1,48,1920]{2,1,0:T(8,128)(2,1)S(1)} collective-permute-done((bf16[1,48,1920]{2,1,0:T(8,128)(2,1)S(1)}, bf16[1,48,1920]{2,1,0:T(8,128)(2,1)S(1)}, u32[]{:S(2)}, u32[]{:S(2)}) %collective-permute-start.38) | collective-permute-done | bytes 184352 | tf_op jit(solution)/shard_map/ppermute | solution.py:63
  277.1 9.6 %collective-permute-done.34.received_ref = bf16[2,128,768]{2,1,0:T(8,128)(2,1)S(1)} collective-permute-done((bf16[2,128,768]{2,1,0:T(8,128)(2,1)S(1)}, bf16[2,128,768]{2,1,0:T(8,128)(2,1)S(1)}, u32[]{:S(2)}, u32[]{:S(2)}) %collective-permute-start.34) | collective-permute-done | bytes 393248 | tf_op jit(solution)/shard_map/ppermute | solution.py:63
  286.8 6.8 %collective-permute-done.41.received_ref = bf16[1,24,2432]{2,1,0:T(8,128)(2,1)S(1)} collective-permute-done((bf16[1,24,2432]{2,1,0:T(8,128)(2,1)S(1)}, bf16[1,24,2432]{2,1,0:T(8,128)(2,1)S(1)}, u32[]{:S(2)}, u32[]{:S(2)}) %collective-permute-start.41) | collective-permute-done | bytes 116768 | tf_op jit(solution)/shard_map/ppermute | solution.py:63
  297.5 5.9 %collective-permute-start.46 = (bf16[8,192,384]{2,1,0:T(8,128)(2,1)S(1)}, bf16[8,192,384]{2,1,0:T(8,128)(2,1)S(1)}, u32[]{:S(2)}, u32[]{:S(2)}) collective-permute-start(bf16[8,192,384]{2,1,0:T(8,128)(2,1)S(1)} %shard_map.416.refs_0_), channel_id=1, source_target_pairs={{0,2},{2,0},{4,6},{6,4},{8,10},{10,8},{12,14},{14,12},{16,18},{18,... | collective-permute-start | bytes 3538952 | tf_op jit(solution)/shard_map/ppermute | solution.py:63
  306.4 11.5 %collective-permute-done.39 = bf16[1,128,768]{2,1,0:T(8,128)(2,1)S(1)} collective-permute-done((bf16[1,128,768]{2,1,0:T(8,128)(2,1)S(1)}, bf16[1,128,768]{2,1,0:T(8,128)(2,1)S(1)}, u32[]{:S(2)}, u32[]{:S(2)}) %collective-permute-start.39) | collective-permute-done | bytes 196640 | tf_op jit(solution)/shard_map/ppermute | solution.py:63
  323.8 4.4 %collective-permute-done.45.refs_1_ = bf16[4,24,2432]{2,1,0:T(8,128)(2,1)S(1)} collective-permute-done((bf16[4,24,2432]{2,1,0:T(8,128)(2,1)S(1)}, bf16[4,24,2432]{2,1,0:T(8,128)(2,1)S(1)}, u32[]{:S(2)}, u32[]{:S(2)}) %collective-permute-start.45) | collective-permute-done | bytes 466976 | tf_op jit(solution)/shard_map/ppermute | solution.py:213
  333.4 4.6 %shard_map.422 = (f32[384,768]{1,0:T(8,128)}, f32[384,768]{1,0:T(8,128)}, f32[384,768]{1,0:T(8,128)}, f32[384,128]{1,0:T(8,128)S(1)}) custom-call(s32[16]{0:T(128)S(1)} %broadcast_select_fusion.1.place_ref, bf16[8,24,2432]{2,1,0:T(8,128)(2,1)S(1)} %shard_map.420.refs_0_, bf16[8,24,2432]{2,1,0:T(8,128)(2,1)S(1)} %collective-permute-done.48.refs_1_), custom_call_target="tpu_custom_call" | custom-call | flops 3000000000 | tf_op jit(solution)/shard_map/pallas_call | solution.py:445
  (281 shorter events, 118.3 us)
Async XLA Ops:
  7.4 37.3 %collective-permute-start = (bf16[192,4224]{1,0:T(8,128)(2,1)S(1)}, bf16[192,4224]{1,0:T(8,128)(2,1)S(1)}, u32[]{:S(2)}, u32[]{:S(2)}) collective-permute-start(bf16[192,4224]{1,0:T(8,128)(2,1)S(1)} %shard_map.382), channel_id=1, source_target_pairs={{0,1},{1,0},{2,3},{3,2},{4,5},{5,4},{6,7},{7,6},{8,9},{9,8},{10,11... | collective-permute-start | bytes 4866056 | tf_op jit(solution)/shard_map/ppermute | solution.py:67
  17.2 17.2 %collective-permute-start.8 = (bf16[144,768]{1,0:T(8,128)(2,1)S(1)}, bf16[144,768]{1,0:T(8,128)(2,1)S(1)}, u32[]{:S(2)}, u32[]{:S(2)}) collective-permute-start(bf16[144,768]{1,0:T(8,128)(2,1)S(1)} %pad_maximum_fusion.3.refs_0_), channel_id=1, source_target_pairs={{0,4},{2,6},{4,0},{6,2},{8,12},{10,14},{12,8},{14,10},{16,20},{18,... | collective-permute-start | bytes 663560 | tf_op jit(solution)/shard_map/ppermute | solution.py:63
  37.2 17.7 %collective-permute-start.12 = (bf16[1152,768]{1,0:T(8,128)(2,1)}, bf16[1152,768]{1,0:T(8,128)(2,1)}, u32[]{:S(2)}, u32[]{:S(2)}) collective-permute-start(bf16[1152,768]{1,0:T(8,128)(2,1)} %constant_dynamic-update-slice_fusion), channel_id=1, source_target_pairs={{0,2},{2,0},{4,6},{6,4},{8,10},{10,8},{12,14},{14,12},{16,18},{18,... | collective-permute-start | bytes 5308424 | tf_op jit(solution)/shard_map/ppermute | solution.py:63
  51.0 36.0 %collective-permute-start.2 = (bf16[768,768]{1,0:T(8,128)(2,1)}, bf16[768,768]{1,0:T(8,128)(2,1)}, u32[]{:S(2)}, u32[]{:S(2)}) collective-permute-start(bf16[768,768]{1,0:T(8,128)(2,1)} %shard_map.383), channel_id=1, source_target_pairs={{0,1},{1,0},{2,3},{3,2},{4,5},{5,4},{6,7},{7,6},{8,9},{9,8},{10,11... | collective-permute-start | bytes 3538952 | tf_op jit(solution)/shard_map/ppermute | solution.py:67
  53.5 33.5 %collective-permute-start.1 = (bf16[192,1920]{1,0:T(8,128)(2,1)}, bf16[192,1920]{1,0:T(8,128)(2,1)}, u32[]{:S(2)}, u32[]{:S(2)}) collective-permute-start(bf16[192,1920]{1,0:T(8,128)(2,1)} %slice.144), channel_id=1, source_target_pairs={{0,4},{2,6},{4,0},{6,2},{8,12},{10,14},{12,8},{14,10},{16,20},{18,... | collective-permute-start | bytes 2211848 | tf_op jit(solution)/shard_map/ppermute | solution.py:63
  88.6 14.9 %collective-permute-start.14 = (bf16[768,768]{1,0:T(8,128)(2,1)}, bf16[768,768]{1,0:T(8,128)(2,1)}, u32[]{:S(2)}, u32[]{:S(2)}) collective-permute-start(bf16[768,768]{1,0:T(8,128)(2,1)} %collective-permute-done.2.got_ref), channel_id=1, source_target_pairs={{0,2},{2,0},{4,6},{6,4},{8,10},{10,8},{12,14},{14,12},{16,18},{18,... | collective-permute-start | bytes 3538952 | tf_op jit(solution)/shard_map/ppermute | solution.py:63
  103.2 26.8 %collective-permute-start.15 = (bf16[256,3072]{1,0:T(8,128)(2,1)}, bf16[256,3072]{1,0:T(8,128)(2,1)S(1)}, u32[]{:S(2)}, u32[]{:S(2)}) collective-permute-start(bf16[256,3072]{1,0:T(8,128)(2,1)} %get-tuple-element.237.active_ref.refs_0_), channel_id=1, source_target_pairs={{0,2},{2,0},{4,6},{6,4},{8,10},{10,8},{12,14},{14,12},{16,18},{18,... | collective-permute-start | bytes 4718600 | tf_op jit(solution)/shard_map/ppermute | solution.py:63
  129.9 44.3 %collective-permute-start.22 = (bf16[8,48,1920]{2,1,0:T(8,128)(2,1)}, bf16[8,48,1920]{2,1,0:T(8,128)(2,1)}, u32[]{:S(2)}, u32[]{:S(2)}) collective-permute-start(bf16[8,48,1920]{2,1,0:T(8,128)(2,1)} %get-tuple-element.261), channel_id=1, source_target_pairs={{0,4},{2,6},{4,0},{6,2},{8,12},{10,14},{12,8},{14,10},{16,20},{18,... | collective-permute-start | bytes 4423688 | tf_op jit(solution)/shard_map/ppermute | solution.py:63
  136.7 37.5 %collective-permute-start.21 = (bf16[8,192,384]{2,1,0:T(8,128)(2,1)}, bf16[8,192,384]{2,1,0:T(8,128)(2,1)}, u32[]{:S(2)}, u32[]{:S(2)}) collective-permute-start(bf16[8,192,384]{2,1,0:T(8,128)(2,1)} %get-tuple-element.254), channel_id=1, source_target_pairs={{0,1},{1,0},{2,3},{3,2},{4,5},{5,4},{6,7},{7,6},{8,9},{9,8},{10,11... | collective-permute-start | bytes 3538952 | tf_op jit(solution)/shard_map/ppermute | solution.py:67
  189.1 17.0 %collective-permute-start.23 = (bf16[4,48,1920]{2,1,0:T(8,128)(2,1)S(1)}, bf16[4,48,1920]{2,1,0:T(8,128)(2,1)S(1)}, u32[]{:S(2)}, u32[]{:S(2)}) collective-permute-start(bf16[4,48,1920]{2,1,0:T(8,128)(2,1)S(1)} %get-tuple-element.281), channel_id=1, source_target_pairs={{0,1},{1,0},{2,3},{3,2},{4,5},{5,4},{6,7},{7,6},{8,9},{9,8},{10,11... | collective-permute-start | bytes 2211848 | tf_op jit(solution)/shard_map/ppermute | solution.py:67
  212.2 19.3 %collective-permute-start.28 = (bf16[8,24,2432]{2,1,0:T(8,128)(2,1)S(1)}, bf16[8,24,2432]{2,1,0:T(8,128)(2,1)S(1)}, u32[]{:S(2)}, u32[]{:S(2)}) collective-permute-start(bf16[8,24,2432]{2,1,0:T(8,128)(2,1)S(1)} %get-tuple-element.314), channel_id=1, source_target_pairs={{0,1},{1,0},{2,6},{3,7},{4,5},{5,4},{6,2},{7,3},{8,9},{9,8},{10,14... | collective-permute-start | bytes 2801672 | tf_op jit(solution)/shard_map/ppermute | solution.py:213
  212.5 15.9 %collective-permute-start.29 = (bf16[2,48,1920]{2,1,0:T(8,128)(2,1)S(1)}, bf16[2,48,1920]{2,1,0:T(8,128)(2,1)S(1)}, u32[]{:S(2)}, u32[]{:S(2)}) collective-permute-start(bf16[2,48,1920]{2,1,0:T(8,128)(2,1)S(1)} %get-tuple-element.316), channel_id=1, source_target_pairs={{0,8},{2,10},{4,12},{6,14},{8,0},{10,2},{12,4},{14,6},{16,24},{18,... | collective-permute-start | bytes 1105928 | tf_op jit(solution)/shard_map/ppermute | solution.py:63
  214.2 35.4 %collective-permute-start.27 = (bf16[4,128,768]{2,1,0:T(8,128)(2,1)S(1)}, bf16[4,128,768]{2,1,0:T(8,128)(2,1)S(1)}, u32[]{:S(2)}, u32[]{:S(2)}) collective-permute-start(bf16[4,128,768]{2,1,0:T(8,128)(2,1)S(1)} %get-tuple-element.312), channel_id=1, source_target_pairs={{0,4},{2,6},{4,0},{6,2},{8,12},{10,14},{12,8},{14,10},{16,20},{18,... | collective-permute-start | bytes 2359304 | tf_op jit(solution)/shard_map/ppermute | solution.py:63
  231.8 17.7 %collective-permute-start.31 = (bf16[4,24,2432]{2,1,0:T(8,128)(2,1)S(1)}, bf16[4,24,2432]{2,1,0:T(8,128)(2,1)S(1)}, u32[]{:S(2)}, u32[]{:S(2)}) collective-permute-start(bf16[4,24,2432]{2,1,0:T(8,128)(2,1)S(1)} %get-tuple-element.332), channel_id=1, source_target_pairs={{0,4},{1,5},{2,3},{3,2},{4,0},{5,1},{6,7},{7,6},{8,12},{9,13},{10,... | collective-permute-start | bytes 1400840 | tf_op jit(solution)/shard_map/ppermute | solution.py:213
  234.1 15.3 %collective-permute-start.32 = (bf16[1,48,1920]{2,1,0:T(8,128)(2,1)S(1)}, bf16[1,48,1920]{2,1,0:T(8,128)(2,1)S(1)}, u32[]{:S(2)}, u32[]{:S(2)}) collective-permute-start(bf16[1,48,1920]{2,1,0:T(8,128)(2,1)S(1)} %get-tuple-element.334), channel_id=1, source_target_pairs={{0,16},{2,18},{4,20},{6,22},{8,24},{10,26},{12,28},{14,30},{16,0},... | collective-permute-start | bytes 552968 | tf_op jit(solution)/shard_map/ppermute | solution.py:63
  255.4 16.5 %collective-permute-start.36 = (bf16[2,192,384]{2,1,0:T(8,128)(2,1)S(1)}, bf16[2,192,384]{2,1,0:T(8,128)(2,1)S(1)}, u32[]{:S(2)}, u32[]{:S(2)}) collective-permute-start(bf16[2,192,384]{2,1,0:T(8,128)(2,1)S(1)} %shard_map.408.refs_0_), channel_id=1, source_target_pairs={{0,8},{2,10},{4,12},{6,14},{8,0},{10,2},{12,4},{14,6},{16,24},{18,... | collective-permute-start | bytes 884744 | tf_op jit(solution)/shard_map/ppermute | solution.py:63
  256.4 15.5 %collective-permute-start.37 = (bf16[2,24,2432]{2,1,0:T(8,128)(2,1)S(1)}, bf16[2,24,2432]{2,1,0:T(8,128)(2,1)S(1)}, u32[]{:S(2)}, u32[]{:S(2)}) collective-permute-start(bf16[2,24,2432]{2,1,0:T(8,128)(2,1)S(1)} %get-tuple-element.359), channel_id=1, source_target_pairs={{0,8},{2,10},{4,12},{6,14},{8,0},{10,2},{12,4},{14,6},{16,24},{18,... | collective-permute-start | bytes 700424 | tf_op jit(solution)/shard_map/ppermute | solution.py:63
  272.1 25.3 %collective-permute-start.40 = (bf16[4,192,384]{2,1,0:T(8,128)(2,1)S(1)}, bf16[4,192,384]{2,1,0:T(8,128)(2,1)S(1)}, u32[]{:S(2)}, u32[]{:S(2)}) collective-permute-start(bf16[4,192,384]{2,1,0:T(8,128)(2,1)S(1)} %shard_map.411.refs_0_), channel_id=1, source_target_pairs={{0,4},{2,6},{4,0},{6,2},{8,12},{10,14},{12,8},{14,10},{16,20},{18,... | collective-permute-start | bytes 1769480 | tf_op jit(solution)/shard_map/ppermute | solution.py:63
  276.0 18.9 %collective-permute-start.43 = (bf16[2,48,1920]{2,1,0:T(8,128)(2,1)S(1)}, bf16[2,48,1920]{2,1,0:T(8,128)(2,1)S(1)}, u32[]{:S(2)}, u32[]{:S(2)}) collective-permute-start(bf16[2,48,1920]{2,1,0:T(8,128)(2,1)S(1)} %shard_map.409.refs_0_), channel_id=1, source_target_pairs={{0,8},{2,10},{4,12},{6,14},{8,0},{10,2},{12,4},{14,6},{16,24},{18,... | collective-permute-start | bytes 1105928 | tf_op jit(solution)/shard_map/ppermute | solution.py:63
  276.0 17.6 %collective-permute-start.41 = (bf16[1,24,2432]{2,1,0:T(8,128)(2,1)S(1)}, bf16[1,24,2432]{2,1,0:T(8,128)(2,1)S(1)}, u32[]{:S(2)}, u32[]{:S(2)}) collective-permute-start(bf16[1,24,2432]{2,1,0:T(8,128)(2,1)S(1)} %get-tuple-element.381), channel_id=1, source_target_pairs={{0,16},{2,18},{4,20},{6,22},{8,24},{10,26},{12,28},{14,30},{16,0},... | collective-permute-start | bytes 350216 | tf_op jit(solution)/shard_map/ppermute | solution.py:63
  295.0 25.2 %collective-permute-start.47 = (bf16[4,48,1920]{2,1,0:T(8,128)(2,1)S(1)}, bf16[4,48,1920]{2,1,0:T(8,128)(2,1)S(1)}, u32[]{:S(2)}, u32[]{:S(2)}) collective-permute-start(bf16[4,48,1920]{2,1,0:T(8,128)(2,1)S(1)} %shard_map.414.refs_0_), channel_id=1, source_target_pairs={{0,4},{2,6},{4,0},{6,2},{8,12},{10,14},{12,8},{14,10},{16,20},{18,... | collective-permute-start | bytes 2211848 | tf_op jit(solution)/shard_map/ppermute | solution.py:63
  297.5 23.1 %collective-permute-start.46 = (bf16[8,192,384]{2,1,0:T(8,128)(2,1)S(1)}, bf16[8,192,384]{2,1,0:T(8,128)(2,1)S(1)}, u32[]{:S(2)}, u32[]{:S(2)}) collective-permute-start(bf16[8,192,384]{2,1,0:T(8,128)(2,1)S(1)} %shard_map.416.refs_0_), channel_id=1, source_target_pairs={{0,2},{2,0},{4,6},{6,4},{8,10},{10,8},{12,14},{14,12},{16,18},{18,... | collective-permute-start | bytes 3538952 | tf_op jit(solution)/shard_map/ppermute | solution.py:63
  303.5 14.4 %collective-permute-start.39 = (bf16[1,128,768]{2,1,0:T(8,128)(2,1)S(1)}, bf16[1,128,768]{2,1,0:T(8,128)(2,1)S(1)}, u32[]{:S(2)}, u32[]{:S(2)}) collective-permute-start(bf16[1,128,768]{2,1,0:T(8,128)(2,1)S(1)} %get-tuple-element.378), channel_id=1, source_target_pairs={{0,16},{2,18},{4,20},{6,22},{8,24},{10,26},{12,28},{14,30},{16,0},... | collective-permute-start | bytes 589832 | tf_op jit(solution)/shard_map/ppermute | solution.py:63
  305.4 14.8 %collective-permute-start.44 = (bf16[2,24,2432]{2,1,0:T(8,128)(2,1)S(1)}, bf16[2,24,2432]{2,1,0:T(8,128)(2,1)S(1)}, u32[]{:S(2)}, u32[]{:S(2)}) collective-permute-start(bf16[2,24,2432]{2,1,0:T(8,128)(2,1)S(1)} %shard_map.415.refs_0_), channel_id=1, source_target_pairs={{0,8},{1,9},{2,18},{3,19},{4,12},{5,13},{6,22},{7,23},{8,0},{9,1},... | collective-permute-start | bytes 700424 | tf_op jit(solution)/shard_map/ppermute | solution.py:213
  (76 other events, 839.9 us)

commit v2 on v1

--- a/solution.py
+++ b/solution.py
@@ -1366,7 +1366,6 @@
     inner_keep, inner_send = fold(inner_keep, inner_got)
     inner_send = order.ready(inner_send)
     inner_got = across(inner_send)
-    content_share = order.ready(share_of_content(order.ready(both_back), weight_both))
     tail_keep, tail_send = cut_gradient(
         wide_places,
         vectors,
@@ -1375,6 +1374,7 @@
         dot_tn(content_all, order.ready(both_back)),
     )
     tail_keep = order.ready(tail_keep)
+    content_share = order.ready(share_of_content(order.ready(both_back), weight_both))
     outer_got = order.wait(outer_got)
     inner_got = order.wait(inner_got)
     tail_send = order.ready(tail_send)
@@ -1407,6 +1407,10 @@
     tail_keep, tail_send = fold(tail_keep, tail_got)
     tail_send = order.ready(tail_send)
     tail_got = pass_mixed(tail_send, cuts[0], 0)
+    tail_got = order.wait(tail_got)
+    tail_keep, tail_send = fold(tail_keep, tail_got)
+    tail_send = order.ready(tail_send)
+    tail_got = partner(tail_send, line[0])
     outer_got = order.wait(outer_got)
     outer_value = order.ready(add_extra(fold_last(outer_keep, outer_got)))
     outer_got = partner(outer_value, last)
@@ -1416,7 +1420,7 @@
     tail_got = order.wait(tail_got)
     tail_keep, tail_send = fold(tail_keep, tail_got)
     tail_send = order.ready(tail_send)
-    tail_got = partner(tail_send, line[0])
+    tail_got = partner(tail_send, last)
     share_got = order.wait(share_got)
     share_keep, share_send = fold(share_keep, share_got)
     share_send = order.ready(share_send)
@@ -1428,9 +1432,8 @@
     inner_value = order.ready(piled(inner_value, inner_got))
     inner_got = partner(inner_value, line[0])
     tail_got = order.wait(tail_got)
-    tail_keep, tail_send = fold(tail_keep, tail_got)
-    tail_send = order.ready(tail_send)
-    tail_got = partner(tail_send, last)
+    tail_value = order.ready(add_extra(fold_last(tail_keep, tail_got)))
+    tail_got = pass_mixed(tail_value, last, cuts[0])
     outer_got = order.wait(outer_got)
     outer_value = order.ready(piled(outer_value, outer_got))
     outer_got = partner(outer_value, cuts[0])
@@ -1440,17 +1443,25 @@
     share_got = partner(share_send, last)
     streams_back = residual_back + dot_nt(order.ready(query_back), weight_query)
     tail_got = order.wait(tail_got)
-    tail_value = order.ready(add_extra(fold_last(tail_keep, tail_got)))
-    tail_got = pass_mixed(tail_value, last, cuts[0])
+    tail_value = order.ready(piled(tail_value, tail_got))
+    tail_got = pass_mixed(tail_value, line[0], last)
     inner_got = order.wait(inner_got)
     inner_value = order.ready(piled(inner_value, inner_got))
     inner_got = partner(inner_value, cuts[0])
     tail_got = order.wait(tail_got)
     tail_value = order.ready(piled(tail_value, tail_got))
-    tail_got = pass_mixed(tail_value, line[0], last)
+    tail_got = pass_mixed(tail_value, cuts[0], line[0])
     outer_got = order.wait(outer_got)
     outer_value = order.ready(piled(outer_value, outer_got))
     outer_got = partner(outer_value, 1)
+    outer_got = order.wait(outer_got)
+    (outer_weight_sum,) = lay_out(
+        places_out,
+        (((0, 0, width // 2, -1), (1, 0, width // 2, -2)),),
+        outer_value,
+        outer_got,
+    )
+    outer_weight_sum = order.ready(outer_weight_sum)
     share_got = order.wait(share_got)
     for bit in extra:
         share_keep, share_send = fold(share_keep, share_got)
@@ -1459,21 +1470,10 @@
     content_back = order.ready(content_back)
     tail_got = order.wait(tail_got)
     tail_value = order.ready(piled(tail_value, tail_got))
-    tail_got = pass_mixed(tail_value, cuts[0], line[0])
+    tail_got = partner(tail_value, 1)
     inner_got = order.wait(inner_got)
     inner_value = order.ready(piled(inner_value, inner_got))
     inner_got = partner(inner_value, 1)
-    outer_got = order.wait(outer_got)
-    (outer_weight_sum,) = lay_out(
-        places_out,
-        (((0, 0, width // 2, -1), (1, 0, width // 2, -2)),),
-        outer_value,
-        outer_got,
-    )
-    outer_weight_sum = order.ready(outer_weight_sum)
-    tail_got = order.wait(tail_got)
-    tail_value = order.ready(piled(tail_value, tail_got))
-    tail_got = partner(tail_value, 1)
     inner_got = order.wait(inner_got)
     inner_weight_sum, output_weight_sum = lay_out(
         places_out,

time: 343 us -> 331 us (0.965)
  waiting for transfers between devices: 106 us -> 89.2 us
  starting transfers between devices: 56.5 us -> 63.1 us
    ppermute x40, waiting for transfers between devices: 92.1 us -> 70.8 us  [partner(): lax.ppermute(value, 'ctx', [(place, place ^ bit) for place in range(count)])]
    ppermute x40, starting transfers between devices: 48.4 us -> 56 us  [partner(): lax.ppermute(value, 'ctx', [(place, place ^ bit) for place in range(count)])]
    ppermute x5, waiting for transfers between devices: 10.1 us -> 16.3 us  [pass_mixed(): return lax.ppermute(value, ('ctx', 'wsh'), pairs)]
    unnamed x109 -> x111, local copies, waits for them, and re-layouts: 19.9 us -> 20.3 us
  transfers between devices with their start and end apart: 50 -> 50, of which waited for: 23 -> 25; matrix products, arithmetic and copies ran while one was open for 9% -> 10% of each run, Pallas kernels for 32% -> 35%
where the time goes in v2:
time: 331 us; the launch traced here: 330 us
  Pallas kernels  125 us (38%)
  waiting for transfers between devices  89.2 us (27%)
  starting transfers between devices  63.1 us (19%)
  local copies, waits for them, and re-layouts  27.6 us (8%)
  matrix products  17.7 us (5%)
  other arithmetic  5.78 us (2%)
    ppermute x40, waiting for transfers between devices, partner(): lax.ppermute(value, 'ctx', [(place, place ^ bit) for place in range(count)])  70.8 us
    ppermute x40, starting transfers between devices, partner(): lax.ppermute(value, 'ctx', [(place, place ^ bit) for place in range(count)])  56 us
    pallas_call x1, Pallas kernels, attention_backward(): pl.pallas_call(backward_kernel, grid=(pairs,), in_specs=[spec['stack'], s...  34.3 us
    unnamed x111, local copies, waits for them, and re-layouts  20.3 us
    pallas_call x1, Pallas kernels, attention_forward(): pl.pallas_call(forward_kernel, grid=(pairs,), in_specs=[spec['rows'], spe...  17.8 us
    ppermute x5, waiting for transfers between devices, pass_mixed(): return lax.ppermute(value, ('ctx', 'wsh'), pairs)  16.3 us
    pallas_call x1, Pallas kernels, backward_half(): pl.pallas_call(backward_half_kernel, grid=(1,), in_specs=[in_smem] + [res...  15.2 us
    pallas_call x1, Pallas kernels, forward_half(): pl.pallas_call(forward_half_kernel, grid=(1,), in_specs=[in_smem] + [resi...  12.4 us
  transfers between devices with their start and end apart: 50, of which 25 were waited for; matrix products, arithmetic and copies ran while one was open for 10% of the time, Pallas kernels for 35%

profile of v2, /device:TPU:1, one launch (start us, length us, event | category | flops | bytes accessed | tf_op | source)
XLA Modules:
  0.0 330.5 jit_solution(13268528213219423993)
XLA Ops:
  18.4 7.1 %collective-permute-done.5.refs_1_ = bf16[144,768]{1,0:T(8,128)(2,1)S(1)} collective-permute-done((bf16[144,768]{1,0:T(8,128)(2,1)S(1)}, bf16[144,768]{1,0:T(8,128)(2,1)S(1)}, u32[]{:S(2)}, u32[]{:S(2)}) %collective-permute-start.5) | collective-permute-done | bytes 221216 | tf_op jit(solution)/shard_map/ppermute | solution.py:63
  27.0 4.1 %collective-permute-done.7.refs_3_ = bf16[144,768]{1,0:T(8,128)(2,1)S(1)} collective-permute-done((bf16[144,768]{1,0:T(8,128)(2,1)S(1)}, bf16[144,768]{1,0:T(8,128)(2,1)S(1)}, u32[]{:S(2)}, u32[]{:S(2)}) %collective-permute-start.7) | collective-permute-done | bytes 221216 | tf_op jit(solution)/shard_map/ppermute | solution.py:63
  37.2 7.1 %collective-permute-start.12 = (bf16[1152,768]{1,0:T(8,128)(2,1)}, bf16[1152,768]{1,0:T(8,128)(2,1)}, u32[]{:S(2)}, u32[]{:S(2)}) collective-permute-start(bf16[1152,768]{1,0:T(8,128)(2,1)} %constant_dynamic-update-slice_fusion), channel_id=1, source_target_pairs={{0,2},{2,0},{4,6},{6,4},{8,10},{10,8},{12,14},{14,12},{16,18},{18,... | collective-permute-start | bytes 5308424 | tf_op jit(solution)/shard_map/ppermute | solution.py:63
  62.9 7.0 %convolution_convert_fusion.both_ref = bf16[2048,1536]{1,0:T(8,128)(2,1)} fusion(bf16[2048,768]{1,0:T(8,128)(2,1)S(1)} %get-tuple-element.231, bf16[768,1536]{1,0:T(8,128)(2,1)S(1)} %get-tuple-element.232.weight_ref), kind=kOutput, calls=%fused_computation | convolution fusion | flops 4834983936 | bytes 11796480 | tf_op jit(solution)/shard_map/dot_general | solution.py:50
  69.8 17.8 %shard_map.387 = (f32[256,768]{1,0:T(8,128)}, f32[6,1,512]{2,1,0:T(1,128)}, bf16[6,512,256]{2,1,0:T(8,128)(2,1)}) custom-call(f32[256,768]{1,0:T(8,128)} %fusion.2.query_ref, f32[1,768]{1,0:T(1,128)} %get-tuple-element.493.content_bias_ref, f32[1,768]{1,0:T(1,128)} %get-tuple-element.492.segment_bias_ref, f32[2,768]{1,0:T(2,128)} %slice.147.embed_ref, ...), custom_call_target="tpu_custom_call" | custom-call | tf_op jit(solution)/shard_map/pallas_call | solution.py:698
  91.5 12.4 %shard_map.388 = (bf16[256,768]{1,0:T(8,128)(2,1)}, f32[256,768]{1,0:T(8,128)}, f32[256,768]{1,0:T(8,128)}, f32[256,128]{1,0:T(8,128)}, bf16[256,768]{1,0:T(8,12...) custom-call(s32[10]{0:T(128)} %concatenate.50.place_ref, ...), custom_call_target="tpu_custom_call" | custom-call | flops 8000000000 | tf_op jit(solution)/shard_map/pallas_call | solution.py:1017
  105.3 15.2 %shard_map.389 = (bf16[128,768]{1,0:T(8,128)(2,1)}, bf16[128,768]{1,0:T(8,128)(2,1)}, f32[256,768]{1,0:T(8,128)}, bf16[256,768]{1,0:T(8,128)(2,1)}, bf16[256,384...) custom-call(s32[10]{0:T(128)} %concatenate.50.place_ref, ...), custom_call_target="tpu_custom_call" | custom-call | flops 12000000000 | tf_op jit(solution)/shard_map/pallas_call | solution.py:1041
  125.3 5.7 %shard_map.391 = (bf16[8,48,1920]{2,1,0:T(8,128)(2,1)}, bf16[8,48,1920]{2,1,0:T(8,128)(2,1)}) custom-call(s32[16]{0:T(128)} %add_add_fusion.3.place_ref, bf16[256,768]{1,0:T(8,128)(2,1)} %get-tuple-element.255.refs_0_, bf16[256,768]{1,0:T(8,128)(2,1)} %copy-done.45, bf16[256,1536]{1,0:T(8,128)(2,1)} %get-tuple-element.256.refs_2_, ...), custom_call_target="tpu_custom_call" | custom-call | flops 4000000000 | tf_op jit(solution)/shard_map/pallas_call | solution.py:359
  131.9 5.5 %shard_map.390 = (bf16[8,192,384]{2,1,0:T(8,128)(2,1)}, bf16[8,192,384]{2,1,0:T(8,128)(2,1)}) custom-call(s32[16]{0:T(128)} %add_add_fusion.4.place_ref, bf16[256,3072]{1,0:T(8,128)(2,1)} %get-tuple-element.237.active_ref.refs_0_, bf16[256,3072]{1,0:T(8,128)(2,1)} %collective-permute-done.15.refs_1_, bf16[256,384]{1,0:T(8,128)(2,1)} %get-tuple-element.252.refs_2_, ...), custom_call_target="tpu_custom_call" | custom-call | flops 4000000000 | tf_op jit(solution)/shard_map/pallas_call | solution.py:359
  138.8 34.3 %shard_map.392 = (bf16[256,768]{1,0:T(8,128)(2,1)}, bf16[2048,1536]{1,0:T(8,128)(2,1)}, f32[8,768]{1,0:T(8,128)}) custom-call(bf16[6,512,256]{2,1,0:T(8,128)(2,1)} %get-tuple-element.249.stack_ref, f32[256,768]{1,0:T(8,128)} %fusion.2.query_ref, f32[1,768]{1,0:T(1,128)} %get-tuple-element.492.segment_bias_ref, f32[2,768]{1,0:T(2,128)} %slice.147.embed_ref, ...), custom_call_target="tpu_custom_call" | custom-call | flops 33999998976 | tf_op jit(solution)/shard_map/pallas_call | solution.py:731
  182.1 7.0 %fusion.24.refs_1_ = f32[768,1536]{1,0:T(8,128)S(1)} fusion(bf16[2048,768]{1,0:T(8,128)(2,1)} %copy-done.20, bf16[2048,1536]{1,0:T(8,128)(2,1)S(1)} %copy-done), kind=kOutput, calls=%fused_computation.88 | convolution fusion | flops 4831838208 | bytes 14155776 | tf_op jit(solution)/shard_map/dot_general | solution.py:58
  190.8 6.5 %shard_map.396 = bf16[16,128,768]{2,1,0:T(8,128)(2,1)S(1)} custom-call(bf16[2048,1536]{1,0:T(8,128)(2,1)S(1)} %copy-done, bf16[768,1536]{1,0:T(8,128)(2,1)S(1)} %copy-done.11), custom_call_target="tpu_custom_call" | custom-call | tf_op jit(solution)/shard_map/pallas_call | solution.py:313
  208.4 12.6 %collective-permute-done.30.received_ref = bf16[2,192,384]{2,1,0:T(8,128)(2,1)S(1)} collective-permute-done((bf16[2,192,384]{2,1,0:T(8,128)(2,1)S(1)}, bf16[2,192,384]{2,1,0:T(8,128)(2,1)S(1)}, u32[]{:S(2)}, u32[]{:S(2)}) %collective-permute-start.30) | collective-permute-done | bytes 294944 | tf_op jit(solution)/shard_map/ppermute | solution.py:63
  226.5 5.3 %collective-permute-done.31.received_ref = bf16[4,24,2432]{2,1,0:T(8,128)(2,1)S(1)} collective-permute-done((bf16[4,24,2432]{2,1,0:T(8,128)(2,1)S(1)}, bf16[4,24,2432]{2,1,0:T(8,128)(2,1)S(1)}, u32[]{:S(2)}, u32[]{:S(2)}) %collective-permute-start.31) | collective-permute-done | bytes 466976 | tf_op jit(solution)/shard_map/ppermute | solution.py:213
  239.5 4.6 %collective-permute-done.36.refs_1_ = bf16[1,192,384]{2,1,0:T(8,128)(2,1)S(1)} collective-permute-done((bf16[1,192,384]{2,1,0:T(8,128)(2,1)S(1)}, bf16[1,192,384]{2,1,0:T(8,128)(2,1)S(1)}, u32[]{:S(2)}, u32[]{:S(2)}) %collective-permute-start.36) | collective-permute-done | bytes 147488 | tf_op jit(solution)/shard_map/ppermute | solution.py:63
  248.0 8.9 %collective-permute-done.39.refs_1_ = bf16[1,48,1920]{2,1,0:T(8,128)(2,1)S(1)} collective-permute-done((bf16[1,48,1920]{2,1,0:T(8,128)(2,1)S(1)}, bf16[1,48,1920]{2,1,0:T(8,128)(2,1)S(1)}, u32[]{:S(2)}, u32[]{:S(2)}) %collective-permute-start.39) | collective-permute-done | bytes 184352 | tf_op jit(solution)/shard_map/ppermute | solution.py:63
  259.9 4.1 %collective-permute-done.35.received_ref = bf16[2,128,768]{2,1,0:T(8,128)(2,1)S(1)} collective-permute-done((bf16[2,128,768]{2,1,0:T(8,128)(2,1)S(1)}, bf16[2,128,768]{2,1,0:T(8,128)(2,1)S(1)}, u32[]{:S(2)}, u32[]{:S(2)}) %collective-permute-start.35) | collective-permute-done | bytes 393248 | tf_op jit(solution)/shard_map/ppermute | solution.py:63
  264.1 4.7 %collective-permute-done.42.refs_1_ = bf16[1,24,2432]{2,1,0:T(8,128)(2,1)S(1)} collective-permute-done((bf16[1,24,2432]{2,1,0:T(8,128)(2,1)S(1)}, bf16[1,24,2432]{2,1,0:T(8,128)(2,1)S(1)}, u32[]{:S(2)}, u32[]{:S(2)}) %collective-permute-start.42) | collective-permute-done | bytes 116768 | tf_op jit(solution)/shard_map/ppermute | solution.py:213
  268.8 5.0 %collective-permute-done.44.refs_1_ = bf16[2,48,1920]{2,1,0:T(8,128)(2,1)S(1)} collective-permute-done((bf16[2,48,1920]{2,1,0:T(8,128)(2,1)S(1)}, bf16[2,48,1920]{2,1,0:T(8,128)(2,1)S(1)}, u32[]{:S(2)}, u32[]{:S(2)}) %collective-permute-start.44) | collective-permute-done | bytes 368672 | tf_op jit(solution)/shard_map/ppermute | solution.py:63
  277.6 11.1 %collective-permute-start.45 = (bf16[8,192,384]{2,1,0:T(8,128)(2,1)S(1)}, bf16[8,192,384]{2,1,0:T(8,128)(2,1)S(1)}, u32[]{:S(2)}, u32[]{:S(2)}) collective-permute-start(bf16[8,192,384]{2,1,0:T(8,128)(2,1)S(1)} %shard_map.417.refs_0_), channel_id=1, source_target_pairs={{0,2},{2,0},{4,6},{6,4},{8,10},{10,8},{12,14},{14,12},{16,18},{18,... | collective-permute-start | bytes 3538952 | tf_op jit(solution)/shard_map/ppermute | solution.py:63
  294.6 5.8 %collective-permute-done.40 = bf16[1,128,768]{2,1,0:T(8,128)(2,1)S(1)} collective-permute-done((bf16[1,128,768]{2,1,0:T(8,128)(2,1)S(1)}, bf16[1,128,768]{2,1,0:T(8,128)(2,1)S(1)}, u32[]{:S(2)}, u32[]{:S(2)}) %collective-permute-start.40) | collective-permute-done | bytes 196640 | tf_op jit(solution)/shard_map/ppermute | solution.py:63
  301.8 6.5 %collective-permute-done.48.refs_1_ = bf16[4,48,1920]{2,1,0:T(8,128)(2,1)S(1)} collective-permute-done((bf16[4,48,1920]{2,1,0:T(8,128)(2,1)S(1)}, bf16[4,48,1920]{2,1,0:T(8,128)(2,1)S(1)}, u32[]{:S(2)}, u32[]{:S(2)}) %collective-permute-start.48) | collective-permute-done | bytes 737312 | tf_op jit(solution)/shard_map/ppermute | solution.py:63
  308.4 6.3 %collective-permute-start.49 = (bf16[8,48,1920]{2,1,0:T(8,128)(2,1)S(1)}, bf16[8,48,1920]{2,1,0:T(8,128)(2,1)S(1)}, u32[]{:S(2)}, u32[]{:S(2)}) collective-permute-start(bf16[8,48,1920]{2,1,0:T(8,128)(2,1)S(1)} %shard_map.420.refs_0_), channel_id=1, source_target_pairs={{0,2},{2,0},{4,6},{6,4},{8,10},{10,8},{12,14},{14,12},{16,18},{18,... | collective-permute-start | bytes 4423688 | tf_op jit(solution)/shard_map/ppermute | solution.py:63
  321.4 4.6 %shard_map.422 = (f32[384,768]{1,0:T(8,128)}, f32[384,768]{1,0:T(8,128)}, f32[384,768]{1,0:T(8,128)}, f32[384,128]{1,0:T(8,128)S(1)}) custom-call(s32[16]{0:T(128)S(1)} %broadcast_select_fusion.place_ref, bf16[8,24,2432]{2,1,0:T(8,128)(2,1)S(1)} %shard_map.419.refs_0_, bf16[8,24,2432]{2,1,0:T(8,128)(2,1)S(1)} %collective-permute-done.47.refs_1_), custom_call_target="tpu_custom_call" | custom-call | flops 3000000000 | tf_op jit(solution)/shard_map/pallas_call | solution.py:445
  (283 shorter events, 118.9 us)
Async XLA Ops:
  7.4 37.3 %collective-permute-start = (bf16[192,4224]{1,0:T(8,128)(2,1)S(1)}, bf16[192,4224]{1,0:T(8,128)(2,1)S(1)}, u32[]{:S(2)}, u32[]{:S(2)}) collective-permute-start(bf16[192,4224]{1,0:T(8,128)(2,1)S(1)} %shard_map.382), channel_id=1, source_target_pairs={{0,1},{1,0},{2,3},{3,2},{4,5},{5,4},{6,7},{7,6},{8,9},{9,8},{10,11... | collective-permute-start | bytes 4866056 | tf_op jit(solution)/shard_map/ppermute | solution.py:67
  17.2 13.9 %collective-permute-start.7 = (bf16[144,768]{1,0:T(8,128)(2,1)S(1)}, bf16[144,768]{1,0:T(8,128)(2,1)S(1)}, u32[]{:S(2)}, u32[]{:S(2)}) collective-permute-start(bf16[144,768]{1,0:T(8,128)(2,1)S(1)} %pad_maximum_fusion.3.refs_0_), channel_id=1, source_target_pairs={{0,24},{2,26},{4,28},{6,30},{8,16},{10,18},{12,20},{14,22},{16,8},... | collective-permute-start | bytes 663560 | tf_op jit(solution)/shard_map/ppermute | solution.py:63
  17.2 17.2 %collective-permute-start.8 = (bf16[144,768]{1,0:T(8,128)(2,1)S(1)}, bf16[144,768]{1,0:T(8,128)(2,1)S(1)}, u32[]{:S(2)}, u32[]{:S(2)}) collective-permute-start(bf16[144,768]{1,0:T(8,128)(2,1)S(1)} %pad_maximum_fusion.3.refs_0_), channel_id=1, source_target_pairs={{0,4},{2,6},{4,0},{6,2},{8,12},{10,14},{12,8},{14,10},{16,20},{18,... | collective-permute-start | bytes 663560 | tf_op jit(solution)/shard_map/ppermute | solution.py:63
  37.2 17.7 %collective-permute-start.12 = (bf16[1152,768]{1,0:T(8,128)(2,1)}, bf16[1152,768]{1,0:T(8,128)(2,1)}, u32[]{:S(2)}, u32[]{:S(2)}) collective-permute-start(bf16[1152,768]{1,0:T(8,128)(2,1)} %constant_dynamic-update-slice_fusion), channel_id=1, source_target_pairs={{0,2},{2,0},{4,6},{6,4},{8,10},{10,8},{12,14},{14,12},{16,18},{18,... | collective-permute-start | bytes 5308424 | tf_op jit(solution)/shard_map/ppermute | solution.py:63
  44.6 14.2 %collective-permute-start.3 = (bf16[192,4224]{1,0:T(8,128)(2,1)S(1)}, bf16[192,4224]{1,0:T(8,128)(2,1)}, u32[]{:S(2)}, u32[]{:S(2)}) collective-permute-start(bf16[192,4224]{1,0:T(8,128)(2,1)S(1)} %collective-permute-done.refs_0_.got_ref), channel_id=1, source_target_pairs={{0,2},{2,0},{4,6},{6,4},{8,10},{10,8},{12,14},{14,12},{16,18},{18,... | collective-permute-start | bytes 4866056 | tf_op jit(solution)/shard_map/ppermute | solution.py:63
  51.0 36.6 %collective-permute-start.2 = (bf16[768,768]{1,0:T(8,128)(2,1)}, bf16[768,768]{1,0:T(8,128)(2,1)}, u32[]{:S(2)}, u32[]{:S(2)}) collective-permute-start(bf16[768,768]{1,0:T(8,128)(2,1)} %shard_map.383), channel_id=1, source_target_pairs={{0,1},{1,0},{2,3},{3,2},{4,5},{5,4},{6,7},{7,6},{8,9},{9,8},{10,11... | collective-permute-start | bytes 3538952 | tf_op jit(solution)/shard_map/ppermute | solution.py:67
  53.5 34.2 %collective-permute-start.1 = (bf16[192,1920]{1,0:T(8,128)(2,1)}, bf16[192,1920]{1,0:T(8,128)(2,1)}, u32[]{:S(2)}, u32[]{:S(2)}) collective-permute-start(bf16[192,1920]{1,0:T(8,128)(2,1)} %slice.144), channel_id=1, source_target_pairs={{0,4},{2,6},{4,0},{6,2},{8,12},{10,14},{12,8},{14,10},{16,20},{18,... | collective-permute-start | bytes 2211848 | tf_op jit(solution)/shard_map/ppermute | solution.py:63
  89.3 14.9 %collective-permute-start.14 = (bf16[768,768]{1,0:T(8,128)(2,1)}, bf16[768,768]{1,0:T(8,128)(2,1)S(1)}, u32[]{:S(2)}, u32[]{:S(2)}) collective-permute-start(bf16[768,768]{1,0:T(8,128)(2,1)} %collective-permute-done.2.got_ref), channel_id=1, source_target_pairs={{0,2},{2,0},{4,6},{6,4},{8,10},{10,8},{12,14},{14,12},{16,18},{18,... | collective-permute-start | bytes 3538952 | tf_op jit(solution)/shard_map/ppermute | solution.py:63
  103.9 27.3 %collective-permute-start.15 = (bf16[256,3072]{1,0:T(8,128)(2,1)}, bf16[256,3072]{1,0:T(8,128)(2,1)}, u32[]{:S(2)}, u32[]{:S(2)}) collective-permute-start(bf16[256,3072]{1,0:T(8,128)(2,1)} %get-tuple-element.237.active_ref.refs_0_), channel_id=1, source_target_pairs={{0,2},{2,0},{4,6},{6,4},{8,10},{10,8},{12,14},{14,12},{16,18},{18,... | collective-permute-start | bytes 4718600 | tf_op jit(solution)/shard_map/ppermute | solution.py:63
  131.1 43.8 %collective-permute-start.22 = (bf16[8,48,1920]{2,1,0:T(8,128)(2,1)}, bf16[8,48,1920]{2,1,0:T(8,128)(2,1)S(1)}, u32[]{:S(2)}, u32[]{:S(2)}) collective-permute-start(bf16[8,48,1920]{2,1,0:T(8,128)(2,1)} %get-tuple-element.261), channel_id=1, source_target_pairs={{0,4},{2,6},{4,0},{6,2},{8,12},{10,14},{12,8},{14,10},{16,20},{18,... | collective-permute-start | bytes 4423688 | tf_op jit(solution)/shard_map/ppermute | solution.py:63
  137.4 37.4 %collective-permute-start.21 = (bf16[8,192,384]{2,1,0:T(8,128)(2,1)}, bf16[8,192,384]{2,1,0:T(8,128)(2,1)}, u32[]{:S(2)}, u32[]{:S(2)}) collective-permute-start(bf16[8,192,384]{2,1,0:T(8,128)(2,1)} %get-tuple-element.254), channel_id=1, source_target_pairs={{0,1},{1,0},{2,3},{3,2},{4,5},{5,4},{6,7},{7,6},{8,9},{9,8},{10,11... | collective-permute-start | bytes 3538952 | tf_op jit(solution)/shard_map/ppermute | solution.py:67
  180.6 16.6 %collective-permute-start.24 = (bf16[4,192,384]{2,1,0:T(8,128)(2,1)}, bf16[4,192,384]{2,1,0:T(8,128)(2,1)S(1)}, u32[]{:S(2)}, u32[]{:S(2)}) collective-permute-start(bf16[4,192,384]{2,1,0:T(8,128)(2,1)} %get-tuple-element.287), channel_id=1, source_target_pairs={{0,4},{2,6},{4,0},{6,2},{8,12},{10,14},{12,8},{14,10},{16,20},{18,... | collective-permute-start | bytes 1769480 | tf_op jit(solution)/shard_map/ppermute | solution.py:63
  181.9 17.2 %collective-permute-start.23 = (bf16[4,48,1920]{2,1,0:T(8,128)(2,1)}, bf16[4,48,1920]{2,1,0:T(8,128)(2,1)S(1)}, u32[]{:S(2)}, u32[]{:S(2)}) collective-permute-start(bf16[4,48,1920]{2,1,0:T(8,128)(2,1)} %get-tuple-element.286), channel_id=1, source_target_pairs={{0,1},{1,0},{2,3},{3,2},{4,5},{5,4},{6,7},{7,6},{8,9},{9,8},{10,11... | collective-permute-start | bytes 2211848 | tf_op jit(solution)/shard_map/ppermute | solution.py:67
  204.9 18.9 %collective-permute-start.28 = (bf16[8,24,2432]{2,1,0:T(8,128)(2,1)S(1)}, bf16[8,24,2432]{2,1,0:T(8,128)(2,1)S(1)}, u32[]{:S(2)}, u32[]{:S(2)}) collective-permute-start(bf16[8,24,2432]{2,1,0:T(8,128)(2,1)S(1)} %get-tuple-element.314), channel_id=1, source_target_pairs={{0,1},{1,0},{2,6},{3,7},{4,5},{5,4},{6,2},{7,3},{8,9},{9,8},{10,14... | collective-permute-start | bytes 2801672 | tf_op jit(solution)/shard_map/ppermute | solution.py:213
  205.3 15.9 %collective-permute-start.29 = (bf16[2,48,1920]{2,1,0:T(8,128)(2,1)S(1)}, bf16[2,48,1920]{2,1,0:T(8,128)(2,1)S(1)}, u32[]{:S(2)}, u32[]{:S(2)}) collective-permute-start(bf16[2,48,1920]{2,1,0:T(8,128)(2,1)S(1)} %get-tuple-element.316), channel_id=1, source_target_pairs={{0,8},{2,10},{4,12},{6,14},{8,0},{10,2},{12,4},{14,6},{16,24},{18,... | collective-permute-start | bytes 1105928 | tf_op jit(solution)/shard_map/ppermute | solution.py:63
  206.5 14.5 %collective-permute-start.30 = (bf16[2,192,384]{2,1,0:T(8,128)(2,1)S(1)}, bf16[2,192,384]{2,1,0:T(8,128)(2,1)S(1)}, u32[]{:S(2)}, u32[]{:S(2)}) collective-permute-start(bf16[2,192,384]{2,1,0:T(8,128)(2,1)S(1)} %get-tuple-element.318), channel_id=1, source_target_pairs={{0,8},{2,10},{4,12},{6,14},{8,0},{10,2},{12,4},{14,6},{16,24},{18,... | collective-permute-start | bytes 884744 | tf_op jit(solution)/shard_map/ppermute | solution.py:63
  207.1 32.1 %collective-permute-start.27 = (bf16[4,128,768]{2,1,0:T(8,128)(2,1)S(1)}, bf16[4,128,768]{2,1,0:T(8,128)(2,1)S(1)}, u32[]{:S(2)}, u32[]{:S(2)}) collective-permute-start(bf16[4,128,768]{2,1,0:T(8,128)(2,1)S(1)} %get-tuple-element.312), channel_id=1, source_target_pairs={{0,4},{2,6},{4,0},{6,2},{8,12},{10,14},{12,8},{14,10},{16,20},{18,... | collective-permute-start | bytes 2359304 | tf_op jit(solution)/shard_map/ppermute | solution.py:63
  244.1 14.1 %collective-permute-start.37 = (bf16[2,192,384]{2,1,0:T(8,128)(2,1)S(1)}, bf16[2,192,384]{2,1,0:T(8,128)(2,1)S(1)}, u32[]{:S(2)}, u32[]{:S(2)}) collective-permute-start(bf16[2,192,384]{2,1,0:T(8,128)(2,1)S(1)} %shard_map.409.refs_0_), channel_id=1, source_target_pairs={{0,8},{2,10},{4,12},{6,14},{8,0},{10,2},{12,4},{14,6},{16,24},{18,... | collective-permute-start | bytes 884744 | tf_op jit(solution)/shard_map/ppermute | solution.py:63
  244.2 12.8 %collective-permute-start.39 = (bf16[1,48,1920]{2,1,0:T(8,128)(2,1)S(1)}, bf16[1,48,1920]{2,1,0:T(8,128)(2,1)S(1)}, u32[]{:S(2)}, u32[]{:S(2)}) collective-permute-start(bf16[1,48,1920]{2,1,0:T(8,128)(2,1)S(1)} %shard_map.406.refs_0_), channel_id=1, source_target_pairs={{0,16},{2,18},{4,20},{6,22},{8,24},{10,26},{12,28},{14,30},{16,0},... | collective-permute-start | bytes 552968 | tf_op jit(solution)/shard_map/ppermute | solution.py:63
  246.7 17.3 %collective-permute-start.35 = (bf16[2,128,768]{2,1,0:T(8,128)(2,1)S(1)}, bf16[2,128,768]{2,1,0:T(8,128)(2,1)S(1)}, u32[]{:S(2)}, u32[]{:S(2)}) collective-permute-start(bf16[2,128,768]{2,1,0:T(8,128)(2,1)S(1)} %get-tuple-element.358), channel_id=1, source_target_pairs={{0,8},{2,10},{4,12},{6,14},{8,0},{10,2},{12,4},{14,6},{16,24},{18,... | collective-permute-start | bytes 1179656 | tf_op jit(solution)/shard_map/ppermute | solution.py:63
  258.4 19.0 %collective-permute-start.41 = (bf16[4,192,384]{2,1,0:T(8,128)(2,1)S(1)}, bf16[4,192,384]{2,1,0:T(8,128)(2,1)S(1)}, u32[]{:S(2)}, u32[]{:S(2)}) collective-permute-start(bf16[4,192,384]{2,1,0:T(8,128)(2,1)S(1)} %shard_map.412.refs_0_), channel_id=1, source_target_pairs={{0,4},{2,6},{4,0},{6,2},{8,12},{10,14},{12,8},{14,10},{16,20},{18,... | collective-permute-start | bytes 1769480 | tf_op jit(solution)/shard_map/ppermute | solution.py:63
  258.7 15.1 %collective-permute-start.44 = (bf16[2,48,1920]{2,1,0:T(8,128)(2,1)S(1)}, bf16[2,48,1920]{2,1,0:T(8,128)(2,1)S(1)}, u32[]{:S(2)}, u32[]{:S(2)}) collective-permute-start(bf16[2,48,1920]{2,1,0:T(8,128)(2,1)S(1)} %shard_map.410.refs_0_), channel_id=1, source_target_pairs={{0,8},{2,10},{4,12},{6,14},{8,0},{10,2},{12,4},{14,6},{16,24},{18,... | collective-permute-start | bytes 1105928 | tf_op jit(solution)/shard_map/ppermute | solution.py:63
  277.6 13.9 %collective-permute-start.45 = (bf16[8,192,384]{2,1,0:T(8,128)(2,1)S(1)}, bf16[8,192,384]{2,1,0:T(8,128)(2,1)S(1)}, u32[]{:S(2)}, u32[]{:S(2)}) collective-permute-start(bf16[8,192,384]{2,1,0:T(8,128)(2,1)S(1)} %shard_map.417.refs_0_), channel_id=1, source_target_pairs={{0,2},{2,0},{4,6},{6,4},{8,10},{10,8},{12,14},{14,12},{16,18},{18,... | collective-permute-start | bytes 3538952 | tf_op jit(solution)/shard_map/ppermute | solution.py:63
  290.5 17.8 %collective-permute-start.48 = (bf16[4,48,1920]{2,1,0:T(8,128)(2,1)S(1)}, bf16[4,48,1920]{2,1,0:T(8,128)(2,1)S(1)}, u32[]{:S(2)}, u32[]{:S(2)}) collective-permute-start(bf16[4,48,1920]{2,1,0:T(8,128)(2,1)S(1)} %shard_map.415.refs_0_), channel_id=1, source_target_pairs={{0,4},{2,6},{4,0},{6,2},{8,12},{10,14},{12,8},{14,10},{16,20},{18,... | collective-permute-start | bytes 2211848 | tf_op jit(solution)/shard_map/ppermute | solution.py:63
  (77 other events, 811.3 us)

commit v3 on v2

--- a/solution.py
+++ b/solution.py
@@ -105,14 +105,14 @@
         targets[target][put(place_ref)] = sources[source][taken(place_ref)]
 
 
-def moved(plan, shapes, places, *sources):
+def moved(plan, shapes, places, *sources, limit=40):
     return pl.pallas_call(
         functools.partial(move_kernel, plan, len(sources)),
         grid=(1,),
         in_specs=[in_smem] + [resident(value) for value in sources],
         out_specs=[resident(shape) for shape in shapes],
         out_shape=shapes,
-        compiler_params=pltpu.CompilerParams(vmem_limit_bytes=40 << 20),
+        compiler_params=pltpu.CompilerParams(vmem_limit_bytes=limit << 20),
         cost_estimate=free,
     )(places, *sources)
 
@@ -1124,6 +1124,7 @@
         value_weight,
         output_weight,
         inner_weight,
+        limit=60,
     )
     first_got = across(first_sent)
     mark_rows = 16
@@ -1421,33 +1422,33 @@
     tail_keep, tail_send = fold(tail_keep, tail_got)
     tail_send = order.ready(tail_send)
     tail_got = partner(tail_send, last)
-    share_got = order.wait(share_got)
-    share_keep, share_send = fold(share_keep, share_got)
-    share_send = order.ready(share_send)
-    share_got = partner(share_send, line[0])
     outer_got = order.wait(outer_got)
     outer_value = order.ready(piled(outer_value, outer_got))
     outer_got = partner(outer_value, line[0])
     inner_got = order.wait(inner_got)
     inner_value = order.ready(piled(inner_value, inner_got))
     inner_got = partner(inner_value, line[0])
+    share_got = order.wait(share_got)
+    share_keep, share_send = fold(share_keep, share_got)
+    share_send = order.ready(share_send)
+    share_got = partner(share_send, line[0])
     tail_got = order.wait(tail_got)
     tail_value = order.ready(add_extra(fold_last(tail_keep, tail_got)))
     tail_got = pass_mixed(tail_value, last, cuts[0])
     outer_got = order.wait(outer_got)
     outer_value = order.ready(piled(outer_value, outer_got))
     outer_got = partner(outer_value, cuts[0])
+    inner_got = order.wait(inner_got)
+    inner_value = order.ready(piled(inner_value, inner_got))
+    inner_got = partner(inner_value, cuts[0])
+    tail_got = order.wait(tail_got)
+    tail_value = order.ready(piled(tail_value, tail_got))
+    tail_got = pass_mixed(tail_value, line[0], last)
     share_got = order.wait(share_got)
     share_keep, share_send = fold(share_keep, share_got)
     share_send = order.ready(share_send)
     share_got = partner(share_send, last)
     streams_back = residual_back + dot_nt(order.ready(query_back), weight_query)
-    tail_got = order.wait(tail_got)
-    tail_value = order.ready(piled(tail_value, tail_got))
-    tail_got = pass_mixed(tail_value, line[0], last)
-    inner_got = order.wait(inner_got)
-    inner_value = order.ready(piled(inner_value, inner_got))
-    inner_got = partner(inner_value, cuts[0])
     tail_got = order.wait(tail_got)
     tail_value = order.ready(piled(tail_value, tail_got))
     tail_got = pass_mixed(tail_value, cuts[0], line[0])

time: 331 us -> 329 us (level)
  waiting for transfers between devices: 89.2 us -> 81.3 us
  starting transfers between devices: 63.1 us -> 70.7 us
  local copies, waits for them, and re-layouts: 27.6 us -> 21.8 us
    ppermute x5, waiting for transfers between devices: 16.3 us -> 5.89 us  [pass_mixed(): return lax.ppermute(value, ('ctx', 'wsh'), pairs)]
    ppermute x40, starting transfers between devices: 56 us -> 63 us  [partner(): lax.ppermute(value, 'ctx', [(place, place ^ bit) for place in range(count)])]
    unnamed x111 -> x101, local copies, waits for them, and re-layouts: 20.3 us -> 14.4 us
  transfers between devices with their start and end apart: 50 -> 50, of which waited for: 25 -> 22; matrix products, arithmetic and copies ran while one was open for 10% -> 10% of each run, Pallas kernels for 35% -> 35%
where the time goes in v3:
time: 329 us; the launch traced here: 328 us
  Pallas kernels  128 us (39%)
  waiting for transfers between devices  81.3 us (25%)
  starting transfers between devices  70.7 us (21%)
  local copies, waits for them, and re-layouts  21.8 us (7%)
  matrix products  17.7 us (5%)
  other arithmetic  6.28 us (2%)
    ppermute x40, waiting for transfers between devices, partner(): lax.ppermute(value, 'ctx', [(place, place ^ bit) for place in range(count)])  73.2 us
    ppermute x40, starting transfers between devices, partner(): lax.ppermute(value, 'ctx', [(place, place ^ bit) for place in range(count)])  63 us
    pallas_call x1, Pallas kernels, attention_backward(): pl.pallas_call(backward_kernel, grid=(pairs,), in_specs=[spec['stack'], s...  34.4 us
    pallas_call x1, Pallas kernels, attention_forward(): pl.pallas_call(forward_kernel, grid=(pairs,), in_specs=[spec['rows'], spe...  17.8 us
    pallas_call x1, Pallas kernels, backward_half(): pl.pallas_call(backward_half_kernel, grid=(1,), in_specs=[in_smem] + [res...  15.2 us
    unnamed x101, local copies, waits for them, and re-layouts  14.4 us
    pallas_call x1, Pallas kernels, forward_half(): pl.pallas_call(forward_half_kernel, grid=(1,), in_specs=[in_smem] + [resi...  12.4 us
    pallas_call x3, Pallas kernels, lay_out(): pl.pallas_call(functools.partial(lay_out_kernel, plan), grid=(1,), in_spe...  11.6 us
  transfers between devices with their start and end apart: 50, of which 22 were waited for; matrix products, arithmetic and copies ran while one was open for 10% of the time, Pallas kernels for 35%

profile of v3, /device:TPU:1, one launch (start us, length us, event | category | flops | bytes accessed | tf_op | source)
XLA Modules:
  0.0 327.9 jit_solution(7053038138797131091)
XLA Ops:
  1.3 3.7 %shard_map.382 = bf16[192,4224]{1,0:T(8,128)(2,1)} custom-call(s32[2]{0:T(128)} %pad_add_fusion.1.place_ref, bf16[384,768]{1,0:T(8,128)(2,1)} %refs_2_.3, bf16[384,768]{1,0:T(8,128)(2,1)} %refs_3_.3, bf16[384,768]{1,0:T(8,128)(2,1)} %refs_4_.3, bf16[384,768]{1,0:T(8,128)(2,1)} %output_own_ref.1, bf16[384,3072]{1,0:T(8,128)(2,1)} %inner_own_ref.1), custom_call_target="tpu_custom_call" | custom-call | tf_op jit(solution)/shard_map/pallas_call | solution.py:109
  16.0 7.1 %collective-permute-done.5.refs_1_ = bf16[144,768]{1,0:T(8,128)(2,1)S(1)} collective-permute-done((bf16[144,768]{1,0:T(8,128)(2,1)S(1)}, bf16[144,768]{1,0:T(8,128)(2,1)S(1)}, u32[]{:S(2)}, u32[]{:S(2)}) %collective-permute-start.5) | collective-permute-done | bytes 221216 | tf_op jit(solution)/shard_map/ppermute | solution.py:63
  24.6 4.1 %collective-permute-done.7.refs_3_ = bf16[144,768]{1,0:T(8,128)(2,1)S(1)} collective-permute-done((bf16[144,768]{1,0:T(8,128)(2,1)S(1)}, bf16[144,768]{1,0:T(8,128)(2,1)S(1)}, u32[]{:S(2)}, u32[]{:S(2)}) %collective-permute-start.7) | collective-permute-done | bytes 221216 | tf_op jit(solution)/shard_map/ppermute | solution.py:63
  34.8 7.1 %collective-permute-start.12 = (bf16[1152,768]{1,0:T(8,128)(2,1)}, bf16[1152,768]{1,0:T(8,128)(2,1)}, u32[]{:S(2)}, u32[]{:S(2)}) collective-permute-start(bf16[1152,768]{1,0:T(8,128)(2,1)} %constant_dynamic-update-slice_fusion), channel_id=1, source_target_pairs={{0,2},{2,0},{4,6},{6,4},{8,10},{10,8},{12,14},{14,12},{16,18},{18,... | collective-permute-start | bytes 5308424 | tf_op jit(solution)/shard_map/ppermute | solution.py:63
  60.7 6.9 %convolution_convert_fusion.both_ref = bf16[2048,1536]{1,0:T(8,128)(2,1)} fusion(bf16[2048,768]{1,0:T(8,128)(2,1)S(1)} %get-tuple-element.231, bf16[768,1536]{1,0:T(8,128)(2,1)S(1)} %get-tuple-element.232.weight_ref), kind=kOutput, calls=%fused_computation | convolution fusion | flops 4834983936 | bytes 11796480 | tf_op jit(solution)/shard_map/dot_general | solution.py:50
  67.6 17.8 %shard_map.387 = (f32[256,768]{1,0:T(8,128)}, f32[6,1,512]{2,1,0:T(1,128)}, bf16[6,512,256]{2,1,0:T(8,128)(2,1)}) custom-call(f32[256,768]{1,0:T(8,128)} %fusion.2.query_ref, f32[1,768]{1,0:T(1,128)} %get-tuple-element.493.content_bias_ref, f32[1,768]{1,0:T(1,128)} %get-tuple-element.492.segment_bias_ref, f32[2,768]{1,0:T(2,128)} %slice.147.embed_ref, ...), custom_call_target="tpu_custom_call" | custom-call | tf_op jit(solution)/shard_map/pallas_call | solution.py:698
  89.2 12.4 %shard_map.388 = (bf16[256,768]{1,0:T(8,128)(2,1)}, f32[256,768]{1,0:T(8,128)}, f32[256,768]{1,0:T(8,128)}, f32[256,128]{1,0:T(8,128)}, bf16[256,768]{1,0:T(8,12...) custom-call(s32[10]{0:T(128)} %concatenate.50.place_ref, ...), custom_call_target="tpu_custom_call" | custom-call | flops 8000000000 | tf_op jit(solution)/shard_map/pallas_call | solution.py:1017
  103.1 15.2 %shard_map.389 = (bf16[128,768]{1,0:T(8,128)(2,1)}, bf16[128,768]{1,0:T(8,128)(2,1)}, f32[256,768]{1,0:T(8,128)}, bf16[256,768]{1,0:T(8,128)(2,1)}, bf16[256,384...) custom-call(s32[10]{0:T(128)} %concatenate.50.place_ref, ...), custom_call_target="tpu_custom_call" | custom-call | flops 12000000000 | tf_op jit(solution)/shard_map/pallas_call | solution.py:1041
  123.1 5.7 %shard_map.391 = (bf16[8,48,1920]{2,1,0:T(8,128)(2,1)}, bf16[8,48,1920]{2,1,0:T(8,128)(2,1)}) custom-call(s32[16]{0:T(128)} %add_add_fusion.3.place_ref, bf16[256,768]{1,0:T(8,128)(2,1)} %get-tuple-element.255.refs_0_, bf16[256,768]{1,0:T(8,128)(2,1)} %copy-done.40, bf16[256,1536]{1,0:T(8,128)(2,1)} %get-tuple-element.256.refs_2_, ...), custom_call_target="tpu_custom_call" | custom-call | flops 4000000000 | tf_op jit(solution)/shard_map/pallas_call | solution.py:359
  129.6 5.5 %shard_map.390 = (bf16[8,192,384]{2,1,0:T(8,128)(2,1)}, bf16[8,192,384]{2,1,0:T(8,128)(2,1)}) custom-call(s32[16]{0:T(128)} %add_add_fusion.4.place_ref, bf16[256,3072]{1,0:T(8,128)(2,1)} %get-tuple-element.237.active_ref.refs_0_, bf16[256,3072]{1,0:T(8,128)(2,1)} %collective-permute-done.15.refs_1_, bf16[256,384]{1,0:T(8,128)(2,1)} %get-tuple-element.252.refs_2_, ...), custom_call_target="tpu_custom_call" | custom-call | flops 4000000000 | tf_op jit(solution)/shard_map/pallas_call | solution.py:359
  136.5 34.4 %shard_map.392 = (bf16[256,768]{1,0:T(8,128)(2,1)}, bf16[2048,1536]{1,0:T(8,128)(2,1)}, f32[8,768]{1,0:T(8,128)}) custom-call(bf16[6,512,256]{2,1,0:T(8,128)(2,1)} %get-tuple-element.249.stack_ref, f32[256,768]{1,0:T(8,128)} %fusion.2.query_ref, f32[1,768]{1,0:T(1,128)} %get-tuple-element.492.segment_bias_ref, f32[2,768]{1,0:T(2,128)} %slice.147.embed_ref, ...), custom_call_target="tpu_custom_call" | custom-call | flops 33999998976 | tf_op jit(solution)/shard_map/pallas_call | solution.py:731
  179.9 7.0 %fusion.24.refs_1_ = f32[768,1536]{1,0:T(8,128)S(1)} fusion(bf16[2048,768]{1,0:T(8,128)(2,1)} %copy-done.15, bf16[2048,1536]{1,0:T(8,128)(2,1)S(1)} %copy-done), kind=kOutput, calls=%fused_computation.88 | convolution fusion | flops 4831838208 | bytes 14155776 | tf_op jit(solution)/shard_map/dot_general | solution.py:58
  188.5 6.5 %shard_map.396 = bf16[16,128,768]{2,1,0:T(8,128)(2,1)S(1)} custom-call(bf16[2048,1536]{1,0:T(8,128)(2,1)S(1)} %copy-done, bf16[768,1536]{1,0:T(8,128)(2,1)S(1)} %copy-done.7), custom_call_target="tpu_custom_call" | custom-call | tf_op jit(solution)/shard_map/pallas_call | solution.py:313
  204.9 13.9 %collective-permute-done.29.received_ref = bf16[2,192,384]{2,1,0:T(8,128)(2,1)S(1)} collective-permute-done((bf16[2,192,384]{2,1,0:T(8,128)(2,1)S(1)}, bf16[2,192,384]{2,1,0:T(8,128)(2,1)S(1)}, u32[]{:S(2)}, u32[]{:S(2)}) %collective-permute-start.29) | collective-permute-done | bytes 294944 | tf_op jit(solution)/shard_map/ppermute | solution.py:63
  242.0 10.3 %collective-permute-done.34.refs_1_ = bf16[1,48,1920]{2,1,0:T(8,128)(2,1)S(1)} collective-permute-done((bf16[1,48,1920]{2,1,0:T(8,128)(2,1)S(1)}, bf16[1,48,1920]{2,1,0:T(8,128)(2,1)S(1)}, u32[]{:S(2)}, u32[]{:S(2)}) %collective-permute-start.34) | collective-permute-done | bytes 184352 | tf_op jit(solution)/shard_map/ppermute | solution.py:63
  255.9 8.1 %collective-permute-done.40.refs_1_ = bf16[2,48,1920]{2,1,0:T(8,128)(2,1)S(1)} collective-permute-done((bf16[2,48,1920]{2,1,0:T(8,128)(2,1)S(1)}, bf16[2,48,1920]{2,1,0:T(8,128)(2,1)S(1)}, u32[]{:S(2)}, u32[]{:S(2)}) %collective-permute-start.40) | collective-permute-done | bytes 368672 | tf_op jit(solution)/shard_map/ppermute | solution.py:63
  266.0 3.3 %collective-permute-done.37.received_ref = bf16[2,128,768]{2,1,0:T(8,128)(2,1)S(1)} collective-permute-done((bf16[2,128,768]{2,1,0:T(8,128)(2,1)S(1)}, bf16[2,128,768]{2,1,0:T(8,128)(2,1)S(1)}, u32[]{:S(2)}, u32[]{:S(2)}) %collective-permute-start.37) | collective-permute-done | bytes 393248 | tf_op jit(solution)/shard_map/ppermute | solution.py:63
  271.7 16.1 %collective-permute-start.45 = (bf16[8,192,384]{2,1,0:T(8,128)(2,1)S(1)}, bf16[8,192,384]{2,1,0:T(8,128)(2,1)S(1)}, u32[]{:S(2)}, u32[]{:S(2)}) collective-permute-start(bf16[8,192,384]{2,1,0:T(8,128)(2,1)S(1)} %shard_map.417.refs_0_), channel_id=1, source_target_pairs={{0,2},{2,0},{4,6},{6,4},{8,10},{10,8},{12,14},{14,12},{16,18},{18,... | collective-permute-start | bytes 3538952 | tf_op jit(solution)/shard_map/ppermute | solution.py:63
  291.5 3.2 shard_map.418
  294.7 5.6 %collective-permute-done.42 = bf16[1,128,768]{2,1,0:T(8,128)(2,1)S(1)} collective-permute-done((bf16[1,128,768]{2,1,0:T(8,128)(2,1)S(1)}, bf16[1,128,768]{2,1,0:T(8,128)(2,1)S(1)}, u32[]{:S(2)}, u32[]{:S(2)}) %collective-permute-start.42) | collective-permute-done | bytes 196640 | tf_op jit(solution)/shard_map/ppermute | solution.py:63
  302.0 4.0 %collective-permute-done.48.refs_1_ = bf16[4,48,1920]{2,1,0:T(8,128)(2,1)S(1)} collective-permute-done((bf16[4,48,1920]{2,1,0:T(8,128)(2,1)S(1)}, bf16[4,48,1920]{2,1,0:T(8,128)(2,1)S(1)}, u32[]{:S(2)}, u32[]{:S(2)}) %collective-permute-start.48) | collective-permute-done | bytes 737312 | tf_op jit(solution)/shard_map/ppermute | solution.py:63
  306.1 6.0 %collective-permute-start.49 = (bf16[8,48,1920]{2,1,0:T(8,128)(2,1)S(1)}, bf16[8,48,1920]{2,1,0:T(8,128)(2,1)S(1)}, u32[]{:S(2)}, u32[]{:S(2)}) collective-permute-start(bf16[8,48,1920]{2,1,0:T(8,128)(2,1)S(1)} %shard_map.420.refs_0_), channel_id=1, source_target_pairs={{0,2},{2,0},{4,6},{6,4},{8,10},{10,8},{12,14},{14,12},{16,18},{18,... | collective-permute-start | bytes 4423688 | tf_op jit(solution)/shard_map/ppermute | solution.py:63
  315.0 3.8 %shard_map.421 = (f32[384,3072]{1,0:T(8,128)}, f32[384,768]{1,0:T(8,128)}) custom-call(s32[9]{0:T(128)S(1)} %pad_add_fusion.4.place_ref, bf16[8,48,1920]{2,1,0:T(8,128)(2,1)S(1)} %shard_map.420.refs_0_, bf16[8,48,1920]{2,1,0:T(8,128)(2,1)S(1)} %collective-permute-done.49.refs_1_), custom_call_target="tpu_custom_call" | custom-call | flops 3000000000 | tf_op jit(solution)/shard_map/pallas_call | solution.py:445
  318.7 4.6 %shard_map.422 = (f32[384,768]{1,0:T(8,128)}, f32[384,768]{1,0:T(8,128)}, f32[384,768]{1,0:T(8,128)}, f32[384,128]{1,0:T(8,128)S(1)}) custom-call(s32[16]{0:T(128)S(1)} %broadcast_select_fusion.place_ref, bf16[8,24,2432]{2,1,0:T(8,128)(2,1)S(1)} %shard_map.419.refs_0_, bf16[8,24,2432]{2,1,0:T(8,128)(2,1)S(1)} %collective-permute-done.47.refs_1_), custom_call_target="tpu_custom_call" | custom-call | flops 3000000000 | tf_op jit(solution)/shard_map/pallas_call | solution.py:445
  (273 shorter events, 113.3 us)
Async XLA Ops:
  5.0 37.4 %collective-permute-start = (bf16[192,4224]{1,0:T(8,128)(2,1)}, bf16[192,4224]{1,0:T(8,128)(2,1)S(1)}, u32[]{:S(2)}, u32[]{:S(2)}) collective-permute-start(bf16[192,4224]{1,0:T(8,128)(2,1)} %shard_map.382), channel_id=1, source_target_pairs={{0,1},{1,0},{2,3},{3,2},{4,5},{5,4},{6,7},{7,6},{8,9},{9,8},{10,11... | collective-permute-start | bytes 4866056 | tf_op jit(solution)/shard_map/ppermute | solution.py:67
  11.1 12.0 %collective-permute-start.5 = (bf16[144,768]{1,0:T(8,128)(2,1)S(1)}, bf16[144,768]{1,0:T(8,128)(2,1)S(1)}, u32[]{:S(2)}, u32[]{:S(2)}) collective-permute-start(bf16[144,768]{1,0:T(8,128)(2,1)S(1)} %pad_maximum_fusion.3.refs_0_), channel_id=1, source_target_pairs={{0,16},{2,18},{4,20},{6,22},{8,24},{10,26},{12,28},{14,30},{16,0},... | collective-permute-start | bytes 663560 | tf_op jit(solution)/shard_map/ppermute | solution.py:63
  14.7 13.9 %collective-permute-start.7 = (bf16[144,768]{1,0:T(8,128)(2,1)S(1)}, bf16[144,768]{1,0:T(8,128)(2,1)S(1)}, u32[]{:S(2)}, u32[]{:S(2)}) collective-permute-start(bf16[144,768]{1,0:T(8,128)(2,1)S(1)} %pad_maximum_fusion.3.refs_0_), channel_id=1, source_target_pairs={{0,24},{2,26},{4,28},{6,30},{8,16},{10,18},{12,20},{14,22},{16,8},... | collective-permute-start | bytes 663560 | tf_op jit(solution)/shard_map/ppermute | solution.py:63
  14.7 17.2 %collective-permute-start.8 = (bf16[144,768]{1,0:T(8,128)(2,1)S(1)}, bf16[144,768]{1,0:T(8,128)(2,1)S(1)}, u32[]{:S(2)}, u32[]{:S(2)}) collective-permute-start(bf16[144,768]{1,0:T(8,128)(2,1)S(1)} %pad_maximum_fusion.3.refs_0_), channel_id=1, source_target_pairs={{0,4},{2,6},{4,0},{6,2},{8,12},{10,14},{12,8},{14,10},{16,20},{18,... | collective-permute-start | bytes 663560 | tf_op jit(solution)/shard_map/ppermute | solution.py:63
  34.8 17.9 %collective-permute-start.12 = (bf16[1152,768]{1,0:T(8,128)(2,1)}, bf16[1152,768]{1,0:T(8,128)(2,1)}, u32[]{:S(2)}, u32[]{:S(2)}) collective-permute-start(bf16[1152,768]{1,0:T(8,128)(2,1)} %constant_dynamic-update-slice_fusion), channel_id=1, source_target_pairs={{0,2},{2,0},{4,6},{6,4},{8,10},{10,8},{12,14},{14,12},{16,18},{18,... | collective-permute-start | bytes 5308424 | tf_op jit(solution)/shard_map/ppermute | solution.py:63
  42.4 14.2 %collective-permute-start.3 = (bf16[192,4224]{1,0:T(8,128)(2,1)S(1)}, bf16[192,4224]{1,0:T(8,128)(2,1)}, u32[]{:S(2)}, u32[]{:S(2)}) collective-permute-start(bf16[192,4224]{1,0:T(8,128)(2,1)S(1)} %collective-permute-done.refs_0_.got_ref), channel_id=1, source_target_pairs={{0,2},{2,0},{4,6},{6,4},{8,10},{10,8},{12,14},{14,12},{16,18},{18,... | collective-permute-start | bytes 4866056 | tf_op jit(solution)/shard_map/ppermute | solution.py:63
  48.8 36.6 %collective-permute-start.2 = (bf16[768,768]{1,0:T(8,128)(2,1)}, bf16[768,768]{1,0:T(8,128)(2,1)}, u32[]{:S(2)}, u32[]{:S(2)}) collective-permute-start(bf16[768,768]{1,0:T(8,128)(2,1)} %shard_map.383), channel_id=1, source_target_pairs={{0,1},{1,0},{2,3},{3,2},{4,5},{5,4},{6,7},{7,6},{8,9},{9,8},{10,11... | collective-permute-start | bytes 3538952 | tf_op jit(solution)/shard_map/ppermute | solution.py:67
  51.2 34.2 %collective-permute-start.1 = (bf16[192,1920]{1,0:T(8,128)(2,1)}, bf16[192,1920]{1,0:T(8,128)(2,1)}, u32[]{:S(2)}, u32[]{:S(2)}) collective-permute-start(bf16[192,1920]{1,0:T(8,128)(2,1)} %slice.144), channel_id=1, source_target_pairs={{0,4},{2,6},{4,0},{6,2},{8,12},{10,14},{12,8},{14,10},{16,20},{18,... | collective-permute-start | bytes 2211848 | tf_op jit(solution)/shard_map/ppermute | solution.py:63
  87.1 15.0 %collective-permute-start.14 = (bf16[768,768]{1,0:T(8,128)(2,1)}, bf16[768,768]{1,0:T(8,128)(2,1)S(1)}, u32[]{:S(2)}, u32[]{:S(2)}) collective-permute-start(bf16[768,768]{1,0:T(8,128)(2,1)} %collective-permute-done.2.got_ref), channel_id=1, source_target_pairs={{0,2},{2,0},{4,6},{6,4},{8,10},{10,8},{12,14},{14,12},{16,18},{18,... | collective-permute-start | bytes 3538952 | tf_op jit(solution)/shard_map/ppermute | solution.py:63
  101.7 27.3 %collective-permute-start.15 = (bf16[256,3072]{1,0:T(8,128)(2,1)}, bf16[256,3072]{1,0:T(8,128)(2,1)}, u32[]{:S(2)}, u32[]{:S(2)}) collective-permute-start(bf16[256,3072]{1,0:T(8,128)(2,1)} %get-tuple-element.237.active_ref.refs_0_), channel_id=1, source_target_pairs={{0,2},{2,0},{4,6},{6,4},{8,10},{10,8},{12,14},{14,12},{16,18},{18,... | collective-permute-start | bytes 4718600 | tf_op jit(solution)/shard_map/ppermute | solution.py:63
  128.8 43.7 %collective-permute-start.22 = (bf16[8,48,1920]{2,1,0:T(8,128)(2,1)}, bf16[8,48,1920]{2,1,0:T(8,128)(2,1)S(1)}, u32[]{:S(2)}, u32[]{:S(2)}) collective-permute-start(bf16[8,48,1920]{2,1,0:T(8,128)(2,1)} %get-tuple-element.261), channel_id=1, source_target_pairs={{0,4},{2,6},{4,0},{6,2},{8,12},{10,14},{12,8},{14,10},{16,20},{18,... | collective-permute-start | bytes 4423688 | tf_op jit(solution)/shard_map/ppermute | solution.py:63
  135.2 37.4 %collective-permute-start.21 = (bf16[8,192,384]{2,1,0:T(8,128)(2,1)}, bf16[8,192,384]{2,1,0:T(8,128)(2,1)}, u32[]{:S(2)}, u32[]{:S(2)}) collective-permute-start(bf16[8,192,384]{2,1,0:T(8,128)(2,1)} %get-tuple-element.254), channel_id=1, source_target_pairs={{0,1},{1,0},{2,3},{3,2},{4,5},{5,4},{6,7},{7,6},{8,9},{9,8},{10,11... | collective-permute-start | bytes 3538952 | tf_op jit(solution)/shard_map/ppermute | solution.py:67
  178.4 16.6 %collective-permute-start.24 = (bf16[4,192,384]{2,1,0:T(8,128)(2,1)}, bf16[4,192,384]{2,1,0:T(8,128)(2,1)S(1)}, u32[]{:S(2)}, u32[]{:S(2)}) collective-permute-start(bf16[4,192,384]{2,1,0:T(8,128)(2,1)} %get-tuple-element.287), channel_id=1, source_target_pairs={{0,4},{2,6},{4,0},{6,2},{8,12},{10,14},{12,8},{14,10},{16,20},{18,... | collective-permute-start | bytes 1769480 | tf_op jit(solution)/shard_map/ppermute | solution.py:63
  179.6 17.2 %collective-permute-start.23 = (bf16[4,48,1920]{2,1,0:T(8,128)(2,1)}, bf16[4,48,1920]{2,1,0:T(8,128)(2,1)S(1)}, u32[]{:S(2)}, u32[]{:S(2)}) collective-permute-start(bf16[4,48,1920]{2,1,0:T(8,128)(2,1)} %get-tuple-element.286), channel_id=1, source_target_pairs={{0,1},{1,0},{2,3},{3,2},{4,5},{5,4},{6,7},{7,6},{8,9},{9,8},{10,11... | collective-permute-start | bytes 2211848 | tf_op jit(solution)/shard_map/ppermute | solution.py:67
  202.7 16.3 %collective-permute-start.32 = (bf16[8,24,2432]{2,1,0:T(8,128)(2,1)S(1)}, bf16[8,24,2432]{2,1,0:T(8,128)(2,1)S(1)}, u32[]{:S(2)}, u32[]{:S(2)}) collective-permute-start(bf16[8,24,2432]{2,1,0:T(8,128)(2,1)S(1)} %get-tuple-element.330), channel_id=1, source_target_pairs={{0,1},{1,0},{2,6},{3,7},{4,5},{5,4},{6,2},{7,3},{8,9},{9,8},{10,14... | collective-permute-start | bytes 2801672 | tf_op jit(solution)/shard_map/ppermute | solution.py:213
  203.0 15.9 %collective-permute-start.28 = (bf16[2,48,1920]{2,1,0:T(8,128)(2,1)S(1)}, bf16[2,48,1920]{2,1,0:T(8,128)(2,1)S(1)}, u32[]{:S(2)}, u32[]{:S(2)}) collective-permute-start(bf16[2,48,1920]{2,1,0:T(8,128)(2,1)S(1)} %get-tuple-element.314), channel_id=1, source_target_pairs={{0,8},{2,10},{4,12},{6,14},{8,0},{10,2},{12,4},{14,6},{16,24},{18,... | collective-permute-start | bytes 1105928 | tf_op jit(solution)/shard_map/ppermute | solution.py:63
  204.3 14.5 %collective-permute-start.29 = (bf16[2,192,384]{2,1,0:T(8,128)(2,1)S(1)}, bf16[2,192,384]{2,1,0:T(8,128)(2,1)S(1)}, u32[]{:S(2)}, u32[]{:S(2)}) collective-permute-start(bf16[2,192,384]{2,1,0:T(8,128)(2,1)S(1)} %get-tuple-element.316), channel_id=1, source_target_pairs={{0,8},{2,10},{4,12},{6,14},{8,0},{10,2},{12,4},{14,6},{16,24},{18,... | collective-permute-start | bytes 884744 | tf_op jit(solution)/shard_map/ppermute | solution.py:63
  219.3 33.2 %collective-permute-start.27 = (bf16[4,128,768]{2,1,0:T(8,128)(2,1)S(1)}, bf16[4,128,768]{2,1,0:T(8,128)(2,1)S(1)}, u32[]{:S(2)}, u32[]{:S(2)}) collective-permute-start(bf16[4,128,768]{2,1,0:T(8,128)(2,1)S(1)} %get-tuple-element.312), channel_id=1, source_target_pairs={{0,4},{2,6},{4,0},{6,2},{8,12},{10,14},{12,8},{14,10},{16,20},{18,... | collective-permute-start | bytes 2359304 | tf_op jit(solution)/shard_map/ppermute | solution.py:63
  239.4 14.2 %collective-permute-start.41 = (bf16[2,192,384]{2,1,0:T(8,128)(2,1)S(1)}, bf16[2,192,384]{2,1,0:T(8,128)(2,1)S(1)}, u32[]{:S(2)}, u32[]{:S(2)}) collective-permute-start(bf16[2,192,384]{2,1,0:T(8,128)(2,1)S(1)} %shard_map.408.refs_0_), channel_id=1, source_target_pairs={{0,8},{2,10},{4,12},{6,14},{8,0},{10,2},{12,4},{14,6},{16,24},{18,... | collective-permute-start | bytes 884744 | tf_op jit(solution)/shard_map/ppermute | solution.py:63
  239.5 12.8 %collective-permute-start.34 = (bf16[1,48,1920]{2,1,0:T(8,128)(2,1)S(1)}, bf16[1,48,1920]{2,1,0:T(8,128)(2,1)S(1)}, u32[]{:S(2)}, u32[]{:S(2)}) collective-permute-start(bf16[1,48,1920]{2,1,0:T(8,128)(2,1)S(1)} %shard_map.406.refs_0_), channel_id=1, source_target_pairs={{0,16},{2,18},{4,20},{6,22},{8,24},{10,26},{12,28},{14,30},{16,0},... | collective-permute-start | bytes 552968 | tf_op jit(solution)/shard_map/ppermute | solution.py:63
  253.8 17.8 %collective-permute-start.43 = (bf16[4,192,384]{2,1,0:T(8,128)(2,1)S(1)}, bf16[4,192,384]{2,1,0:T(8,128)(2,1)S(1)}, u32[]{:S(2)}, u32[]{:S(2)}) collective-permute-start(bf16[4,192,384]{2,1,0:T(8,128)(2,1)S(1)} %shard_map.412.refs_0_), channel_id=1, source_target_pairs={{0,4},{2,6},{4,0},{6,2},{8,12},{10,14},{12,8},{14,10},{16,20},{18,... | collective-permute-start | bytes 1769480 | tf_op jit(solution)/shard_map/ppermute | solution.py:63
  255.3 14.0 %collective-permute-start.37 = (bf16[2,128,768]{2,1,0:T(8,128)(2,1)S(1)}, bf16[2,128,768]{2,1,0:T(8,128)(2,1)S(1)}, u32[]{:S(2)}, u32[]{:S(2)}) collective-permute-start(bf16[2,128,768]{2,1,0:T(8,128)(2,1)S(1)} %get-tuple-element.366), channel_id=1, source_target_pairs={{0,8},{2,10},{4,12},{6,14},{8,0},{10,2},{12,4},{14,6},{16,24},{18,... | collective-permute-start | bytes 1179656 | tf_op jit(solution)/shard_map/ppermute | solution.py:63
  271.7 19.8 %collective-permute-start.45 = (bf16[8,192,384]{2,1,0:T(8,128)(2,1)S(1)}, bf16[8,192,384]{2,1,0:T(8,128)(2,1)S(1)}, u32[]{:S(2)}, u32[]{:S(2)}) collective-permute-start(bf16[8,192,384]{2,1,0:T(8,128)(2,1)S(1)} %shard_map.417.refs_0_), channel_id=1, source_target_pairs={{0,2},{2,0},{4,6},{6,4},{8,10},{10,8},{12,14},{14,12},{16,18},{18,... | collective-permute-start | bytes 3538952 | tf_op jit(solution)/shard_map/ppermute | solution.py:63
  287.9 18.1 %collective-permute-start.48 = (bf16[4,48,1920]{2,1,0:T(8,128)(2,1)S(1)}, bf16[4,48,1920]{2,1,0:T(8,128)(2,1)S(1)}, u32[]{:S(2)}, u32[]{:S(2)}) collective-permute-start(bf16[4,48,1920]{2,1,0:T(8,128)(2,1)S(1)} %shard_map.413.refs_0_), channel_id=1, source_target_pairs={{0,4},{2,6},{4,0},{6,2},{8,12},{10,14},{12,8},{14,10},{16,20},{18,... | collective-permute-start | bytes 2211848 | tf_op jit(solution)/shard_map/ppermute | solution.py:63
  (72 other events, 820.9 us)
